TPU v7x, 32 devices: a whole 2x2x4 slice. The times are simulated.
32 devices in a mesh: row: 8 (over z, x), col: 4 (over y, core).
Axes of the slice: x: 2, y: 2, z: 4, core: 2. Of those that a mesh axis runs over, the one named last changes fastest.
Arguments:
- alignment: bfloat16 [256, 192, 256], P('row', 'col'), may hold values from -8 to 8
- alignment_mask: int32 [256, 192], P('row', 'col'), may hold values from 0 to 1, as said below
- residue_mask: int32 [192], replicated, may hold values from 0 to 1, as said below
- pair_features: bfloat16 [192, 192, 128], P('row', 'col'), may hold values from -6 to 6
- outer_product_left: bfloat16 [256, 32], replicated, may hold values from -0.375 to 0.375
- outer_product_right: bfloat16 [256, 32], replicated, may hold values from -0.375 to 0.375
- outer_proj: bfloat16 [1024, 128], replicated, may hold values from -0.1875 to 0.1875
- triangle_proj: bfloat16 [128, 512], replicated, may hold values from -0.5 to 0.5
- triangle_gate: bfloat16 [128, 128], replicated, may hold values from -0.5 to 0.5
- triangle_out: bfloat16 [128, 128], replicated, may hold values from -0.5 to 0.5
- transition_in: bfloat16 [128, 512], replicated, may hold values from -0.5 to 0.5
- transition_out: bfloat16 [512, 128], replicated, may hold values from -0.25 to 0.25
Outputs:
- pair_out: bfloat16 [192, 192, 128], P('row', 'col')
Inputs may be any that keep to these rules, and one draw needn't show every extreme that they name: `residue_mask`: masked residues scattered anywhere; at least one residue is masked and at least one takes part. `alignment_mask`: 0 wherever residue_mask is 0.
All inputs are finite; a program needn't handle non-finite values.
Results may differ from a plain program's by a relative error of at most 0.014.
Values may be sent and summed in bfloat16 or wider, within the bound.
No kernel may reach another device: no remote copies, remote signals or barrier semaphores. Data moves between devices by JAX's collectives and lax.ppermute only.
A program may use at most 64 MiB of HBM per device.

v0:
```python
import jax
import jax.numpy as jnp
from jax import lax
from jax.sharding import PartitionSpec as P

epsilon = 1e-05


def normalize(values):
    mean_value = jnp.mean(values, axis=-1, keepdims=True)
    centered = values - mean_value
    variance = jnp.mean(centered * centered, axis=-1, keepdims=True)
    return centered * lax.rsqrt(variance + epsilon)


def shards(
    alignment,
    alignment_mask,
    residue_mask,
    pair_features,
    outer_product_left,
    outer_product_right,
    outer_proj,
    triangle_proj,
    triangle_gate,
    triangle_out,
    transition_in,
    transition_out,
):
    block_rows, block_cols, channels = pair_features.shape
    inner = triangle_out.shape[0]
    narrow = outer_product_left.shape[1]
    mask_float = alignment_mask.astype(jnp.float32)
    normed = normalize(alignment.astype(jnp.float32)).astype(jnp.bfloat16)
    left_side = (
        jnp.dot(normed, outer_product_left, preferred_element_type=jnp.float32)
        * mask_float[..., None]
    ).astype(jnp.bfloat16)
    right_side = (
        jnp.dot(normed, outer_product_right, preferred_element_type=jnp.float32)
        * mask_float[..., None]
    ).astype(jnp.bfloat16)
    mask_wire = alignment_mask.astype(jnp.bfloat16)
    right_all, right_mask = (
        lax.all_gather(right_side, "row", axis=0, tiled=True),
        lax.all_gather(mask_wire, "row", axis=0, tiled=True),
    )
    left_rows, left_row_mask = (
        lax.all_gather(left_side, "col", axis=1, tiled=True),
        lax.all_gather(mask_wire, "col", axis=1, tiled=True),
    )
    left_all, left_mask = (
        lax.all_to_all(left_rows, "row", split_axis=1, concat_axis=0, tiled=True),
        lax.all_to_all(left_row_mask, "row", split_axis=1, concat_axis=0, tiled=True),
    )
    sequences = left_all.shape[0]
    contract = (((0,), (0,)), ((), ()))
    outer = lax.dot_general(
        left_all.reshape(sequences, block_rows * narrow),
        right_all.reshape(sequences, block_cols * narrow),
        contract,
        preferred_element_type=jnp.float32,
    )
    outer = (
        outer.reshape(block_rows, narrow, block_cols, narrow)
        .transpose(0, 2, 1, 3)
        .astype(jnp.bfloat16)
    )
    outer = outer.reshape(block_rows, block_cols, narrow * narrow)
    projected = jnp.dot(outer, outer_proj, preferred_element_type=jnp.float32)
    counts = lax.dot_general(left_mask, right_mask, contract, preferred_element_type=jnp.float32)
    first = (
        pair_features.astype(jnp.float32) + projected / jnp.maximum(counts, 1.0)[..., None]
    ).astype(jnp.bfloat16)
    normed_pair = normalize(first.astype(jnp.float32)).astype(jnp.bfloat16)
    projections = jnp.dot(normed_pair, triangle_proj, preferred_element_type=jnp.float32)
    row_mask = lax.dynamic_slice_in_dim(
        residue_mask, lax.axis_index("row") * block_rows, block_rows
    ).astype(jnp.float32)
    col_mask = lax.dynamic_slice_in_dim(
        residue_mask, lax.axis_index("col") * block_cols, block_cols
    ).astype(jnp.float32)
    pair_mask = (row_mask[:, None] * col_mask[None, :])[..., None]
    left_tri = (
        jax.nn.sigmoid(projections[..., :inner]) * projections[..., inner : 2 * inner] * pair_mask
    ).astype(jnp.bfloat16)
    right_tri = (
        jax.nn.sigmoid(projections[..., 2 * inner : 3 * inner])
        * projections[..., 3 * inner :]
        * pair_mask
    ).astype(jnp.bfloat16)
    right_cols = lax.all_gather(right_tri, "row", axis=0, tiled=True)
    right_rows = lax.all_to_all(right_cols, "col", split_axis=0, concat_axis=1, tiled=True)
    summed = jnp.einsum(
        "ikc,jkc->ijc",
        lax.all_gather(left_tri, "col", axis=1, tiled=True),
        right_rows,
        preferred_element_type=jnp.float32,
    )
    normed_sum = normalize(summed).astype(jnp.bfloat16)
    update = jax.nn.sigmoid(
        jnp.dot(normed_pair, triangle_gate, preferred_element_type=jnp.float32)
    ) * jnp.dot(normed_sum, triangle_out, preferred_element_type=jnp.float32)
    second = (first.astype(jnp.float32) + update).astype(jnp.bfloat16)
    normed_second = normalize(second.astype(jnp.float32)).astype(jnp.bfloat16)
    hidden_units = jnp.maximum(
        jnp.dot(normed_second, transition_in, preferred_element_type=jnp.float32), 0.0
    ).astype(jnp.bfloat16)
    return (
        second.astype(jnp.float32)
        + jnp.dot(hidden_units, transition_out, preferred_element_type=jnp.float32)
    ).astype(jnp.bfloat16)


def solution(mesh):
    placed = (
        P("row", "col", None),
        P("row", "col"),
        P(),
        P("row", "col", None),
        P(),
        P(),
        P(),
        P(),
        P(),
        P(),
        P(),
        P(),
    )
    return jax.shard_map(
        shards, mesh=mesh, in_specs=placed, out_specs=P("row", "col", None), check_vma=False
    )
```

profile of v0, /device:TPU:0, one launch (start us, length us, event | category | flops | bytes accessed | tf_op | source)
XLA Modules:
  0.0 276.2 jit_solution(16021958013082864905)
XLA Ops:
  6.5 0.8 fusion.48
  7.4 6.2 %all-gather = bf16[4,48,32]{1,2,0:T(8,128)(2,1)S(1)} all-gather(bf16[1,48,32]{1,2,0:T(8,128)(2,1)S(1)} %bitcast.93), channel_id=1, replica_groups=mesh['row'=8,'col'=4] {'col'}, dimensions={0}, use_global_device_ids=true | all-gather | bytes 15360 | tf_op jit(solution)/shard_map/all_gather | solution.py:50
  13.6 0.1 reshape.97
  13.7 0.1 copy.69
  13.8 0.7 reshape.110
  14.5 6.2 %all-to-all-start.1 = ((bf16[8,2,384]{2,1,0:T(2,128)(2,1)}), bf16[8,2,384]{2,1,0:T(2,128)(2,1)S(1)}, u32[]{:S(2)}, u32[]{:S(2)}) async-start(bf16[8,2,384]{2,1,0:T(2,128)(2,1)} %reshape.110), calls=%async_computation.1 | async-start | bytes 24576 | tf_op jit(solution)/shard_map/all_to_all | solution.py:54
  20.8 1.4 convert_reduce_fusion
  22.2 0.5 fusion.2
  22.7 0.0 copy-done.11
  22.7 0.7 fusion.16
  23.4 0.0 copy-start.12
  23.4 0.6 copy.51
  24.1 13.4 %all_gather.18 = bf16[32,192,32]{2,0,1:T(8,128)(2,1)} all-gather(bf16[32,48,32]{2,0,1:T(8,128)(2,1)S(1)} %copy.51), channel_id=1, replica_groups=mesh['row'=8,'col'=4] {'col'}, dimensions={1}, use_global_device_ids=true | all-gather | bytes 491520 | tf_op jit(solution)/shard_map/all_gather | solution.py:49
  37.4 0.7 fusion.17
  38.1 0.0 copy-start.13
  38.1 45.3 %all_gather.19 = bf16[256,48,32]{1,2,0:T(8,128)(2,1)S(1)} all-gather(bf16[32,48,32]{1,2,0:T(8,128)(2,1)S(1)} %fusion.17), channel_id=1, replica_groups=mesh['row'=8,'col'=4] {'row'}, dimensions={0}, use_global_device_ids=true | all-gather | bytes 884736 | tf_op jit(solution)/shard_map/all_gather | solution.py:45
  83.4 0.1 dynamic-slice_convert_fusion.1
  83.5 0.1 dynamic-slice_convert_fusion
  83.6 3.8 %reshape.108 = bf16[8,2,12288]{2,1,0:T(2,128)(2,1)} reshape(bf16[192,32,32]{2,1,0:T(8,128)(2,1)} %bitcast.89) | data formatting | bytes 786432
  87.4 2.4 copy.56
  89.8 0.0 all-to-all-done.1
  89.8 3.6 %all-to-all-start = ((bf16[8,2,12288]{2,1,0:T(2,128)(2,1)}), bf16[8,2,12288]{2,1,0:T(2,128)(2,1)S(1)}, u32[]{:S(2)}, u32[]{:S(2)}) async-start(bf16[8,2,12288]{2,1,0:T(2,128)(2,1)} %reshape.108), calls=%async_computation | async-start | bytes 786432 | tf_op jit(solution)/shard_map/all_to_all | solution.py:53
  93.4 0.0 all-gather.4.cloned.1.call-start
  93.4 35.2 %all_gather.21 = bf16[256,48]{1,0:T(8,128)(2,1)S(1)} all-gather(bf16[32,48]{1,0:T(8,128)(2,1)S(1)} %get-tuple-element.7), channel_id=1, replica_groups=mesh['row'=8,'col'=4] {'row'}, dimensions={0}, use_global_device_ids=true | all-gather | bytes 27648 | tf_op jit(solution)/shard_map/all_gather | solution.py:46
  128.6 0.1 broadcast_multiply_fusion.1
  128.7 0.1 reshape.111
  128.8 0.1 all_to_all.44
  128.9 0.1 convolution_maximum_fusion
  129.0 0.0 all-to-all-done
  129.0 0.8 reshape.109
  129.8 0.6 copy.53
  130.4 1.0 reshape.93
  131.4 0.2 copy.54
  131.6 3.7 %convert_bitcast_fusion = bf16[24,48,32,32]{1,2,3,0:T(8,128)(2,1)} fusion(bf16[24,32,256,1]{2,1,3,0:T(8,128)(2,1)S(1)} %bitcast.90, bf16[48,32,256]{2,0,1:T(8,128)(2,1)S(1)} %copy-done.4), kind=kOutput, calls=%fused_computation | convolution fusion | flops 605159424 | bytes 3538944 | tf_op jit(solution)/shard_map/dot_general | solution.py:58
  135.3 17.8 %copy.57 = bf16[24,48,32,32]{3,2,1,0:T(8,128)(2,1)} copy(bf16[24,48,32,32]{1,2,3,0:T(8,128)(2,1)} %convert_bitcast_fusion) | data formatting | bytes 4718592 | tf_op jit(solution)/shard_map/convert_element_type | solution.py:67
  153.1 12.7 %reshape.95 = bf16[24,48,1024]{2,1,0:T(8,128)(2,1)S(1)} reshape(bf16[24,48,32,32]{3,2,1,0:T(8,128)(2,1)} %copy.57) | data formatting | bytes 4718592 | tf_op jit(solution)/shard_map/reshape | solution.py:69
  165.9 0.0 copy-start.6
  165.9 1.8 fusion.49
  167.8 0.4 multiply_reduce_fusion.2
  168.2 0.5 fusion.41
  168.7 1.2 fusion.22
  169.9 0.0 all-gather.4.cloned.1.call-update
  169.9 0.0 all-gather.6.cloned.1.call-start
  170.0 0.7 all-gather.6.cloned.1.call-update
  170.7 0.0 copy-start.10
  170.7 48.0 %all-gather.4.cloned.1.call-done = bf16[192,48,128]{2,1,0:T(8,128)(2,1)} async-done(((bf16[24,48,128]{2,1,0:T(8,128)(2,1)}), bf16[192,48,128]{2,1,0:T(8,128)(2,1)}) %all-gather.4.cloned.1.call-update) | async-done | bytes 2359312 | tf_op jit(solution)/shard_map/all_gather | solution.py:92
  218.7 3.9 %all-to-all-start.2 = ((bf16[192,48,128]{2,1,0:T(8,128)(2,1)}), bf16[192,48,128]{2,1,0:T(8,128)(2,1)S(1)}, u32[]{:S(2)}, u32[]{:S(2)}) async-start(bf16[192,48,128]{2,1,0:T(8,128)(2,1)} %all-gather.4.cloned.1.call-done), calls=%async_computation.2 | async-start | bytes 4718592 | tf_op jit(solution)/shard_map/all_to_all | solution.py:93
  222.6 1.3 fusion.9
  223.9 18.8 %all-gather.6.cloned.1.call-done = bf16[24,192,128]{2,1,0:T(8,128)(2,1)} async-done(((bf16[24,48,128]{2,1,0:T(8,128)(2,1)}), bf16[24,192,128]{2,1,0:T(8,128)(2,1)}) %all-gather.6.cloned.1.call-update) | async-done | bytes 1179664 | tf_op jit(solution)/shard_map/all_gather | solution.py:96
  242.7 2.8 %copy.63 = bf16[24,192,128]{1,0,2:T(8,128)(2,1)} copy(bf16[24,192,128]{2,1,0:T(8,128)(2,1)} %all-gather.6.cloned.1.call-done) | data formatting | bytes 2359296 | tf_op jit(solution)/shard_map/all_gather | solution.py:96
  245.5 11.6 %all-to-all-done.2 = bf16[192,48,128]{2,1,0:T(8,128)(2,1)S(1)} async-done(((bf16[192,48,128]{2,1,0:T(8,128)(2,1)}), bf16[192,48,128]{2,1,0:T(8,128)(2,1)S(1)}, u32[]{:S(2)}, u32[]{:S(2)}) %all-to-all-start.2) | async-done | bytes 2359328 | tf_op jit(solution)/shard_map/all_to_all | solution.py:93
  257.1 2.1 copy.61
  259.2 3.8 %copy.62 = bf16[48,192,128]{1,0,2:T(8,128)(2,1)S(1)} copy(bf16[48,192,128]{2,1,0:T(8,128)(2,1)} %bitcast.86) | data formatting | bytes 4718592 | tf_op jit(solution)/shard_map/all_to_all | solution.py:93
  263.0 2.4 bitcast_reduce_fusion
  265.4 0.3 multiply_reduce_fusion
  265.6 0.0 copy-start.7
  265.7 0.2 multiply_convert_fusion
  265.9 0.8 copy-done.2
  266.7 0.2 copy-done.5
  266.9 0.5 fusion.50
  267.4 0.4 multiply_reduce_fusion.1
  267.8 0.0 copy-done.8
  267.8 0.0 copy-done.9
  267.8 1.5 fusion.15
  (29 shorter events, 0.1 us)
Async XLA Ops:
  6.5 159.3 %copy-start = (bf16[1024,128]{1,0:T(8,128)(2,1)S(1)}, bf16[1024,128]{1,0:T(8,128)(2,1)}, u32[]{:S(2)}) copy-start(bf16[1024,128]{1,0:T(8,128)(2,1)} %param.18) | copy-start | bytes 786436
  6.5 15.7 %copy-start.3 = (bf16[32,48,256]{2,1,0:T(8,128)(2,1)S(1)}, bf16[32,48,256]{2,1,0:T(8,128)(2,1)}, u32[]{:S(2)}) copy-start(bf16[32,48,256]{2,1,0:T(8,128)(2,1)} %param.12) | copy-start | bytes 2359300
  6.5 16.2 %copy-start.11 = (bf16[256,32]{0,1:T(8,128)(2,1)S(1)}, bf16[256,32]{0,1:T(8,128)(2,1)}, u32[]{:S(2)}) copy-start(bf16[256,32]{0,1:T(8,128)(2,1)} %param.16) | copy-start | bytes 49156
  14.5 75.3 %all-to-all-start.1 = ((bf16[8,2,384]{2,1,0:T(2,128)(2,1)}), bf16[8,2,384]{2,1,0:T(2,128)(2,1)S(1)}, u32[]{:S(2)}, u32[]{:S(2)}) async-start(bf16[8,2,384]{2,1,0:T(2,128)(2,1)} %reshape.110), calls=%async_computation.1 | async-start | bytes 24576 | tf_op jit(solution)/shard_map/all_to_all | solution.py:54
  23.4 14.0 %copy-start.12 = (bf16[256,32]{0,1:T(8,128)(2,1)S(1)}, bf16[256,32]{0,1:T(8,128)(2,1)}, u32[]{:S(2)}) copy-start(bf16[256,32]{0,1:T(8,128)(2,1)} %param.17) | copy-start | bytes 49156
  38.1 45.4 %copy-start.13 = (s32[192]{0:T(256)S(1)}, s32[192]{0:T(256)}, u32[]{:S(2)}) copy-start(s32[192]{0:T(256)} %param.14) | copy-start | bytes 2308
  89.8 39.2 %all-to-all-start = ((bf16[8,2,12288]{2,1,0:T(2,128)(2,1)}), bf16[8,2,12288]{2,1,0:T(2,128)(2,1)S(1)}, u32[]{:S(2)}, u32[]{:S(2)}) async-start(bf16[8,2,12288]{2,1,0:T(2,128)(2,1)} %reshape.108), calls=%async_computation | async-start | bytes 786432 | tf_op jit(solution)/shard_map/all_to_all | solution.py:53
  93.4 125.3 %all-gather.4.cloned.1.call-start = ((), (), s32[]{:S(2)}) async-start(), calls=%async_computation.3 | async-start | bytes 2654208 | tf_op jit(solution)/shard_map/all_gather | solution.py:92
  130.4 1.2 copy-start.4
  165.9 2.3 copy-start.6
  167.7 54.8 %copy-start.1 = (f32[24,48,128]{2,1,0:T(8,128)}, f32[24,48,128]{2,1,0:T(8,128)S(1)}, u32[]{:S(2)}) copy-start(f32[24,48,128]{2,1,0:T(8,128)S(1)} %get-tuple-element.10) | copy-start | bytes 1769476
  169.9 72.8 %all-gather.6.cloned.1.call-start = ((), (), s32[]{:S(2)}) async-start(), calls=%async_computation.4 | async-start | bytes 1474560 | tf_op jit(solution)/shard_map/all_gather | solution.py:96
  170.7 51.9 %copy-start.10 = (bf16[128,128]{1,0:T(8,128)(2,1)S(1)}, bf16[128,128]{1,0:T(8,128)(2,1)}, u32[]{:S(2)}) copy-start(bf16[128,128]{1,0:T(8,128)(2,1)} %param.20) | copy-start | bytes 98308
  218.7 38.4 %all-to-all-start.2 = ((bf16[192,48,128]{2,1,0:T(8,128)(2,1)}), bf16[192,48,128]{2,1,0:T(8,128)(2,1)S(1)}, u32[]{:S(2)}, u32[]{:S(2)}) async-start(bf16[192,48,128]{2,1,0:T(8,128)(2,1)} %all-gather.4.cloned.1.call-done), calls=%async_computation.2 | async-start | bytes 4718592 | tf_op jit(solution)/shard_map/all_to_all | solution.py:93
  265.6 1.1 copy-start.2
  265.6 1.2 copy-start.5
  265.6 1.2 copy-start.7
  266.9 0.9 copy-start.8
  266.9 1.0 copy-start.9
Sparse Core Ops, SparseCore 0:
  170.0 48.6 all-gather.3
  220.2 22.3 all-gather.5
where the time goes:
time: 277 us; the launch traced here: 276 us
  blocking collectives  100 us (36%)
  waiting for transfers between devices  79.1 us (29%)
  local copies, waits for them, and re-layouts  50.8 us (18%)
  starting transfers between devices  13.7 us (5%)
  between operations  13.7 us (5%)
  matrix products  13.2 us (5%)
  other arithmetic  5.45 us (2%)
    all_gather x1, waiting for transfers between devices, shards(): right_cols = lax.all_gather(right_tri, 'row', axis=0, tiled=True)  48 us
    all_gather x1, blocking collectives, shards(): lax.all_gather(right_side, 'row', axis=0, tiled=True)  45.3 us
    all_gather x1, blocking collectives, shards(): lax.all_gather(mask_wire, 'row', axis=0, tiled=True)  35.2 us
    all_gather x1, waiting for transfers between devices, shards(): lax.all_gather(left_tri, 'col', axis=1, tiled=True)  18.8 us
    convert_element_type x1, local copies, waits for them, and re-layouts, shards(): outer = outer.reshape(block_rows, narrow, block_cols, narrow).transpose(0...  17.8 us
    all_gather x1, blocking collectives, shards(): lax.all_gather(left_side, 'col', axis=1, tiled=True)  13.4 us
    reshape x1, local copies, waits for them, and re-layouts, shards(): outer = outer.reshape(block_rows, block_cols, narrow * narrow)  12.7 us
    all_to_all x1, waiting for transfers between devices, shards(): lax.all_to_all(right_cols, 'col', split_axis=0, concat_axis=1, tiled=True)  11.6 us
  transfers between devices with their start and end apart: 5, of which 3 were waited for; matrix products, arithmetic and copies ran while one was open for 5% of the time, Pallas kernels for 0%

commit v1 on v0

v1 whole, which is shorter than its diff:
```python
import functools

import jax
import jax.numpy as jnp
from jax import lax
from jax.experimental import pallas as pl
from jax.experimental.pallas import tpu as pltpu
from jax.sharding import PartitionSpec as P

epsilon = 1e-05
LANES = 128
BF16 = jnp.bfloat16
F32 = jnp.float32
NT = (((1,), (1,)), ((), ()))
TN = (((0,), (0,)), ((), ()))


def matmul(a, b, dims=(((1,), (0,)), ((), ()))):
    return lax.dot_general(a, b, dims, preferred_element_type=F32)


def iota(shape, axis):
    return lax.broadcasted_iota(jnp.int32, shape, axis)


def normalize(values, axis=-1):
    mean_value = jnp.mean(values, axis=axis, keepdims=True)
    centered = values - mean_value
    variance = jnp.mean(centered * centered, axis=axis, keepdims=True)
    return centered * lax.rsqrt(variance + epsilon)


def params(cost=None):
    return dict(
        compiler_params=pltpu.CompilerParams(vmem_limit_bytes=56 * 1024 * 1024),
        cost_estimate=cost,
    )


VMEM = pl.BlockSpec(memory_space=pltpu.VMEM)
SMEM = pl.BlockSpec(memory_space=pltpu.SMEM)


def side_kernel(
    sequences, cols, half, copies, narrow,
    index_ref, align_ref, mask_ref, left_w_ref, right_w_ref,
    right_ref, left_ref, left_projected, right_projected,
):
    members = LANES // narrow
    rows = sequences * cols
    chunk = rows // 12 if rows % (12 * 16) == 0 else rows
    left_w = jnp.concatenate([left_w_ref[...]] * members, axis=1)
    right_w = jnp.concatenate([right_w_ref[...]] * members, axis=1)

    def project(step, carry):
        start = pl.multiple_of(step * chunk, chunk)
        normed = normalize(align_ref[pl.ds(start, chunk), :].astype(F32)).astype(BF16)
        left_projected[pl.ds(start, chunk), :] = matmul(normed, left_w)
        right_projected[pl.ds(start, chunk), :] = matmul(normed, right_w)
        return carry

    lax.fori_loop(0, rows // chunk, project, 0)
    mask = mask_ref[...].astype(BF16)
    lane = iota((sequences, LANES), 1)

    def group_of(projected, first, groups, group):
        value = None
        for member in range(members):
            j = first + member * groups + group
            part = projected[pl.ds(j, sequences, stride=cols), :]
            value = part if value is None else jnp.where(lane >= member * narrow, part, value)
        return value

    def spread(first, groups):
        width = groups * LANES
        at = iota((cols, width), 1)
        residue = first + (at % LANES) // narrow * groups + at // LANES
        return matmul(mask, (iota((cols, width), 0) == residue).astype(BF16))

    def mask_lanes(first, count):
        pick = iota((cols, LANES), 0) - first == iota((cols, LANES), 1)
        pick = pick & (iota((cols, LANES), 1) < count)
        return matmul(mask, pick.astype(BF16)).astype(BF16)

    groups = cols // members
    masks = spread(0, groups)
    for group in range(groups):
        at = slice(group * LANES, (group + 1) * LANES)
        value = (group_of(right_projected, 0, groups, group) * masks[:, at]).astype(BF16)
        for copy in range(copies):
            right_ref[copy, :, at] = value
    tail = mask_lanes(0, cols)
    for copy in range(copies):
        right_ref[copy, :, groups * LANES :] = tail
    halves = cols // half
    groups = half // members
    turn = index_ref[0]
    for h in range(halves):
        place = lax.rem(h - turn + halves, halves)
        masks = spread(h * half, groups)
        for group in range(groups):
            at = slice(group * LANES, (group + 1) * LANES)
            value = group_of(left_projected, h * half, groups, group) * masks[:, at]
            left_ref[place, :, at] = value.astype(BF16)
        left_ref[place, :, groups * LANES :] = mask_lanes(h * half, half)


def outer_kernel(
    rows, cols, narrow, width, turns,
    index_ref, left_ref, right_ref, pair_ref, proj_ref, tri_ref, pair_mask_ref,
    first_ref, normed_ref, tri_out_ref, left_t, stacked, spread_w, moved,
):
    members = LANES // narrow
    left_groups, groups = rows // members, cols // members
    left_width, right_width = rows * narrow, cols * narrow
    sources = left_ref.shape[0]
    h = index_ref[0]
    left = jnp.concatenate(
        [left_ref[c, lax.rem(h - t + turns, turns)] for c in range(sources) for t in range(turns)], axis=0
    )
    right_mask = right_ref[:, right_width:]
    left_mask = left[:, left_width:]
    left = left[:, :left_width]
    at = iota((left_width, left_width), 0)
    channel, residue = at // rows, at % rows
    column = residue % left_groups * LANES + residue // left_groups * narrow + channel
    pick = (iota((left_width, left_width), 1) == column).astype(BF16)
    left_t[...] = matmul(pick, left, NT).astype(BF16)
    spread_w[...] = jnp.zeros_like(spread_w)
    for c in range(narrow):
        part = proj_ref[c * narrow : (c + 1) * narrow, :]
        for m in range(members):
            start = c * LANES + m * narrow
            spread_w[start : start + narrow, m * width : (m + 1) * width] = part
    step = 8
    for first in range(0, narrow, step):
        block = matmul(left_t[first * rows : (first + step) * rows, :], right_ref[:, :right_width])
        for c in range(step):
            lanes = slice((first + c) * LANES, (first + c + 1) * LANES)
            for g in range(0, groups, 2):
                two = [
                    block[c * rows : (c + 1) * rows, (g + n) * LANES : (g + n + 1) * LANES] for n in range(2)
                ]
                stacked[g * rows : (g + 2) * rows, lanes] = jnp.concatenate(two, axis=0).astype(BF16)
    total = matmul(stacked[...], spread_w[...])
    counts = matmul(left_mask, right_mask, TN)[:rows, :]
    scale = 1.0 / jnp.maximum(counts, 1.0)
    for m in range(members):
        for g in range(groups):
            j = m * groups + g
            part = total[g * rows : (g + 1) * rows, m * width : (m + 1) * width]
            moved[j * rows : (j + 1) * rows, :] = part * scale[:, j : j + 1]
    for i in range(rows):
        at = slice(i * cols, (i + 1) * cols)
        first = pair_ref[at, :].astype(F32) + moved[pl.ds(i, cols, stride=rows), :]
        first = first.astype(BF16)
        first_ref[at, :] = first
        normed_ref[at, :] = normalize(first.astype(F32)).astype(BF16)
    devices = tri_out_ref.shape[0]
    own = width // devices
    at = iota((4 * width, 4 * width), 0)
    kind, rest = at // (2 * width), at % (2 * width)
    owner, side, channel = rest // (2 * own), rest // own % 2, rest % own
    column = side * 2 * width + kind * width + owner * own + channel
    pick = (iota((4 * width, 4 * width), 1) == column).astype(BF16)
    weights = matmul(pick, tri_ref[...], NT).astype(BF16)
    projections = matmul(weights, normed_ref[...], NT)
    gated = jax.nn.sigmoid(projections[: 2 * width]) * projections[2 * width :] * pair_mask_ref[...]
    gated = gated.astype(BF16)
    for d in range(devices):
        tri_out_ref[d] = gated[d * 2 * own : (d + 1) * 2 * own, :]


def triangle_kernel(row_count, col_count, rows, cols, own, given_ref, out_ref, opened, summed):
    residues = row_count * rows
    pair = 2 * own
    planes = opened.shape[0]
    each = -(-col_count // planes)

    def open_row(r, carry):
        for c in range(col_count):
            value = given_ref[r * col_count + c].astype(F32)
            lanes = slice(c % each * cols, (c % each + 1) * cols)
            for i in range(rows):
                start = pl.multiple_of((r * rows + i) * pair, pair)
                opened[c // each, pl.ds(start, pair), lanes] = value[:, i * cols : (i + 1) * cols]
        return carry

    lax.fori_loop(0, row_count, open_row, 0)
    used = each * cols
    for t in range(own):
        left = [opened.at[p][pl.ds(t, residues, stride=pair), :].astype(BF16) for p in range(planes)]
        right = [opened.at[p][pl.ds(own + t, residues, stride=pair), :].astype(BF16) for p in range(planes)]
        for q in range(planes):
            total = None
            for p in range(planes):
                width = min(each, col_count - p * each) * cols
                some = right[p][q * used : min((q + 1) * used, residues), :width]
                if some.shape[0] < LANES:
                    some = jnp.concatenate([some, jnp.zeros((LANES - some.shape[0], width), BF16)], axis=0)
                term = matmul(left[p][:, :width], some, NT)
                total = term if total is None else total + term
            summed.at[q][pl.ds(t, residues, stride=pair), :] = total

    def close_row(r, carry):
        for c in range(col_count):
            lanes = slice(c % each * cols, (c % each + 1) * cols)
            parts = []
            for i in range(rows):
                start = pl.multiple_of((r * rows + i) * pair, pair)
                parts.append(summed[c // each, pl.ds(start, pair), lanes])
            out_ref[r * col_count + c] = jnp.concatenate(parts, axis=1)[:own].astype(BF16)
        return carry

    lax.fori_loop(0, row_count, close_row, 0)


def triangle_by_channel(row_count, col_count, rows, cols, gated):
    devices, pair, places = gated.shape
    own = pair // 2
    gated = lax.all_to_all(gated, ("row", "col"), split_axis=0, concat_axis=0, tiled=True)
    residues = row_count * rows
    planes = -(-col_count // (LANES // cols))
    summed = pl.pallas_call(
        functools.partial(triangle_kernel, row_count, col_count, rows, cols, own),
        out_shape=jax.ShapeDtypeStruct((devices, own, places), BF16),
        in_specs=[VMEM],
        out_specs=VMEM,
        scratch_shapes=[pltpu.VMEM((planes, residues * 2 * own, LANES), F32)] * 2,
        **params(),
    )(gated)
    summed = lax.all_to_all(summed, ("row", "col"), split_axis=0, concat_axis=0, tiled=True)
    return summed.reshape(devices * own, places)


def triangle_by_residue(row_count, col_count, rows, cols, gated):
    _, pair, places = gated.shape
    both = gated.reshape(2, pair // 2, rows, cols).transpose(0, 2, 3, 1)
    right = lax.all_gather(both[1], "row", axis=0, tiled=True)
    right = lax.all_to_all(right, "col", split_axis=0, concat_axis=1, tiled=True)
    left = lax.all_gather(both[0], "col", axis=1, tiled=True)
    summed = jnp.einsum("ikc,jkc->cij", left, right, preferred_element_type=F32)
    return summed.reshape(pair // 2, places).astype(BF16)


def tail_kernel(first_ref, normed_ref, summed_ref, gate_ref, out_w_ref, in_ref, back_ref, out_ref):
    normed_sum = normalize(summed_ref[...].astype(F32), 0).astype(BF16)
    gate = jax.nn.sigmoid(matmul(gate_ref[...].T, normed_ref[...], NT))
    update = gate * matmul(out_w_ref[...].T, normed_sum)
    second = (first_ref[...].astype(F32).T + update).astype(BF16).astype(F32)
    normed_second = normalize(second, 0).astype(BF16)
    hidden = jnp.maximum(matmul(in_ref[...].T, normed_second), 0.0).astype(BF16)
    result = second + matmul(back_ref[...].T, hidden)
    out_ref[...] = result.T.astype(BF16)


def shards(
    row_count, col_count, alignment, alignment_mask, residue_mask, pair_features, outer_product_left, outer_product_right,
    outer_proj, triangle_proj, triangle_gate, triangle_out, transition_in, transition_out,
):
    rows, cols, width = pair_features.shape
    sequences, _, channels = alignment.shape
    narrow = outer_product_left.shape[1]
    inner = triangle_out.shape[0]
    devices = row_count * col_count
    turns = cols // rows
    places = rows * cols
    r, c = lax.axis_index("row"), lax.axis_index("col")
    turn = (r % turns).astype(jnp.int32).reshape(1)

    members = LANES // narrow
    right_lanes = cols * narrow + LANES
    left_lanes = rows * narrow + LANES
    right, left = pl.pallas_call(
        functools.partial(side_kernel, sequences, cols, rows, row_count, narrow),
        out_shape=(
            jax.ShapeDtypeStruct((row_count, sequences, right_lanes), BF16),
            jax.ShapeDtypeStruct((turns, sequences, left_lanes), BF16),
        ),
        in_specs=[SMEM] + [VMEM] * 4,
        out_specs=(VMEM, VMEM),
        scratch_shapes=[pltpu.VMEM((sequences * cols, LANES), F32)] * 2,
        **params(),
    )(turn, alignment.reshape(sequences * cols, channels), alignment_mask, outer_product_left, outer_product_right)

    sent = []
    for p in range(turns):
        route = []
        for source_row in range(row_count):
            for source_col in range(col_count):
                to_row = turns * source_col + (source_row + p) % turns
                route.append((source_row * col_count + source_col, to_row * col_count + source_row // turns))
        sent.append(lax.ppermute(left[p], ("row", "col"), route))
    left = jnp.stack(sent)
    left = lax.all_to_all(
        jnp.broadcast_to(left[None], (col_count,) + left.shape), "col", split_axis=0, concat_axis=0, tiled=True
    )
    right = lax.all_to_all(right, "row", split_axis=0, concat_axis=0, tiled=True)
    right = right.reshape(row_count * sequences, right_lanes)

    residue_float = residue_mask.astype(F32)
    row_mask = lax.dynamic_slice_in_dim(residue_float, r * rows, rows)
    col_mask = lax.dynamic_slice_in_dim(residue_float, c * cols, cols)
    pair_mask = (row_mask[:, None] * col_mask[None, :]).reshape(1, places)

    by_channel = inner % devices == 0
    owners = devices if by_channel else 1
    own = inner // owners
    first, normed_pair, gated = pl.pallas_call(
        functools.partial(outer_kernel, rows, cols, narrow, width, turns),
        out_shape=(
            jax.ShapeDtypeStruct((places, width), BF16),
            jax.ShapeDtypeStruct((places, width), BF16),
            jax.ShapeDtypeStruct((owners, 2 * own, places), BF16),
        ),
        in_specs=[SMEM] + [VMEM] * 6,
        out_specs=(VMEM,) * 3,
        scratch_shapes=[
            pltpu.VMEM((rows * narrow, row_count * sequences), BF16),
            pltpu.VMEM((cols // members * rows, narrow * LANES), BF16),
            pltpu.VMEM((narrow * LANES, members * width), BF16),
            pltpu.VMEM((places, width), F32),
        ],
        **params(),
    )(turn, left, right, pair_features.reshape(places, width), outer_proj, triangle_proj, pair_mask)

    triangle = triangle_by_channel if by_channel else triangle_by_residue
    summed = triangle(row_count, col_count, rows, cols, gated)
    out = pl.pallas_call(
        tail_kernel,
        out_shape=jax.ShapeDtypeStruct((places, width), BF16),
        in_specs=[VMEM] * 7,
        out_specs=VMEM,
        **params(),
    )(first, normed_pair, summed, triangle_gate, triangle_out, transition_in, transition_out)
    return out.reshape(rows, cols, width)


def solution(mesh):
    placed = (
        P("row", "col", None),
        P("row", "col"),
        P(),
        P("row", "col", None),
    ) + (P(),) * 8
    body = functools.partial(shards, mesh.shape["row"], mesh.shape["col"])
    return jax.shard_map(body, mesh=mesh, in_specs=placed, out_specs=P("row", "col", None), check_vma=False)
```

time: 277 us -> 111 us (0.40)
  waiting for transfers between devices: 79.1 us -> 22.2 us
  blocking collectives: 100 us -> 53.7 us
  local copies, waits for them, and re-layouts: 50.8 us -> 6.28 us
  Pallas kernels: 0 us -> 21 us
  between operations: 13.7 us -> 0.04 us
  matrix products: 13.2 us -> 0 us
  starting transfers between devices: 13.7 us -> 7.53 us
  other arithmetic: 5.45 us -> 0.09 us
    all_gather x4 -> x0, blocking collectives: 100 us -> none  [the longest x1 45.3 us: shards(): lax.all_gather(right_side, 'row', axis=0, tiled=True)]
    all_gather x2 -> x0, waiting for transfers between devices: 66.8 us -> none  [the longest x1 48 us: shards(): right_cols = lax.all_gather(right_tri, 'row', axis=0, tiled=True)]
    all_to_all x0 -> x3, blocking collectives: none -> 53.7 us  [the longest x1 20.1 us: triangle_by_channel(): lax.all_to_all(gated, ('row', 'col'), split_axis=0, concat_axis=0, tiled=...]
    pallas_call x0 -> x4, Pallas kernels: none -> 21 us  [the longest x1 6.92 us: shards(): pl.pallas_call(functools.partial(outer_kernel, rows, cols, narrow, width,...]
    convert_element_type x2 -> x0, local copies, waits for them, and re-layouts: 18.4 us -> none  [the longest x1 17.8 us: shards(): outer = outer.reshape(block_rows, narrow, block_cols, narrow).transpose(0...]
    dot_general x10 -> x0, matrix products: 13.2 us -> none  [the longest x1 3.7 us: shards(): lax.dot_general(left_all.reshape(sequences, block_rows * narrow), right_a...]
    reshape x2 -> x1, local copies, waits for them, and re-layouts: 13.7 us -> 0.78 us  [triangle_by_channel(): return summed.reshape(devices * own, places)]
    all_to_all x3 -> x1, starting transfers between devices: 13.7 us -> 3.83 us  [shards(): lax.all_to_all(right, 'row', split_axis=0, concat_axis=0, tiled=True)]
  transfers between devices with their start and end apart: 5 -> 3, of which waited for: 3 -> 2; matrix products, arithmetic and copies ran while one was open for 5% -> 1% of each run, Pallas kernels for 0% -> 0%
where the time goes in v1:
time: 111 us
  blocking collectives  53.7 us (48%)
  waiting for transfers between devices  22.2 us (20%)
  Pallas kernels  21 us (19%)
  starting transfers between devices  7.53 us (7%)
  local copies, waits for them, and re-layouts  6.28 us (6%)
    all_to_all x1, blocking collectives, triangle_by_channel(): lax.all_to_all(gated, ('row', 'col'), split_axis=0, concat_axis=0, tiled=...  20.1 us
    all_to_all x1, waiting for transfers between devices, shards(): lax.all_to_all(right, 'row', split_axis=0, concat_axis=0, tiled=True)  20 us
    all_to_all x1, blocking collectives, shards(): lax.all_to_all(jnp.broadcast_to(left[None], (col_count,) + left.shape), '...  19.1 us
    all_to_all x1, blocking collectives, triangle_by_channel(): lax.all_to_all(summed, ('row', 'col'), split_axis=0, concat_axis=0, tiled...  14.5 us
    pallas_call x1, Pallas kernels, shards(): pl.pallas_call(functools.partial(outer_kernel, rows, cols, narrow, width,...  6.92 us
    pallas_call x1, Pallas kernels, shards(): pl.pallas_call(functools.partial(side_kernel, sequences, cols, rows, row_...  6.74 us
    pallas_call x1, Pallas kernels, triangle_by_channel(): pl.pallas_call(functools.partial(triangle_kernel, row_count, col_count, r...  4.19 us
    all_to_all x1, starting transfers between devices, shards(): lax.all_to_all(right, 'row', split_axis=0, concat_axis=0, tiled=True)  3.83 us
  transfers between devices with their start and end apart: 3, of which 2 were waited for; matrix products, arithmetic and copies ran while one was open for 1% of the time, Pallas kernels for 0%

profile of v1, /device:TPU:0, one launch (start us, length us, event | category | flops | bytes accessed | tf_op | source)
XLA Modules:
  0.0 110.8 jit_solution(1687126303491448246)
XLA Ops:
  0.0 0.0 copy-start.1
  0.0 0.7 copy-done.1
  0.7 0.0 copy-start.2
  0.7 0.7 copy.13.left_w_ref
  1.4 0.0 copy-done.2
  1.4 0.7 copy.14.right_w_ref
  2.2 6.7 %shard_map.118 = (bf16[8,32,1664]{2,1,0:T(8,128)(2,1)}, bf16[2,32,896]{2,1,0:T(8,128)(2,1)}) custom-call(s32[1]{0:T(128)} %bitcast.index_ref, bf16[1536,256]{1,0:T(8,128)(2,1)} %bitcast.12, s32[32,48]{1,0:T(8,128)} %mask_ref.1, bf16[256,32]{1,0:T(8,128)(2,1)} %copy.13.left_w_ref, bf16[256,32]{1,0:T(8,128)(2,1)} %copy.14.right_w_ref), custom_call_target="tpu_custom_call" | custom-call | tf_op jit(solution)/shard_map/pallas_call | solution.py:274
  8.9 0.9 slice_bitcast_fusion.1
  9.8 0.7 collective-permute-start
  10.4 3.0 %collective-permute-start.1 = (bf16[32,896]{1,0:T(8,128)(2,1)S(1)}, bf16[32,896]{1,0:T(8,128)(2,1)S(1)}, u32[]{:S(2)}, u32[]{:S(2)}) collective-permute-start(bf16[32,896]{1,0:T(8,128)(2,1)S(1)} %get-tuple-element.16), channel_id=1, source_target_pairs={{0,4},{1,12},{2,20},{3,28},{4,0},{5,8},{6,16},{7,24},{8,5},{9,13},... | collective-permute-start | bytes 172040 | tf_op jit(solution)/shard_map/ppermute | solution.py:293
  13.5 0.0 collective-permute-done
  13.5 2.2 %collective-permute-done.1 = bf16[32,896]{1,0:T(8,128)(2,1)S(1)} collective-permute-done((bf16[32,896]{1,0:T(8,128)(2,1)S(1)}, bf16[32,896]{1,0:T(8,128)(2,1)S(1)}, u32[]{:S(2)}, u32[]{:S(2)}) %collective-permute-start.1) | collective-permute-done | bytes 57376 | tf_op jit(solution)/shard_map/ppermute | solution.py:293
  15.7 19.1 %all_to_all.20.left_ref = bf16[4,2,32,896]{3,2,1,0:T(8,128)(2,1)} all-to-all(bf16[4,2,32,896]{3,2,1,0:T(8,128)(2,1)S(1)} %broadcast_in_dim.2), channel_id=1, replica_groups=mesh['row'=8,'col'=4] {'col'}, dimensions={0} | all-to-all | bytes 917504 | tf_op jit(solution)/shard_map/all_to_all | solution.py:295
  34.7 3.8 %all-to-all-start.1 = ((bf16[8,32,1664]{2,1,0:T(8,128)(2,1)}), bf16[8,32,1664]{2,1,0:T(8,128)(2,1)S(1)}, u32[]{:S(2)}, u32[]{:S(2)}) async-start(bf16[8,32,1664]{2,1,0:T(8,128)(2,1)} %get-tuple-element.11), calls=%async_computation.1 | async-start | bytes 1703936 | tf_op jit(solution)/shard_map/all_to_all | solution.py:298
  38.6 0.0 copy-start.3
  38.6 0.7 copy-done.3
  39.3 0.1 dynamic_slice.7
  39.3 0.1 dynamic_slice.6
  39.4 0.1 broadcast_multiply_fusion
  39.5 0.7 mul.34.pair_mask_ref
  40.2 20.0 %all-to-all-done.1 = bf16[8,32,1664]{2,1,0:T(8,128)(2,1)S(1)} async-done(((bf16[8,32,1664]{2,1,0:T(8,128)(2,1)}), bf16[8,32,1664]{2,1,0:T(8,128)(2,1)S(1)}, u32[]{:S(2)}, u32[]{:S(2)}) %all-to-all-start.1) | async-done | bytes 852000 | tf_op jit(solution)/shard_map/all_to_all | solution.py:298
  60.2 0.0 copy-start
  60.2 0.9 copy-done
  61.1 6.9 %shard_map.119 = (bf16[1152,128]{1,0:T(8,128)(2,1)}, bf16[1152,128]{1,0:T(8,128)(2,1)}, bf16[32,8,1152]{2,1,0:T(8,128)(2,1)}) custom-call(s32[1]{0:T(128)} %bitcast.index_ref, bf16[4,2,32,896]{3,2,1,0:T(8,128)(2,1)} %all_to_all.20.left_ref, bf16[256,1664]{1,0:T(8,128)(2,1)} %bitcast.11, bf16[1152,128]{1,0:T(8,128)(2,1)} %bitcast.13, ...), custom_call_target="tpu_custom_call" | custom-call | tf_op jit(solution)/shard_map/pallas_call | solution.py:309
  68.0 20.1 %all_to_all.21.given_ref = bf16[32,8,1152]{2,1,0:T(8,128)(2,1)} all-to-all(bf16[32,8,1152]{2,1,0:T(8,128)(2,1)} %get-tuple-element.14), channel_id=1, replica_groups=mesh['row'=8,'col'=4] {'row','col'}, dimensions={0} | all-to-all | bytes 1179648 | tf_op jit(solution)/shard_map/all_to_all | solution.py:221
  88.1 4.2 %shard_map.120 = bf16[32,4,1152]{2,1,0:T(4,128)(2,1)} custom-call(bf16[32,8,1152]{2,1,0:T(8,128)(2,1)} %all_to_all.21.given_ref), custom_call_target="tpu_custom_call" | custom-call | tf_op jit(solution)/shard_map/pallas_call | solution.py:224
  92.3 14.5 %all_to_all.22 = bf16[32,4,1152]{2,1,0:T(4,128)(2,1)S(1)} all-to-all(bf16[32,4,1152]{2,1,0:T(4,128)(2,1)} %shard_map.120), channel_id=1, replica_groups=mesh['row'=8,'col'=4] {'row','col'}, dimensions={0} | all-to-all | bytes 589824 | tf_op jit(solution)/shard_map/all_to_all | solution.py:232
  106.8 0.8 reshape.48.summed_ref
  107.6 3.2 %shard_map.121 = bf16[1152,128]{1,0:T(8,128)(2,1)} custom-call(bf16[1152,128]{1,0:T(8,128)(2,1)} %get-tuple-element.12.first_ref, bf16[1152,128]{1,0:T(8,128)(2,1)} %get-tuple-element.13.normed_ref, bf16[128,1152]{1,0:T(8,128)(2,1)} %reshape.48.summed_ref, bf16[128,128]{1,0:T(8,128)(2,1)} %gate_ref.1, bf16[128,128]{1,0:T(8,128)(2,1)} %out_w_ref.1, ...), custom_call_target="tpu_custom_call" | custom-call | tf_op jit(solution)/shard_map/pallas_call | solution.py:329
  (3 shorter events, 0.1 us)
Async XLA Ops:
  0.0 0.7 copy-start.1
  0.7 0.7 copy-start.2
  9.8 3.7 %collective-permute-start = (bf16[32,896]{1,0:T(8,128)(2,1)S(1)}, bf16[32,896]{1,0:T(8,128)(2,1)S(1)}, u32[]{:S(2)}, u32[]{:S(2)}) collective-permute-start(bf16[32,896]{1,0:T(8,128)(2,1)S(1)} %get-tuple-element.15), channel_id=1, source_target_pairs={{0,0},{1,8},{2,16},{3,24},{4,4},{5,12},{6,20},{7,28},{8,1},{9,9},{... | collective-permute-start | bytes 172040 | tf_op jit(solution)/shard_map/ppermute | solution.py:293
  10.4 5.2 %collective-permute-start.1 = (bf16[32,896]{1,0:T(8,128)(2,1)S(1)}, bf16[32,896]{1,0:T(8,128)(2,1)S(1)}, u32[]{:S(2)}, u32[]{:S(2)}) collective-permute-start(bf16[32,896]{1,0:T(8,128)(2,1)S(1)} %get-tuple-element.16), channel_id=1, source_target_pairs={{0,4},{1,12},{2,20},{3,28},{4,0},{5,8},{6,16},{7,24},{8,5},{9,13},... | collective-permute-start | bytes 172040 | tf_op jit(solution)/shard_map/ppermute | solution.py:293
  34.7 25.4 %all-to-all-start.1 = ((bf16[8,32,1664]{2,1,0:T(8,128)(2,1)}), bf16[8,32,1664]{2,1,0:T(8,128)(2,1)S(1)}, u32[]{:S(2)}, u32[]{:S(2)}) async-start(bf16[8,32,1664]{2,1,0:T(8,128)(2,1)} %get-tuple-element.11), calls=%async_computation.1 | async-start | bytes 1703936 | tf_op jit(solution)/shard_map/all_to_all | solution.py:298
  38.6 0.7 copy-start.3
  60.2 0.9 copy-start

commit v2 on v1

--- a/solution.py
+++ b/solution.py
@@ -7,6 +7,7 @@
 from jax.experimental.pallas import tpu as pltpu
 from jax.sharding import PartitionSpec as P
 
+
 epsilon = 1e-05
 LANES = 128
 BF16 = jnp.bfloat16
@@ -30,94 +31,75 @@
     return centered * lax.rsqrt(variance + epsilon)
 
 
-def params(cost=None):
-    return dict(
-        compiler_params=pltpu.CompilerParams(vmem_limit_bytes=56 * 1024 * 1024),
-        cost_estimate=cost,
-    )
+def params(mebibytes):
+    return dict(compiler_params=pltpu.CompilerParams(vmem_limit_bytes=mebibytes * 1024 * 1024))
 
 
 VMEM = pl.BlockSpec(memory_space=pltpu.VMEM)
 SMEM = pl.BlockSpec(memory_space=pltpu.SMEM)
 
 
-def side_kernel(
-    sequences, cols, half, copies, narrow,
-    index_ref, align_ref, mask_ref, left_w_ref, right_w_ref,
-    right_ref, left_ref, left_projected, right_projected,
-):
+def side_kernel(sequences, cols, parts, copies, narrow, index_ref, align_ref, mask_ref, weights_ref, *refs):
+    *out_refs, projected = refs
     members = LANES // narrow
     rows = sequences * cols
     chunk = rows // 12 if rows % (12 * 16) == 0 else rows
-    left_w = jnp.concatenate([left_w_ref[...]] * members, axis=1)
-    right_w = jnp.concatenate([right_w_ref[...]] * members, axis=1)
+    weights = jnp.concatenate([weights_ref[...]] * members, axis=0)
 
     def project(step, carry):
         start = pl.multiple_of(step * chunk, chunk)
         normed = normalize(align_ref[pl.ds(start, chunk), :].astype(F32)).astype(BF16)
-        left_projected[pl.ds(start, chunk), :] = matmul(normed, left_w)
-        right_projected[pl.ds(start, chunk), :] = matmul(normed, right_w)
+        projected[pl.ds(start, chunk), :] = matmul(normed, weights, NT)
         return carry
 
     lax.fori_loop(0, rows // chunk, project, 0)
     mask = mask_ref[...].astype(BF16)
     lane = iota((sequences, LANES), 1)
-
-    def group_of(projected, first, groups, group):
-        value = None
-        for member in range(members):
-            j = first + member * groups + group
-            part = projected[pl.ds(j, sequences, stride=cols), :]
-            value = part if value is None else jnp.where(lane >= member * narrow, part, value)
-        return value
-
-    def spread(first, groups):
-        width = groups * LANES
+    count = cols // parts
+    groups = count // members
+    width = groups * LANES
+    for h in range(parts):
+        first = h * count
         at = iota((cols, width), 1)
         residue = first + (at % LANES) // narrow * groups + at // LANES
-        return matmul(mask, (iota((cols, width), 0) == residue).astype(BF16))
-
-    def mask_lanes(first, count):
-        pick = iota((cols, LANES), 0) - first == iota((cols, LANES), 1)
-        pick = pick & (iota((cols, LANES), 1) < count)
-        return matmul(mask, pick.astype(BF16)).astype(BF16)
-
-    groups = cols // members
-    masks = spread(0, groups)
-    for group in range(groups):
-        at = slice(group * LANES, (group + 1) * LANES)
-        value = (group_of(right_projected, 0, groups, group) * masks[:, at]).astype(BF16)
-        for copy in range(copies):
-            right_ref[copy, :, at] = value
-    tail = mask_lanes(0, cols)
-    for copy in range(copies):
-        right_ref[copy, :, groups * LANES :] = tail
-    halves = cols // half
-    groups = half // members
-    turn = index_ref[0]
-    for h in range(halves):
-        place = lax.rem(h - turn + halves, halves)
-        masks = spread(h * half, groups)
+        masks = matmul(mask, (iota((cols, width), 0) == residue).astype(BF16))
+        values = []
         for group in range(groups):
-            at = slice(group * LANES, (group + 1) * LANES)
-            value = group_of(left_projected, h * half, groups, group) * masks[:, at]
-            left_ref[place, :, at] = value.astype(BF16)
-        left_ref[place, :, groups * LANES :] = mask_lanes(h * half, half)
+            value = None
+            for member in range(members):
+                part = projected[pl.ds(first + member * groups + group, sequences, stride=cols), :]
+                value = part if value is None else jnp.where(lane >= member * narrow, part, value)
+            values.append((value * masks[:, group * LANES : (group + 1) * LANES]).astype(BF16))
+        at = iota((cols, LANES), 1)
+        pick = (iota((cols, LANES), 0) - first == at) & (at < count)
+        values.append(matmul(mask, pick.astype(BF16)).astype(BF16))
+        for p in range(parts):
+
+            @pl.when(lax.rem(index_ref[0] + p, parts) == h)
+            def _():
+                for group, value in enumerate(values):
+                    lanes = slice(group * LANES, (group + 1) * LANES)
+                    for copy in range(copies):
+                        out_refs[p][copy, :, lanes] = value
 
 
 def outer_kernel(
-    rows, cols, narrow, width, turns,
-    index_ref, left_ref, right_ref, pair_ref, proj_ref, tri_ref, pair_mask_ref,
-    first_ref, normed_ref, tri_out_ref, left_t, stacked, spread_w, moved,
+    rows, cols, narrow, width, turns, sources,
+    index_ref, *refs,
 ):
+    left_refs, refs = refs[:sources], refs[sources:]
+    right_ref, pair_ref, proj_ref, tri_ref, pair_mask_ref, first_ref, normed_ref, tri_out_ref = refs[:8]
+    gathered, left_t, stacked, spread_w, moved = refs[8:]
     members = LANES // narrow
     left_groups, groups = rows // members, cols // members
     left_width, right_width = rows * narrow, cols * narrow
-    sources = left_ref.shape[0]
-    h = index_ref[0]
-    left = jnp.concatenate(
-        [left_ref[c, lax.rem(h - t + turns, turns)] for c in range(sources) for t in range(turns)], axis=0
-    )
+    h, column = index_ref[0], index_ref[1]
+    block = left_refs[0].shape[1]
+    for k, left_ref in enumerate(left_refs):
+        for t in range(turns):
+            start = (source(column, k, sources) * turns + t) * block
+            gathered[pl.ds(pl.multiple_of(start, block), block), :] = left_ref[lax.rem(h - t + turns, turns)]
+    left = gathered[...]
     right_mask = right_ref[:, right_width:]
     left_mask = left[:, left_width:]
     left = left[:, :left_width]
@@ -215,6 +197,14 @@
     lax.fori_loop(0, row_count, close_row, 0)
 
 
+def partner(index, k, count):
+    return index ^ k if count & (count - 1) == 0 else (index + k) % count
+
+
+def source(index, k, count):
+    return index ^ k if count & (count - 1) == 0 else lax.rem(index - k + count, count)
+
+
 def triangle_by_channel(row_count, col_count, rows, cols, gated):
     devices, pair, places = gated.shape
     own = pair // 2
@@ -227,10 +217,10 @@
         in_specs=[VMEM],
         out_specs=VMEM,
         scratch_shapes=[pltpu.VMEM((planes, residues * 2 * own, LANES), F32)] * 2,
-        **params(),
+        **params(24),
     )(gated)
     summed = lax.all_to_all(summed, ("row", "col"), split_axis=0, concat_axis=0, tiled=True)
-    return summed.reshape(devices * own, places)
+    return summed
 
 
 def triangle_by_residue(row_count, col_count, rows, cols, gated):
@@ -240,11 +230,14 @@
     right = lax.all_to_all(right, "col", split_axis=0, concat_axis=1, tiled=True)
     left = lax.all_gather(both[0], "col", axis=1, tiled=True)
     summed = jnp.einsum("ikc,jkc->cij", left, right, preferred_element_type=F32)
-    return summed.reshape(pair // 2, places).astype(BF16)
-
-
-def tail_kernel(first_ref, normed_ref, summed_ref, gate_ref, out_w_ref, in_ref, back_ref, out_ref):
-    normed_sum = normalize(summed_ref[...].astype(F32), 0).astype(BF16)
+    return summed.reshape(1, pair // 2, places).astype(BF16)
+
+
+def tail_kernel(first_ref, normed_ref, summed_ref, gate_ref, out_w_ref, in_ref, back_ref, out_ref, summed):
+    own = summed_ref.shape[1]
+    for d in range(summed_ref.shape[0]):
+        summed[d * own : (d + 1) * own, :] = summed_ref[d].astype(F32)
+    normed_sum = normalize(summed[...], 0).astype(BF16)
     gate = jax.nn.sigmoid(matmul(gate_ref[...].T, normed_ref[...], NT))
     update = gate * matmul(out_w_ref[...].T, normed_sum)
     second = (first_ref[...].astype(F32).T + update).astype(BF16).astype(F32)
@@ -266,23 +259,28 @@
     turns = cols // rows
     places = rows * cols
     r, c = lax.axis_index("row"), lax.axis_index("col")
-    turn = (r % turns).astype(jnp.int32).reshape(1)
+    place = jnp.stack([r % turns, c]).astype(jnp.int32)
 
     members = LANES // narrow
     right_lanes = cols * narrow + LANES
     left_lanes = rows * narrow + LANES
-    right, left = pl.pallas_call(
-        functools.partial(side_kernel, sequences, cols, rows, row_count, narrow),
-        out_shape=(
-            jax.ShapeDtypeStruct((row_count, sequences, right_lanes), BF16),
-            jax.ShapeDtypeStruct((turns, sequences, left_lanes), BF16),
-        ),
-        in_specs=[SMEM] + [VMEM] * 4,
-        out_specs=(VMEM, VMEM),
-        scratch_shapes=[pltpu.VMEM((sequences * cols, LANES), F32)] * 2,
-        **params(),
-    )(turn, alignment.reshape(sequences * cols, channels), alignment_mask, outer_product_left, outer_product_right)
-
+
+    def side(weights, parts, copies):
+        shape = (copies, sequences, cols // parts * narrow + LANES)
+        return pl.pallas_call(
+            functools.partial(side_kernel, sequences, cols, parts, copies, narrow),
+            out_shape=(jax.ShapeDtypeStruct(shape, BF16),) * parts,
+            in_specs=[SMEM] + [VMEM] * 3,
+            out_specs=(VMEM,) * parts,
+            scratch_shapes=[pltpu.VMEM((sequences * cols, LANES), F32)],
+            **params(12),
+        )(place, alignment.reshape(sequences * cols, channels), alignment_mask, weights.T)
+
+    left = side(outer_product_left, turns, 1)
+    (right,) = side(outer_product_right, 1, row_count)
+
+    right = lax.all_to_all(right, "row", split_axis=0, concat_axis=0, tiled=True)
+    right = right.reshape(row_count * sequences, right_lanes)
     sent = []
     for p in range(turns):
         route = []
@@ -290,13 +288,11 @@
             for source_col in range(col_count):
                 to_row = turns * source_col + (source_row + p) % turns
                 route.append((source_row * col_count + source_col, to_row * col_count + source_row // turns))
-        sent.append(lax.ppermute(left[p], ("row", "col"), route))
+        sent.append(lax.ppermute(left[p][0], ("row", "col"), route))
     left = jnp.stack(sent)
-    left = lax.all_to_all(
-        jnp.broadcast_to(left[None], (col_count,) + left.shape), "col", split_axis=0, concat_axis=0, tiled=True
-    )
-    right = lax.all_to_all(right, "row", split_axis=0, concat_axis=0, tiled=True)
-    right = right.reshape(row_count * sequences, right_lanes)
+    lefts = [left]
+    for k in range(1, col_count):
+        lefts.append(lax.ppermute(left, "col", [(col, partner(col, k, col_count)) for col in range(col_count)]))
 
     residue_float = residue_mask.astype(F32)
     row_mask = lax.dynamic_slice_in_dim(residue_float, r * rows, rows)
@@ -307,22 +303,23 @@
     owners = devices if by_channel else 1
     own = inner // owners
     first, normed_pair, gated = pl.pallas_call(
-        functools.partial(outer_kernel, rows, cols, narrow, width, turns),
+        functools.partial(outer_kernel, rows, cols, narrow, width, turns, col_count),
         out_shape=(
             jax.ShapeDtypeStruct((places, width), BF16),
             jax.ShapeDtypeStruct((places, width), BF16),
             jax.ShapeDtypeStruct((owners, 2 * own, places), BF16),
         ),
-        in_specs=[SMEM] + [VMEM] * 6,
+        in_specs=[SMEM] + [VMEM] * (5 + col_count),
         out_specs=(VMEM,) * 3,
         scratch_shapes=[
+            pltpu.VMEM((row_count * sequences, left_lanes), BF16),
             pltpu.VMEM((rows * narrow, row_count * sequences), BF16),
             pltpu.VMEM((cols // members * rows, narrow * LANES), BF16),
             pltpu.VMEM((narrow * LANES, members * width), BF16),
             pltpu.VMEM((places, width), F32),
         ],
-        **params(),
-    )(turn, left, right, pair_features.reshape(places, width), outer_proj, triangle_proj, pair_mask)
+        **params(16),
+    )(place, *lefts, right, pair_features.reshape(places, width), outer_proj, triangle_proj, pair_mask)
 
     triangle = triangle_by_channel if by_channel else triangle_by_residue
     summed = triangle(row_count, col_count, rows, cols, gated)
@@ -331,7 +328,8 @@
         out_shape=jax.ShapeDtypeStruct((places, width), BF16),
         in_specs=[VMEM] * 7,
         out_specs=VMEM,
-        **params(),
+        scratch_shapes=[pltpu.VMEM((inner, places), F32)],
+        **params(16),
     )(first, normed_pair, summed, triangle_gate, triangle_out, transition_in, transition_out)
     return out.reshape(rows, cols, width)
 
@@ -343,5 +341,8 @@
         P(),
         P("row", "col", None),
     ) + (P(),) * 8
-    body = functools.partial(shards, mesh.shape["row"], mesh.shape["col"])
+
+    def body(*args):
+        return shards(mesh.shape["row"], mesh.shape["col"], *args)
+
     return jax.shard_map(body, mesh=mesh, in_specs=placed, out_specs=P("row", "col", None), check_vma=False)

time: 111 us -> 92.1 us (0.83)
  starting transfers between devices: 7.53 us -> 29.2 us
  blocking collectives: 53.7 us -> 33.4 us
  waiting for transfers between devices: 22.2 us -> 7.1 us
  local copies, waits for them, and re-layouts: 6.28 us -> 2.08 us
  Pallas kernels: 21 us -> 19.7 us
    all_to_all x1, waiting for transfers between devices: 20 us -> 0.01 us  [shards(): lax.all_to_all(right, 'row', split_axis=0, concat_axis=0, tiled=True)]
    all_to_all x1 -> x0, blocking collectives: 19.1 us -> none  [shards(): lax.all_to_all(jnp.broadcast_to(left[None], (col_count,) + left.shape), '...]
    ppermute x2 -> x5, starting transfers between devices: 3.69 us -> 21.8 us  [the longest x3 19 us: shards(): lax.ppermute(left, 'col', [(col, partner(col, k, col_count)) for col in r...]
    ppermute x2 -> x5, waiting for transfers between devices: 2.16 us -> 7.1 us  [the longest x3 4.95 us: shards(): lax.ppermute(left, 'col', [(col, partner(col, k, col_count)) for col in r...]
    all_to_all x1, starting transfers between devices: 3.83 us -> 7.41 us  [shards(): lax.all_to_all(right, 'row', split_axis=0, concat_axis=0, tiled=True)]
    pallas_call x1 -> x2, Pallas kernels: 6.74 us -> 10.1 us  [side(): pl.pallas_call(functools.partial(side_kernel, sequences, cols, parts, cop...]
    unnamed x10 -> x26, local copies, waits for them, and re-layouts: 3.78 us -> 1.85 us
    pallas_call x1, Pallas kernels: 4.19 us -> 2.41 us  [triangle_by_channel(): pl.pallas_call(functools.partial(triangle_kernel, row_count, col_count, r...]
  transfers between devices with their start and end apart: 3 -> 6, of which waited for: 2 -> 2; matrix products, arithmetic and copies ran while one was open for 1% -> 0% of each run, Pallas kernels for 0% -> 5%
where the time goes in v2:
time: 92.1 us; the launch traced here: 91.8 us
  blocking collectives  33.4 us (36%)
  starting transfers between devices  29.2 us (32%)
  Pallas kernels  19.7 us (21%)
  waiting for transfers between devices  7.1 us (8%)
  local copies, waits for them, and re-layouts  2.08 us (2%)
    ppermute x3, starting transfers between devices, shards(): lax.ppermute(left, 'col', [(col, partner(col, k, col_count)) for col in r...  19 us
    all_to_all x1, blocking collectives, triangle_by_channel(): lax.all_to_all(gated, ('row', 'col'), split_axis=0, concat_axis=0, tiled=...  19 us
    all_to_all x1, blocking collectives, triangle_by_channel(): lax.all_to_all(summed, ('row', 'col'), split_axis=0, concat_axis=0, tiled...  14.4 us
    pallas_call x2, Pallas kernels, side(): pl.pallas_call(functools.partial(side_kernel, sequences, cols, parts, cop...  10.1 us
    all_to_all x1, starting transfers between devices, shards(): lax.all_to_all(right, 'row', split_axis=0, concat_axis=0, tiled=True)  7.41 us
    pallas_call x1, Pallas kernels, shards(): pl.pallas_call(functools.partial(outer_kernel, rows, cols, narrow, width,...  5.21 us
    ppermute x3, waiting for transfers between devices, shards(): lax.ppermute(left, 'col', [(col, partner(col, k, col_count)) for col in r...  4.95 us
    ppermute x2, starting transfers between devices, shards(): sent.append(lax.ppermute(left[p][0], ('row', 'col'), route))  2.73 us
  transfers between devices with their start and end apart: 6, of which 2 were waited for; matrix products, arithmetic and copies ran while one was open for 0% of the time, Pallas kernels for 5%

profile of v2, /device:TPU:0, one launch (start us, length us, event | category | flops | bytes accessed | tf_op | source)
XLA Modules:
  0.0 91.8 jit_solution(16178196573961219242)
XLA Ops:
  0.0 0.0 copy-start.7
  0.0 0.0 copy-start.10
  0.0 0.1 pad_add_fusion.index_ref
  0.1 0.6 copy-done.7
  0.7 0.0 copy-done.10
  0.7 0.0 copy-start
  0.7 1.1 %copy-done = bf16[32,48,256]{2,1,0:T(8,128)(2,1)S(1)} copy-done((bf16[32,48,256]{2,1,0:T(8,128)(2,1)S(1)}, bf16[32,48,256]{2,1,0:T(8,128)(2,1)}, u32[]{:S(2)}) %copy-start) | copy-done | bytes 786456
  1.9 5.5 %shard_map.119 = bf16[8,32,1664]{2,1,0:T(8,128)(2,1)} custom-call(s32[2]{0:T(128)S(1)} %pad_add_fusion.index_ref, bf16[1536,256]{1,0:T(8,128)(2,1)S(1)} %bitcast.13, s32[32,48]{1,0:T(8,128)S(1)} %copy-done.7, bf16[32,256]{1,0:T(8,128)(2,1)S(1)} %bitcast.16), custom_call_target="tpu_custom_call" | custom-call | tf_op jit(solution)/shard_map/pallas_call | solution.py:270
  7.4 0.0 copy-start.1
  7.4 0.0 copy-start.11
  7.4 7.4 %all-to-all-start = ((bf16[8,32,1664]{2,1,0:T(8,128)(2,1)}), bf16[8,32,1664]{2,1,0:T(8,128)(2,1)S(1)}, u32[]{:S(2)}, u32[]{:S(2)}) async-start(bf16[8,32,1664]{2,1,0:T(8,128)(2,1)} %shard_map.119), calls=%async_computation | async-start | bytes 1703936 | tf_op jit(solution)/shard_map/all_to_all | solution.py:282
  14.8 0.0 copy-done.1
  14.8 0.0 copy-done.11
  14.8 0.0 copy-start.12
  14.8 0.0 copy-start.3
  14.9 0.0 copy-start.4
  14.9 4.6 %shard_map.118 = (bf16[1,32,896]{2,1,0:T(8,128)(2,1)S(1)}, bf16[1,32,896]{2,1,0:T(8,128)(2,1)S(1)}) custom-call(s32[2]{0:T(128)S(1)} %pad_add_fusion.index_ref, bf16[1536,256]{1,0:T(8,128)(2,1)S(1)} %bitcast.14, s32[32,48]{1,0:T(8,128)S(1)} %copy-done.7, bf16[32,256]{1,0:T(8,128)(2,1)S(1)} %bitcast.17), custom_call_target="tpu_custom_call" | custom-call | tf_op jit(solution)/shard_map/pallas_call | solution.py:270
  19.5 0.0 copy-start.2
  19.5 2.1 %collective-permute-start.1 = (bf16[32,896]{1,0:T(8,128)(2,1)S(1)}, bf16[32,896]{1,0:T(8,128)(2,1)S(1)}, u32[]{:S(2)}, u32[]{:S(2)}) collective-permute-start(bf16[32,896]{1,0:T(8,128)(2,1)S(1)} %bitcast.19), channel_id=1, source_target_pairs={{0,4},{1,12},{2,20},{3,28},{4,0},{5,8},{6,16},{7,24},{8,5},{9,13},... | collective-permute-start | bytes 172040 | tf_op jit(solution)/shard_map/ppermute | solution.py:291
  21.6 0.7 collective-permute-start
  22.2 0.0 copy-done.12
  22.3 0.1 dynamic_slice.7
  22.3 0.1 dynamic_slice.6
  22.4 2.1 %collective-permute-done.1 = bf16[32,896]{1,0:T(8,128)(2,1)S(1)} collective-permute-done((bf16[32,896]{1,0:T(8,128)(2,1)S(1)}, bf16[32,896]{1,0:T(8,128)(2,1)S(1)}, u32[]{:S(2)}, u32[]{:S(2)}) %collective-permute-start.1) | collective-permute-done | bytes 57376 | tf_op jit(solution)/shard_map/ppermute | solution.py:291
  24.6 0.0 collective-permute-done
  24.6 12.2 %collective-permute-start.4 = (bf16[2,32,896]{2,1,0:T(8,128)(2,1)S(1)}, bf16[2,32,896]{2,1,0:T(8,128)(2,1)S(1)}, u32[]{:S(2)}, u32[]{:S(2)}) collective-permute-start(bf16[2,32,896]{2,1,0:T(8,128)(2,1)S(1)} %pad_maximum_fusion.refs_0_), channel_id=1, source_target_pairs={{0,3},{1,2},{2,1},{3,0},{4,7},{5,6},{6,5},{7,4},{8,11},{9,10},{10,... | collective-permute-start | bytes 344072 | tf_op jit(solution)/shard_map/ppermute | solution.py:295
  36.8 6.8 %collective-permute-start.3 = (bf16[2,32,896]{2,1,0:T(8,128)(2,1)S(1)}, bf16[2,32,896]{2,1,0:T(8,128)(2,1)S(1)}, u32[]{:S(2)}, u32[]{:S(2)}) collective-permute-start(bf16[2,32,896]{2,1,0:T(8,128)(2,1)S(1)} %pad_maximum_fusion.refs_0_), channel_id=1, source_target_pairs={{0,2},{1,3},{2,0},{3,1},{4,6},{5,7},{6,4},{7,5},{8,10},{9,11},{10,... | collective-permute-start | bytes 344072 | tf_op jit(solution)/shard_map/ppermute | solution.py:295
  43.6 0.0 collective-permute-start.2
  43.6 0.1 broadcast_multiply_fusion
  43.7 0.1 mul.34.refs_8_
  43.8 0.0 collective-permute-done.4.refs_3_
  43.8 4.9 %collective-permute-done.3.refs_2_ = bf16[2,32,896]{2,1,0:T(8,128)(2,1)S(1)} collective-permute-done((bf16[2,32,896]{2,1,0:T(8,128)(2,1)S(1)}, bf16[2,32,896]{2,1,0:T(8,128)(2,1)S(1)}, u32[]{:S(2)}, u32[]{:S(2)}) %collective-permute-start.3) | collective-permute-done | bytes 114720 | tf_op jit(solution)/shard_map/ppermute | solution.py:295
  48.7 0.0 collective-permute-done.2.refs_1_
  48.7 0.0 all-to-all-done
  48.7 0.0 copy-done.3
  48.7 0.0 copy-done.4
  48.8 0.0 copy-done.2
  48.8 5.2 %shard_map.120 = (bf16[1152,128]{1,0:T(8,128)(2,1)S(1)}, bf16[1152,128]{1,0:T(8,128)(2,1)S(1)}, bf16[32,8,1152]{2,1,0:T(8,128)(2,1)S(1)}) custom-call(s32[2]{0:T(128)S(1)} %pad_add_fusion.index_ref, bf16[2,32,896]{2,1,0:T(8,128)(2,1)S(1)} %pad_maximum_fusion.refs_0_, bf16[2,32,896]{2,1,0:T(8,128)(2,1)S(1)} %collective-permute-done.2.refs_1_, ...), custom_call_target="tpu_custom_call" | custom-call | tf_op jit(solution)/shard_map/pallas_call | solution.py:305
  54.0 19.0 %all_to_all.15.given_ref = bf16[32,8,1152]{2,1,0:T(8,128)(2,1)S(1)} all-to-all(bf16[32,8,1152]{2,1,0:T(8,128)(2,1)S(1)} %get-tuple-element.14), channel_id=1, replica_groups=mesh['row'=8,'col'=4] {'row','col'}, dimensions={0} | all-to-all | bytes 1179648 | tf_op jit(solution)/shard_map/all_to_all | solution.py:211
  72.9 2.4 %shard_map.121 = bf16[32,4,1152]{2,1,0:T(4,128)(2,1)S(1)} custom-call(bf16[32,8,1152]{2,1,0:T(8,128)(2,1)S(1)} %all_to_all.15.given_ref), custom_call_target="tpu_custom_call" | custom-call | tf_op jit(solution)/shard_map/pallas_call | solution.py:214
  75.4 0.0 copy-start.5
  75.4 0.0 copy-start.6
  75.4 0.0 copy-start.8
  75.4 0.0 copy-start.9
  75.4 14.4 %all_to_all.16.summed_ref = bf16[32,4,1152]{2,1,0:T(4,128)(2,1)S(1)} all-to-all(bf16[32,4,1152]{2,1,0:T(4,128)(2,1)S(1)} %shard_map.121), channel_id=1, replica_groups=mesh['row'=8,'col'=4] {'row','col'}, dimensions={0} | all-to-all | bytes 589824 | tf_op jit(solution)/shard_map/all_to_all | solution.py:222
  89.8 0.0 copy-done.5
  89.8 0.0 copy-done.6
  89.8 0.0 copy-done.8
  89.8 0.0 copy-done.9
  89.8 1.9 %shard_map.122 = bf16[1152,128]{1,0:T(8,128)(2,1)} custom-call(bf16[1152,128]{1,0:T(8,128)(2,1)S(1)} %get-tuple-element.12.first_ref, bf16[1152,128]{1,0:T(8,128)(2,1)S(1)} %get-tuple-element.13.normed_ref, bf16[32,4,1152]{2,1,0:T(4,128)(2,1)S(1)} %all_to_all.16.summed_ref, bf16[128,128]{1,0:T(8,128)(2,1)S(1)} %copy-done.8, bf16[128,128]{1,0:T(8,128)(2,1)S(1)} %copy-done.9, ...), custom_call_target="tpu_custom_call" | custom-call | tf_op jit(solution)/shard_map/pallas_call | solution.py:326
  (2 shorter events, 0.0 us)
Async XLA Ops:
  0.0 0.7 copy-start.7
  0.0 0.7 copy-start.10
  0.7 1.1 %copy-start = (bf16[32,48,256]{2,1,0:T(8,128)(2,1)S(1)}, bf16[32,48,256]{2,1,0:T(8,128)(2,1)}, u32[]{:S(2)}) copy-start(bf16[32,48,256]{2,1,0:T(8,128)(2,1)} %param.12) | copy-start | bytes 2359300
  7.4 7.4 %copy-start.1 = (bf16[32,48,256]{2,1,0:T(8,128)(2,1)S(1)}, bf16[32,48,256]{2,1,0:T(8,128)(2,1)}, u32[]{:S(2)}) copy-start(bf16[32,48,256]{2,1,0:T(8,128)(2,1)} %param.12) | copy-start | bytes 2359300
  7.4 7.4 %copy-start.11 = (bf16[256,32]{0,1:T(8,128)(2,1)S(1)}, bf16[256,32]{0,1:T(8,128)(2,1)}, u32[]{:S(2)}) copy-start(bf16[256,32]{0,1:T(8,128)(2,1)} %param.16) | copy-start | bytes 49156
  7.4 41.3 %all-to-all-start = ((bf16[8,32,1664]{2,1,0:T(8,128)(2,1)}), bf16[8,32,1664]{2,1,0:T(8,128)(2,1)S(1)}, u32[]{:S(2)}, u32[]{:S(2)}) async-start(bf16[8,32,1664]{2,1,0:T(8,128)(2,1)} %shard_map.119), calls=%async_computation | async-start | bytes 1703936 | tf_op jit(solution)/shard_map/all_to_all | solution.py:282
  14.8 7.4 %copy-start.12 = (s32[192]{0:T(256)S(1)}, s32[192]{0:T(256)}, u32[]{:S(2)}) copy-start(s32[192]{0:T(256)} %param.14) | copy-start | bytes 2308
  14.8 33.9 %copy-start.3 = (bf16[1024,128]{1,0:T(8,128)(2,1)S(1)}, bf16[1024,128]{1,0:T(8,128)(2,1)}, u32[]{:S(2)}) copy-start(bf16[1024,128]{1,0:T(8,128)(2,1)} %refs_6_.1) | copy-start | bytes 786436
  14.9 33.9 %copy-start.4 = (bf16[128,512]{1,0:T(8,128)(2,1)S(1)}, bf16[128,512]{1,0:T(8,128)(2,1)}, u32[]{:S(2)}) copy-start(bf16[128,512]{1,0:T(8,128)(2,1)} %refs_7_.1) | copy-start | bytes 393220
  19.5 29.3 %copy-start.2 = (bf16[24,48,128]{2,1,0:T(8,128)(2,1)S(1)}, bf16[24,48,128]{2,1,0:T(8,128)(2,1)}, u32[]{:S(2)}) copy-start(bf16[24,48,128]{2,1,0:T(8,128)(2,1)} %param.15) | copy-start | bytes 884740
  19.5 5.1 %collective-permute-start.1 = (bf16[32,896]{1,0:T(8,128)(2,1)S(1)}, bf16[32,896]{1,0:T(8,128)(2,1)S(1)}, u32[]{:S(2)}, u32[]{:S(2)}) collective-permute-start(bf16[32,896]{1,0:T(8,128)(2,1)S(1)} %bitcast.19), channel_id=1, source_target_pairs={{0,4},{1,12},{2,20},{3,28},{4,0},{5,8},{6,16},{7,24},{8,5},{9,13},... | collective-permute-start | bytes 172040 | tf_op jit(solution)/shard_map/ppermute | solution.py:291
  21.6 3.0 %collective-permute-start = (bf16[32,896]{1,0:T(8,128)(2,1)S(1)}, bf16[32,896]{1,0:T(8,128)(2,1)S(1)}, u32[]{:S(2)}, u32[]{:S(2)}) collective-permute-start(bf16[32,896]{1,0:T(8,128)(2,1)S(1)} %bitcast.18), channel_id=1, source_target_pairs={{0,0},{1,8},{2,16},{3,24},{4,4},{5,12},{6,20},{7,28},{8,1},{9,9},{... | collective-permute-start | bytes 172040 | tf_op jit(solution)/shard_map/ppermute | solution.py:291
  24.6 19.2 %collective-permute-start.4 = (bf16[2,32,896]{2,1,0:T(8,128)(2,1)S(1)}, bf16[2,32,896]{2,1,0:T(8,128)(2,1)S(1)}, u32[]{:S(2)}, u32[]{:S(2)}) collective-permute-start(bf16[2,32,896]{2,1,0:T(8,128)(2,1)S(1)} %pad_maximum_fusion.refs_0_), channel_id=1, source_target_pairs={{0,3},{1,2},{2,1},{3,0},{4,7},{5,6},{6,5},{7,4},{8,11},{9,10},{10,... | collective-permute-start | bytes 344072 | tf_op jit(solution)/shard_map/ppermute | solution.py:295
  36.8 11.9 %collective-permute-start.3 = (bf16[2,32,896]{2,1,0:T(8,128)(2,1)S(1)}, bf16[2,32,896]{2,1,0:T(8,128)(2,1)S(1)}, u32[]{:S(2)}, u32[]{:S(2)}) collective-permute-start(bf16[2,32,896]{2,1,0:T(8,128)(2,1)S(1)} %pad_maximum_fusion.refs_0_), channel_id=1, source_target_pairs={{0,2},{1,3},{2,0},{3,1},{4,6},{5,7},{6,4},{7,5},{8,10},{9,11},{10,... | collective-permute-start | bytes 344072 | tf_op jit(solution)/shard_map/ppermute | solution.py:295
  43.6 5.2 %collective-permute-start.2 = (bf16[2,32,896]{2,1,0:T(8,128)(2,1)S(1)}, bf16[2,32,896]{2,1,0:T(8,128)(2,1)S(1)}, u32[]{:S(2)}, u32[]{:S(2)}) collective-permute-start(bf16[2,32,896]{2,1,0:T(8,128)(2,1)S(1)} %pad_maximum_fusion.refs_0_), channel_id=1, source_target_pairs={{0,1},{1,0},{2,3},{3,2},{4,5},{5,4},{6,7},{7,6},{8,9},{9,8},{10,11... | collective-permute-start | bytes 344072 | tf_op jit(solution)/shard_map/ppermute | solution.py:295
  75.4 14.4 %copy-start.5 = (bf16[128,512]{1,0:T(8,128)(2,1)S(1)}, bf16[128,512]{1,0:T(8,128)(2,1)}, u32[]{:S(2)}) copy-start(bf16[128,512]{1,0:T(8,128)(2,1)} %in_ref.1) | copy-start | bytes 393220
  75.4 14.4 %copy-start.6 = (bf16[512,128]{1,0:T(8,128)(2,1)S(1)}, bf16[512,128]{1,0:T(8,128)(2,1)}, u32[]{:S(2)}) copy-start(bf16[512,128]{1,0:T(8,128)(2,1)} %back_ref.1) | copy-start | bytes 393220
  75.4 14.4 %copy-start.8 = (bf16[128,128]{1,0:T(8,128)(2,1)S(1)}, bf16[128,128]{1,0:T(8,128)(2,1)}, u32[]{:S(2)}) copy-start(bf16[128,128]{1,0:T(8,128)(2,1)} %gate_ref.1) | copy-start | bytes 98308
  75.4 14.4 %copy-start.9 = (bf16[128,128]{1,0:T(8,128)(2,1)S(1)}, bf16[128,128]{1,0:T(8,128)(2,1)}, u32[]{:S(2)}) copy-start(bf16[128,128]{1,0:T(8,128)(2,1)} %out_w_ref.1) | copy-start | bytes 98308

commit v3 on v2

v3 whole, which is shorter than its diff:
```python
import functools

import jax
import jax.numpy as jnp
from jax import lax
from jax.experimental import pallas as pl
from jax.experimental.pallas import tpu as pltpu
from jax.sharding import PartitionSpec as P


epsilon = 1e-05
LANES = 128
BF16 = jnp.bfloat16
F32 = jnp.float32
NT = (((1,), (1,)), ((), ()))
TN = (((0,), (0,)), ((), ()))


def matmul(a, b, dims=(((1,), (0,)), ((), ()))):
    return lax.dot_general(a, b, dims, preferred_element_type=F32)


def iota(shape, axis):
    return lax.broadcasted_iota(jnp.int32, shape, axis)


def normalize(values, axis=-1):
    mean_value = jnp.mean(values, axis=axis, keepdims=True)
    centered = values - mean_value
    variance = jnp.mean(centered * centered, axis=axis, keepdims=True)
    return centered * lax.rsqrt(variance + epsilon)


def in_hbm(values):
    return [pltpu.with_memory_space_constraint(value, pltpu.HBM) for value in values]


def call(kernel, mebibytes, outs, scratch, in_specs=None, out_specs=None):
    return pl.pallas_call(
        kernel,
        out_shape=tuple(jax.ShapeDtypeStruct(*out) for out in outs),
        out_specs=out_specs or (VMEM,) * len(outs),
        scratch_shapes=scratch,
        compiler_params=pltpu.CompilerParams(vmem_limit_bytes=mebibytes * 1024 * 1024),
        **({} if in_specs is None else {"in_specs": in_specs}),
    )


VMEM = pl.BlockSpec(memory_space=pltpu.VMEM)


def pack_side(projected, mask, narrow, first, count, put):
    sequences, cols = mask.shape
    members = LANES // narrow
    lane = iota((sequences, LANES), 1)
    groups = count // members
    width = groups * LANES
    at = iota((cols, width), 1)
    residue = first + (at % LANES) // narrow * groups + at // LANES
    masks = matmul(mask, (iota((cols, width), 0) == residue).astype(BF16))
    for group in range(groups):
        value = None
        for member in range(members):
            part = projected[pl.ds(first + member * groups + group, sequences, stride=cols), :]
            value = part if value is None else jnp.where(lane >= member * narrow, part, value)
        put(group, (value * masks[:, group * LANES : (group + 1) * LANES]).astype(BF16))
    at = iota((cols, LANES), 1)
    pick = (iota((cols, LANES), 0) - first == at) & (at < count)
    put(groups, matmul(mask, pick.astype(BF16)).astype(BF16))


def side_kernel(
    chunks, narrow, align_hbm, mask_hbm, left_w_hbm, right_w_hbm, right_hbm, left_ref,
    left_rows, right_rows, align, mask_int, left_w, right_w, packed, align_sem, mask_sem, left_sem, right_sem, out_sem,
):
    chunk = align.shape[0] // chunks
    small = [
        pltpu.make_async_copy(left_w_hbm, left_w, left_sem),
        pltpu.make_async_copy(right_w_hbm, right_w, right_sem),
        pltpu.make_async_copy(mask_hbm, mask_int, mask_sem),
    ]
    parts = []
    for n in range(chunks):
        at = pl.ds(n * chunk, chunk)
        parts.append(pltpu.make_async_copy(align_hbm.at[at, :], align.at[at, :], align_sem.at[n]))
    for copy in small[:2] + parts + small[2:]:
        copy.start()
    small[0].wait()
    small[1].wait()
    members = LANES // narrow
    both = jnp.concatenate([left_w[...]] * members + [right_w[...]] * members, axis=0)
    for n in range(chunks):
        parts[n].wait()
        at = slice(n * chunk, (n + 1) * chunk)
        normed = normalize(align[at, :].astype(F32)).astype(BF16)
        value = matmul(normed, both, NT)
        left_rows[at, :] = value[:, :LANES]
        right_rows[at, :] = value[:, LANES:]
    small[2].wait()
    mask = mask_int[...].astype(BF16)
    cols = mask.shape[1]

    def put_right(group, value):
        packed[:, group * LANES : (group + 1) * LANES] = value

    pack_side(right_rows, mask, narrow, 0, cols, put_right)
    copies = [pltpu.make_async_copy(packed, right_hbm.at[n], out_sem.at[n]) for n in range(right_hbm.shape[0])]
    for copy in copies:
        copy.start()
    turns = left_ref.shape[0]
    turn = lax.rem(lax.axis_index("row"), turns)
    for h in range(turns):
        place = lax.rem(h - turn + turns, turns)

        def put_left(group, value):
            left_ref[place, :, group * LANES : (group + 1) * LANES] = value

        pack_side(left_rows, mask, narrow, h * (cols // turns), cols // turns, put_left)
    for copy in copies:
        copy.wait()


def prepare_kernel(rows, narrow, turns, sources, own, tri_ref, *refs):
    left_refs, refs = refs[: turns * sources], refs[turns * sources :]
    tri_rows_ref, left_t_ref, mask_ref, gathered = refs
    block = left_refs[0].shape[0]
    h, column = lax.rem(lax.axis_index("row"), turns), lax.axis_index("col")
    for n, left_ref in enumerate(left_refs):
        d, k = n // sources, n % sources
        start = (source(column, k, sources) * turns + lax.rem(h - d + turns, turns)) * block
        gathered[pl.ds(pl.multiple_of(start, block), block), :] = left_ref[...]
    out = tri_ref.shape[0]
    members = LANES // narrow
    width = rows * narrow
    groups = rows // members
    at = iota((width, width), 0)
    channel, residue = at // rows, at % rows
    place = residue % groups * LANES + residue // groups * narrow + channel
    pick = (iota((width, width), 1) == place).astype(BF16)
    left_t_ref[...] = matmul(pick, gathered[:, :width], NT).astype(BF16)
    mask_ref[...] = gathered[:, width:]
    at = iota((4 * out, 4 * out), 0)
    kind, rest = at // (2 * out), at % (2 * out)
    owner, side, channel = rest // (2 * own), rest // own % 2, rest % own
    column = side * 2 * out + kind * out + owner * own + channel
    pick = (iota((4 * out, 4 * out), 1) == column).astype(BF16)
    tri_rows_ref[...] = matmul(pick, tri_ref[...], NT).astype(BF16)


def outer_kernel(
    rows, cols, narrow, left_t, left_mask_ref, right_ref, tri_ref, pair_mask_ref, pair_ref, proj_ref,
    first_ref, normed_ref, tri_out_ref, stacked, spread, moved,
):
    members = LANES // narrow
    groups = cols // members
    right_width = cols * narrow
    width = pair_ref.shape[1]
    steps = stacked.shape[0]
    step = narrow // steps
    spread[...] = jnp.zeros_like(spread)
    total = None
    for first in range(0, narrow, step):
        block = matmul(left_t[first * rows : (first + step) * rows, :], right_ref[:, :right_width])
        for c in range(step):
            lanes = slice(c * LANES, (c + 1) * LANES)
            for g in range(0, groups, 2):
                two = [
                    block[c * rows : (c + 1) * rows, (g + n) * LANES : (g + n + 1) * LANES] for n in range(2)
                ]
                stacked[first // step, g * rows : (g + 2) * rows, lanes] = jnp.concatenate(two, axis=0).astype(BF16)
        turn = first // step % 2
        for c in range(step):
            part = proj_ref[(first + c) * narrow : (first + c + 1) * narrow, :]
            for m in range(members):
                start = c * LANES + m * narrow
                spread[turn, start : start + narrow, m * width : (m + 1) * width] = part
        term = matmul(stacked[first // step], spread[turn])
        total = term if total is None else total + term
    counts = matmul(left_mask_ref[...], right_ref[:, right_width:], TN)[:rows, :]
    scale = 1.0 / jnp.maximum(counts, 1.0)
    for m in range(members):
        for g in range(groups):
            j = m * groups + g
            part = total[g * rows : (g + 1) * rows, m * width : (m + 1) * width]
            moved[j * rows : (j + 1) * rows, :] = part * scale[:, j : j + 1]
    for i in range(rows):
        at = slice(i * cols, (i + 1) * cols)
        first = pair_ref[at, :].astype(F32) + moved[pl.ds(i, cols, stride=rows), :]
        first = first.astype(BF16)
        first_ref[at, :] = first
        normed_ref[at, :] = normalize(first.astype(F32)).astype(BF16)
    devices, pair, _ = tri_out_ref.shape
    half = devices * pair
    projections = matmul(tri_ref[...], normed_ref[...], NT)
    gated = jax.nn.sigmoid(projections[:half]) * projections[half:] * pair_mask_ref[...]
    gated = gated.astype(BF16)
    for d in range(devices):
        tri_out_ref[d] = gated[d * pair : (d + 1) * pair, :]


def triangle_kernel(row_count, col_count, rows, cols, own, given_ref, out_ref, opened, summed):
    residues = row_count * rows
    pair = 2 * own
    planes = opened.shape[0]
    each = -(-col_count // planes)

    def open_row(r, carry):
        for c in range(col_count):
            value = given_ref[r * col_count + c].astype(F32)
            lanes = slice(c % each * cols, (c % each + 1) * cols)
            for i in range(rows):
                start = pl.multiple_of((r * rows + i) * pair, pair)
                opened[c // each, pl.ds(start, pair), lanes] = value[:, i * cols : (i + 1) * cols]
        return carry

    lax.fori_loop(0, row_count, open_row, 0)
    used = each * cols
    for t in range(own):
        left = [opened.at[p][pl.ds(t, residues, stride=pair), :].astype(BF16) for p in range(planes)]
        right = [opened.at[p][pl.ds(own + t, residues, stride=pair), :].astype(BF16) for p in range(planes)]
        for q in range(planes):
            total = None
            for p in range(planes):
                width = min(each, col_count - p * each) * cols
                some = right[p][q * used : min((q + 1) * used, residues), :width]
                if some.shape[0] < LANES:
                    some = jnp.concatenate([some, jnp.zeros((LANES - some.shape[0], width), BF16)], axis=0)
                term = matmul(left[p][:, :width], some, NT)
                total = term if total is None else total + term
            summed.at[q][pl.ds(t, residues, stride=pair), :] = total

    def close_row(r, carry):
        for c in range(col_count):
            lanes = slice(c % each * cols, (c % each + 1) * cols)
            parts = []
            for i in range(rows):
                start = pl.multiple_of((r * rows + i) * pair, pair)
                parts.append(summed[c // each, pl.ds(start, pair), lanes])
            out_ref[r * col_count + c] = jnp.concatenate(parts, axis=1)[:own].astype(BF16)
        return carry

    lax.fori_loop(0, row_count, close_row, 0)


def partner(index, k, count):
    return index ^ k if count & (count - 1) == 0 else (index + k) % count


def source(index, k, count):
    return index ^ k if count & (count - 1) == 0 else lax.rem(index - k + count, count)


def triangle_by_channel(row_count, col_count, rows, cols, gated):
    devices, pair, places = gated.shape
    own = pair // 2
    gated = lax.all_to_all(gated, ("row", "col"), split_axis=0, concat_axis=0, tiled=True)
    residues = row_count * rows
    planes = -(-col_count // (LANES // cols))
    (summed,) = call(
        functools.partial(triangle_kernel, row_count, col_count, rows, cols, own),
        16,
        [((devices, own, places), BF16)],
        [pltpu.VMEM((planes, residues * pair, LANES), F32)] * 2,
    )(gated)
    summed = lax.all_to_all(summed, ("row", "col"), split_axis=0, concat_axis=0, tiled=True)
    return summed


def triangle_by_residue(row_count, col_count, rows, cols, gated):
    _, pair, places = gated.shape
    both = gated.reshape(2, pair // 2, rows, cols).transpose(0, 2, 3, 1)
    right = lax.all_gather(both[1], "row", axis=0, tiled=True)
    right = lax.all_to_all(right, "col", split_axis=0, concat_axis=1, tiled=True)
    left = lax.all_gather(both[0], "col", axis=1, tiled=True)
    summed = jnp.einsum("ikc,jkc->cij", left, right, preferred_element_type=F32)
    return summed.reshape(1, pair // 2, places).astype(BF16)


def gate_kernel(first_ref, normed_ref, gate_ref, first_t_ref, gated_ref):
    first_t_ref[...] = first_ref[...].astype(F32).T
    gated_ref[...] = jax.nn.sigmoid(matmul(gate_ref[...].T, normed_ref[...], NT))


def tail_kernel(first_ref, gated_ref, summed_ref, out_w_ref, in_ref, back_ref, out_ref, summed):
    own = summed_ref.shape[1]
    for d in range(summed_ref.shape[0]):
        summed[d * own : (d + 1) * own, :] = summed_ref[d].astype(F32)
    normed_sum = normalize(summed[...], 0).astype(BF16)
    update = gated_ref[...] * matmul(out_w_ref[...].T, normed_sum)
    second = (first_ref[...] + update).astype(BF16).astype(F32)
    normed_second = normalize(second, 0).astype(BF16)
    hidden = jnp.maximum(matmul(in_ref[...].T, normed_second), 0.0).astype(BF16)
    result = second + matmul(back_ref[...].T, hidden)
    out_ref[...] = result.T.astype(BF16)


def shards(
    row_count, col_count, alignment, alignment_mask, residue_mask, pair_features, outer_product_left, outer_product_right,
    outer_proj, triangle_proj, triangle_gate, triangle_out, transition_in, transition_out,
):
    rows, cols, width = pair_features.shape
    sequences, _, channels = alignment.shape
    narrow = outer_product_left.shape[1]
    inner = triangle_out.shape[0]
    devices = row_count * col_count
    turns = cols // rows
    places = rows * cols
    r, c = lax.axis_index("row"), lax.axis_index("col")
    by_channel = inner % devices == 0
    owners = devices if by_channel else 1
    own = inner // owners

    members = LANES // narrow
    right_lanes = cols * narrow + LANES
    left_lanes = rows * narrow + LANES
    lines = sequences * cols
    chunks = 4 if lines % 64 == 0 else 1
    pieces = 4 if narrow % 4 == 0 else 1

    hbm = pl.BlockSpec(memory_space=pltpu.HBM)
    right, left = call(
        functools.partial(side_kernel, chunks, narrow),
        16,
        [((row_count, sequences, right_lanes), BF16), ((turns, sequences, left_lanes), BF16)],
        [
            pltpu.VMEM((lines, LANES), F32),
            pltpu.VMEM((lines, LANES), F32),
            pltpu.VMEM((lines, channels), BF16),
            pltpu.VMEM((sequences, cols), jnp.int32),
            pltpu.VMEM((narrow, channels), BF16),
            pltpu.VMEM((narrow, channels), BF16),
            pltpu.VMEM((sequences, right_lanes), BF16),
            pltpu.SemaphoreType.DMA((chunks,)),
            pltpu.SemaphoreType.DMA,
            pltpu.SemaphoreType.DMA,
            pltpu.SemaphoreType.DMA,
            pltpu.SemaphoreType.DMA((row_count,)),
        ],
        [hbm] * 4,
        (hbm, VMEM),
    )(*in_hbm([alignment.reshape(lines, channels), alignment_mask, outer_product_left.T, outer_product_right.T]))
    right = lax.all_to_all(right, "row", split_axis=0, concat_axis=0, tiled=True)
    right = right.reshape(row_count * sequences, right_lanes)
    places_of = [(row, col) for row in range(row_count) for col in range(col_count)]

    def route(to):
        return [(row * col_count + col, to(row, col)[0] * col_count + to(row, col)[1]) for row, col in places_of]

    turned = route(lambda row, col: (turns * col + row % turns, row // turns))
    left = lax.ppermute(left, ("row", "col"), turned)
    lefts = []
    for d in range(turns):
        for k in range(col_count):
            near = route(
                lambda row, col: (row // turns * turns + (row + d) % turns, partner(col, k, col_count))
            )
            lefts.append(lax.ppermute(left[d], ("row", "col"), near) if d + k else left[0])

    residue_float = residue_mask.astype(F32)
    row_mask = lax.dynamic_slice_in_dim(residue_float, r * rows, rows)
    col_mask = lax.dynamic_slice_in_dim(residue_float, c * cols, cols)
    pair_mask = (row_mask[:, None] * col_mask[None, :]).reshape(1, places)
    tri_rows, left_t, left_mask = call(
        functools.partial(prepare_kernel, rows, narrow, turns, col_count, own),
        16,
        [
            ((4 * inner, width), BF16),
            ((rows * narrow, row_count * sequences), BF16),
            ((row_count * sequences, LANES), BF16),
        ],
        [pltpu.VMEM((row_count * sequences, left_lanes), BF16)],
    )(*in_hbm([triangle_proj] + lefts))

    first, normed_pair, gated = call(
        functools.partial(outer_kernel, rows, cols, narrow),
        24,
        [((places, width), BF16), ((places, width), BF16), ((owners, 2 * own, places), BF16)],
        [
            pltpu.VMEM((pieces, cols // members * rows, narrow // pieces * LANES), BF16),
            pltpu.VMEM((2, narrow // pieces * LANES, members * width), BF16),
            pltpu.VMEM((places, width), F32),
        ],
    )(left_t, left_mask, right, tri_rows, pair_mask, *in_hbm([pair_features.reshape(places, width), outer_proj]))

    first_t, gate = call(gate_kernel, 16, [((width, places), F32)] * 2, [])(first, normed_pair, triangle_gate)
    triangle = triangle_by_channel if by_channel else triangle_by_residue
    summed = triangle(row_count, col_count, rows, cols, gated)
    (out,) = call(tail_kernel, 16, [((places, width), BF16)], [pltpu.VMEM((inner, places), F32)])(
        first_t, gate, summed, triangle_out, transition_in, transition_out
    )
    return out.reshape(rows, cols, width)


def solution(mesh):
    placed = (
        P("row", "col", None),
        P("row", "col"),
        P(),
        P("row", "col", None),
    ) + (P(),) * 8

    def body(*args):
        return shards(mesh.shape["row"], mesh.shape["col"], *args)

    return jax.shard_map(body, mesh=mesh, in_specs=placed, out_specs=P("row", "col", None), check_vma=False)
```

time: 92.1 us -> 96.7 us (1.050)
  starting transfers between devices: 29.2 us -> 43.1 us
  blocking collectives: 33.4 us -> 19.9 us
  waiting for transfers between devices: 7.1 us -> 14.5 us
  Pallas kernels: 19.7 us -> 16.4 us
    all_to_all x1 -> x0, blocking collectives: 14.4 us -> none  [triangle_by_channel(): lax.all_to_all(summed, ('row', 'col'), split_axis=0, concat_axis=0, tiled...]
    all_to_all x0 -> x1, waiting for transfers between devices: none -> 11.1 us  [triangle_by_channel(): lax.all_to_all(summed, ('row', 'col'), split_axis=0, concat_axis=0, tiled...]
    ppermute x5 -> x8, starting transfers between devices: 21.8 us -> 32.7 us  [the longest x7 32 us: shards(): lax.ppermute(left[d], ('row', 'col'), near)]
    ppermute x5 -> x8, waiting for transfers between devices: 7.1 us -> 3.42 us  [the longest x7 3.42 us: shards(): lax.ppermute(left[d], ('row', 'col'), near)]
    pallas_call x5 -> x6, Pallas kernels: 19.7 us -> 16.4 us  [the longest x1 4.65 us: shards(): call(functools.partial(outer_kernel, rows, cols, narrow), 24, [((places,...]
    all_to_all x0 -> x1, starting transfers between devices: none -> 3.2 us  [triangle_by_channel(): lax.all_to_all(summed, ('row', 'col'), split_axis=0, concat_axis=0, tiled...]
  transfers between devices with their start and end apart: 6 -> 10, of which waited for: 2 -> 4; matrix products, arithmetic and copies ran while one was open for 0% -> 0% of each run, Pallas kernels for 5% -> 3%
where the time goes in v3:
time: 96.7 us; the launch traced here: 96.3 us
  starting transfers between devices  43.1 us (45%)
  blocking collectives  19.9 us (21%)
  Pallas kernels  16.4 us (17%)
  waiting for transfers between devices  14.5 us (15%)
  local copies, waits for them, and re-layouts  2.15 us (2%)
    ppermute x7, starting transfers between devices, shards(): lax.ppermute(left[d], ('row', 'col'), near)  32 us
    all_to_all x1, blocking collectives, triangle_by_channel(): lax.all_to_all(gated, ('row', 'col'), split_axis=0, concat_axis=0, tiled=...  19.9 us
    all_to_all x1, waiting for transfers between devices, triangle_by_channel(): lax.all_to_all(summed, ('row', 'col'), split_axis=0, concat_axis=0, tiled...  11.1 us
    all_to_all x1, starting transfers between devices, shards(): lax.all_to_all(right, 'row', split_axis=0, concat_axis=0, tiled=True)  7.29 us
    pallas_call x1, Pallas kernels, shards(): call(functools.partial(outer_kernel, rows, cols, narrow), 24, [((places,...  4.65 us
    pallas_call x1, Pallas kernels, shards(): call(functools.partial(side_kernel, chunks, narrow), 16, [((row_count, se...  4.29 us
    ppermute x7, waiting for transfers between devices, shards(): lax.ppermute(left[d], ('row', 'col'), near)  3.42 us
    all_to_all x1, starting transfers between devices, triangle_by_channel(): lax.all_to_all(summed, ('row', 'col'), split_axis=0, concat_axis=0, tiled...  3.2 us
  transfers between devices with their start and end apart: 10, of which 4 were waited for; matrix products, arithmetic and copies ran while one was open for 0% of the time, Pallas kernels for 3%

profile of v3, /device:TPU:0, one launch (start us, length us, event | category | flops | bytes accessed | tf_op | source)
XLA Modules:
  0.0 96.3 jit_solution(3673416132286457502)
XLA Ops:
  0.0 4.3 %shard_map.118 = (bf16[8,32,1664]{2,1,0:T(8,128)(2,1)}, bf16[2,32,896]{2,1,0:T(8,128)(2,1)S(1)}) custom-call(bf16[1536,256]{1,0:T(8,128)(2,1)} %bitcast.11, s32[32,48]{1,0:T(8,128)} %mask_hbm.1, bf16[32,256]{1,0:T(8,128)(2,1)} %bitcast.13, bf16[32,256]{1,0:T(8,128)(2,1)} %bitcast.14), custom_call_target="tpu_custom_call" | custom-call | tf_op jit(solution)/shard_map/pallas_call | solution.py:321
  4.3 7.3 %all-to-all-start = ((bf16[8,32,1664]{2,1,0:T(8,128)(2,1)}), bf16[8,32,1664]{2,1,0:T(8,128)(2,1)S(1)}, u32[]{:S(2)}, u32[]{:S(2)}) async-start(bf16[8,32,1664]{2,1,0:T(8,128)(2,1)} %get-tuple-element.18), calls=%async_computation | async-start | bytes 1703936 | tf_op jit(solution)/shard_map/all_to_all | solution.py:342
  11.6 0.7 collective-permute-start
  12.3 0.0 collective-permute-done
  12.3 0.0 copy-start.4
  12.3 21.5 %collective-permute-start.7 = (bf16[32,896]{1,0:T(8,128)(2,1)S(1)}, bf16[32,896]{1,0:T(8,128)(2,1)S(1)}, u32[]{:S(2)}, u32[]{:S(2)}) collective-permute-start(bf16[32,896]{1,0:T(8,128)(2,1)S(1)} %get-tuple-element.25), channel_id=1, source_target_pairs={{0,7},{1,6},{2,5},{3,4},{4,3},{5,2},{6,1},{7,0},{8,15},{9,14},{10,... | collective-permute-start | bytes 172040 | tf_op jit(solution)/shard_map/ppermute | solution.py:357
  33.8 6.7 %collective-permute-start.6 = (bf16[32,896]{1,0:T(8,128)(2,1)S(1)}, bf16[32,896]{1,0:T(8,128)(2,1)S(1)}, u32[]{:S(2)}, u32[]{:S(2)}) collective-permute-start(bf16[32,896]{1,0:T(8,128)(2,1)S(1)} %get-tuple-element.25), channel_id=1, source_target_pairs={{0,6},{1,7},{2,4},{3,5},{4,2},{5,3},{6,0},{7,1},{8,14},{9,15},{10,... | collective-permute-start | bytes 172040 | tf_op jit(solution)/shard_map/ppermute | solution.py:357
  40.5 0.0 copy-start.12
  40.5 0.7 copy-done.12
  41.2 0.1 dynamic_slice.7
  41.3 0.1 dynamic_slice.6
  41.4 0.3 collective-permute-start.5
  41.7 1.3 %collective-permute-start.4 = (bf16[32,896]{1,0:T(8,128)(2,1)S(1)}, bf16[32,896]{1,0:T(8,128)(2,1)S(1)}, u32[]{:S(2)}, u32[]{:S(2)}) collective-permute-start(bf16[32,896]{1,0:T(8,128)(2,1)S(1)} %get-tuple-element.25), channel_id=1, source_target_pairs={{0,4},{1,5},{2,6},{3,7},{4,0},{5,1},{6,2},{7,3},{8,12},{9,13},{10,... | collective-permute-start | bytes 172040 | tf_op jit(solution)/shard_map/ppermute | solution.py:357
  43.1 0.9 collective-permute-start.3
  44.0 0.0 collective-permute-done.7.refs_7_
  44.0 0.0 copy-start.5
  44.0 1.0 %collective-permute-start.2 = (bf16[32,896]{1,0:T(8,128)(2,1)S(1)}, bf16[32,896]{1,0:T(8,128)(2,1)S(1)}, u32[]{:S(2)}, u32[]{:S(2)}) collective-permute-start(bf16[32,896]{1,0:T(8,128)(2,1)S(1)} %get-tuple-element.26.refs_0_), channel_id=1, source_target_pairs={{0,2},{1,3},{2,0},{3,1},{4,6},{5,7},{6,4},{7,5},{8,10},{9,11},{10,... | collective-permute-start | bytes 172040 | tf_op jit(solution)/shard_map/ppermute | solution.py:357
  45.0 0.0 collective-permute-done.6.refs_6_
  45.0 0.0 copy-start.6
  45.0 0.1 collective-permute-start.1
  45.1 0.1 broadcast_multiply_fusion
  45.2 0.1 mul.34.pair_mask_ref
  45.3 0.1 collective-permute-done.5.refs_5_
  45.4 0.0 copy-start.7
  45.4 1.5 %collective-permute-done.4.refs_4_ = bf16[32,896]{1,0:T(8,128)(2,1)S(1)} collective-permute-done((bf16[32,896]{1,0:T(8,128)(2,1)S(1)}, bf16[32,896]{1,0:T(8,128)(2,1)S(1)}, u32[]{:S(2)}, u32[]{:S(2)}) %collective-permute-start.4) | collective-permute-done | bytes 57376 | tf_op jit(solution)/shard_map/ppermute | solution.py:357
  46.8 0.0 copy-start.8
  46.8 0.0 collective-permute-done.3.refs_3_
  46.8 0.0 copy-start.9
  46.8 1.9 %collective-permute-done.2.refs_2_ = bf16[32,896]{1,0:T(8,128)(2,1)S(1)} collective-permute-done((bf16[32,896]{1,0:T(8,128)(2,1)S(1)}, bf16[32,896]{1,0:T(8,128)(2,1)S(1)}, u32[]{:S(2)}, u32[]{:S(2)}) %collective-permute-start.2) | collective-permute-done | bytes 57376 | tf_op jit(solution)/shard_map/ppermute | solution.py:357
  48.7 0.0 copy-start.10
  48.7 0.0 collective-permute-done.1.refs_1_
  48.7 0.0 copy-done.4
  48.7 0.0 copy-done.5
  48.7 0.0 copy-done.6
  48.8 0.0 copy-done.7
  48.8 0.0 copy-done.8
  48.8 0.0 copy-done.9
  48.8 0.6 copy-done.10
  49.3 0.0 copy-start.11
  49.3 0.6 copy-done.11
  50.0 2.2 %shard_map.119 = (bf16[512,128]{1,0:T(8,128)(2,1)S(1)}, bf16[768,256]{1,0:T(8,128)(2,1)S(1)}, bf16[256,128]{1,0:T(8,128)(2,1)S(1)}) custom-call(bf16[128,512]{1,0:T(8,128)(2,1)} %tri_ref.1, bf16[32,896]{1,0:T(8,128)(2,1)} %copy-done.4, bf16[32,896]{1,0:T(8,128)(2,1)} %copy-done.11, bf16[32,896]{1,0:T(8,128)(2,1)} %copy-done.10, bf16[32,896]{1,0:T(8,128)(2,1)} %copy-done.9, ...), custom_call_target="tpu_custom_call" | custom-call | tf_op jit(solution)/shard_map/pallas_call | solution.py:363
  52.2 0.0 all-to-all-done
  52.2 4.7 %shard_map.120 = (bf16[1152,128]{1,0:T(8,128)(2,1)S(1)}, bf16[1152,128]{1,0:T(8,128)(2,1)S(1)}, bf16[32,8,1152]{2,1,0:T(8,128)(2,1)S(1)}) custom-call(bf16[768,256]{1,0:T(8,128)(2,1)S(1)} %get-tuple-element.16.left_t, bf16[256,128]{1,0:T(8,128)(2,1)S(1)} %get-tuple-element.17.left_mask_ref, bf16[256,1664]{1,0:T(8,128)(2,1)S(1)} %bitcast.10, ...), custom_call_target="tpu_custom_call" | custom-call | tf_op jit(solution)/shard_map/pallas_call | solution.py:374
  56.9 19.9 %all_to_all.15.given_ref = bf16[32,8,1152]{2,1,0:T(8,128)(2,1)S(1)} all-to-all(bf16[32,8,1152]{2,1,0:T(8,128)(2,1)S(1)} %get-tuple-element.24), channel_id=1, replica_groups=mesh['row'=8,'col'=4] {'row','col'}, dimensions={0} | all-to-all | bytes 1179648 | tf_op jit(solution)/shard_map/all_to_all | solution.py:256
  76.7 3.1 %shard_map.122 = bf16[32,4,1152]{2,1,0:T(4,128)(2,1)} custom-call(bf16[32,8,1152]{2,1,0:T(8,128)(2,1)S(1)} %all_to_all.15.given_ref), custom_call_target="tpu_custom_call" | custom-call | tf_op jit(solution)/shard_map/pallas_call | solution.py:259
  79.9 0.0 copy-start.3
  79.9 3.2 %all-to-all-start.2 = ((bf16[32,4,1152]{2,1,0:T(4,128)(2,1)}), bf16[32,4,1152]{2,1,0:T(4,128)(2,1)S(1)}, u32[]{:S(2)}, u32[]{:S(2)}) async-start(bf16[32,4,1152]{2,1,0:T(4,128)(2,1)} %shard_map.122), calls=%async_computation.2 | async-start | bytes 589824 | tf_op jit(solution)/shard_map/all_to_all | solution.py:265
  83.1 0.0 copy-done.3
  83.1 0.0 copy-start
  83.1 0.0 copy-start.1
  83.1 0.0 copy-start.2
  83.1 0.3 shard_map.121
  83.4 11.1 %all-to-all-done.2.summed_ref = bf16[32,4,1152]{2,1,0:T(4,128)(2,1)S(1)} async-done(((bf16[32,4,1152]{2,1,0:T(4,128)(2,1)}), bf16[32,4,1152]{2,1,0:T(4,128)(2,1)S(1)}, u32[]{:S(2)}, u32[]{:S(2)}) %all-to-all-start.2) | async-done | bytes 294944 | tf_op jit(solution)/shard_map/all_to_all | solution.py:265
  94.5 0.0 copy-done
  94.5 0.0 copy-done.1
  94.5 0.0 copy-done.2
  94.5 1.9 %shard_map.123 = bf16[1152,128]{1,0:T(8,128)(2,1)} custom-call(f32[128,1152]{1,0:T(8,128)S(1)} %get-tuple-element.22.first_ref, f32[128,1152]{1,0:T(8,128)S(1)} %get-tuple-element.23.gated_ref, bf16[32,4,1152]{2,1,0:T(4,128)(2,1)S(1)} %all-to-all-done.2.summed_ref, bf16[128,128]{1,0:T(8,128)(2,1)S(1)} %copy-done.2, bf16[128,512]{1,0:T(8,128)(2,1)S(1)} %copy-done, ...), custom_call_target="tpu_custom_call" | custom-call | tf_op jit(solution)/shard_map/pallas_call | solution.py:388
  (2 shorter events, 0.0 us)
Async XLA Ops:
  4.3 47.9 %all-to-all-start = ((bf16[8,32,1664]{2,1,0:T(8,128)(2,1)}), bf16[8,32,1664]{2,1,0:T(8,128)(2,1)S(1)}, u32[]{:S(2)}, u32[]{:S(2)}) async-start(bf16[8,32,1664]{2,1,0:T(8,128)(2,1)} %get-tuple-element.18), calls=%async_computation | async-start | bytes 1703936 | tf_op jit(solution)/shard_map/all_to_all | solution.py:342
  11.6 0.7 collective-permute-start
  12.3 36.4 %copy-start.4 = (bf16[32,896]{1,0:T(8,128)(2,1)}, bf16[32,896]{1,0:T(8,128)(2,1)S(1)}, u32[]{:S(2)}) copy-start(bf16[32,896]{1,0:T(8,128)(2,1)S(1)} %get-tuple-element.26.refs_0_) | copy-start | bytes 172036
  12.3 31.7 %collective-permute-start.7 = (bf16[32,896]{1,0:T(8,128)(2,1)S(1)}, bf16[32,896]{1,0:T(8,128)(2,1)S(1)}, u32[]{:S(2)}, u32[]{:S(2)}) collective-permute-start(bf16[32,896]{1,0:T(8,128)(2,1)S(1)} %get-tuple-element.25), channel_id=1, source_target_pairs={{0,7},{1,6},{2,5},{3,4},{4,3},{5,2},{6,1},{7,0},{8,15},{9,14},{10,... | collective-permute-start | bytes 172040 | tf_op jit(solution)/shard_map/ppermute | solution.py:357
  33.8 11.2 %collective-permute-start.6 = (bf16[32,896]{1,0:T(8,128)(2,1)S(1)}, bf16[32,896]{1,0:T(8,128)(2,1)S(1)}, u32[]{:S(2)}, u32[]{:S(2)}) collective-permute-start(bf16[32,896]{1,0:T(8,128)(2,1)S(1)} %get-tuple-element.25), channel_id=1, source_target_pairs={{0,6},{1,7},{2,4},{3,5},{4,2},{5,3},{6,0},{7,1},{8,14},{9,15},{10,... | collective-permute-start | bytes 172040 | tf_op jit(solution)/shard_map/ppermute | solution.py:357
  40.5 0.7 copy-start.12
  41.4 4.0 %collective-permute-start.5 = (bf16[32,896]{1,0:T(8,128)(2,1)S(1)}, bf16[32,896]{1,0:T(8,128)(2,1)S(1)}, u32[]{:S(2)}, u32[]{:S(2)}) collective-permute-start(bf16[32,896]{1,0:T(8,128)(2,1)S(1)} %get-tuple-element.25), channel_id=1, source_target_pairs={{0,5},{1,4},{2,7},{3,6},{4,1},{5,0},{6,3},{7,2},{8,13},{9,12},{10,... | collective-permute-start | bytes 172040 | tf_op jit(solution)/shard_map/ppermute | solution.py:357
  41.7 5.1 %collective-permute-start.4 = (bf16[32,896]{1,0:T(8,128)(2,1)S(1)}, bf16[32,896]{1,0:T(8,128)(2,1)S(1)}, u32[]{:S(2)}, u32[]{:S(2)}) collective-permute-start(bf16[32,896]{1,0:T(8,128)(2,1)S(1)} %get-tuple-element.25), channel_id=1, source_target_pairs={{0,4},{1,5},{2,6},{3,7},{4,0},{5,1},{6,2},{7,3},{8,12},{9,13},{10,... | collective-permute-start | bytes 172040 | tf_op jit(solution)/shard_map/ppermute | solution.py:357
  43.1 3.8 %collective-permute-start.3 = (bf16[32,896]{1,0:T(8,128)(2,1)S(1)}, bf16[32,896]{1,0:T(8,128)(2,1)S(1)}, u32[]{:S(2)}, u32[]{:S(2)}) collective-permute-start(bf16[32,896]{1,0:T(8,128)(2,1)S(1)} %get-tuple-element.26.refs_0_), channel_id=1, source_target_pairs={{0,3},{1,2},{2,1},{3,0},{4,7},{5,6},{6,5},{7,4},{8,11},{9,10},{10,... | collective-permute-start | bytes 172040 | tf_op jit(solution)/shard_map/ppermute | solution.py:357
  44.0 4.7 %copy-start.5 = (bf16[32,896]{1,0:T(8,128)(2,1)}, bf16[32,896]{1,0:T(8,128)(2,1)S(1)}, u32[]{:S(2)}) copy-start(bf16[32,896]{1,0:T(8,128)(2,1)S(1)} %collective-permute-done.7.refs_7_) | copy-start | bytes 172036
  44.0 4.7 %collective-permute-start.2 = (bf16[32,896]{1,0:T(8,128)(2,1)S(1)}, bf16[32,896]{1,0:T(8,128)(2,1)S(1)}, u32[]{:S(2)}, u32[]{:S(2)}) collective-permute-start(bf16[32,896]{1,0:T(8,128)(2,1)S(1)} %get-tuple-element.26.refs_0_), channel_id=1, source_target_pairs={{0,2},{1,3},{2,0},{3,1},{4,6},{5,7},{6,4},{7,5},{8,10},{9,11},{10,... | collective-permute-start | bytes 172040 | tf_op jit(solution)/shard_map/ppermute | solution.py:357
  45.0 3.7 %copy-start.6 = (bf16[32,896]{1,0:T(8,128)(2,1)}, bf16[32,896]{1,0:T(8,128)(2,1)S(1)}, u32[]{:S(2)}) copy-start(bf16[32,896]{1,0:T(8,128)(2,1)S(1)} %collective-permute-done.6.refs_6_) | copy-start | bytes 172036
  45.0 3.7 %collective-permute-start.1 = (bf16[32,896]{1,0:T(8,128)(2,1)S(1)}, bf16[32,896]{1,0:T(8,128)(2,1)S(1)}, u32[]{:S(2)}, u32[]{:S(2)}) collective-permute-start(bf16[32,896]{1,0:T(8,128)(2,1)S(1)} %get-tuple-element.26.refs_0_), channel_id=1, source_target_pairs={{0,1},{1,0},{2,3},{3,2},{4,5},{5,4},{6,7},{7,6},{8,9},{9,8},{10,11... | collective-permute-start | bytes 172040 | tf_op jit(solution)/shard_map/ppermute | solution.py:357
  45.4 3.4 %copy-start.7 = (bf16[32,896]{1,0:T(8,128)(2,1)}, bf16[32,896]{1,0:T(8,128)(2,1)S(1)}, u32[]{:S(2)}) copy-start(bf16[32,896]{1,0:T(8,128)(2,1)S(1)} %collective-permute-done.5.refs_5_) | copy-start | bytes 172036
  46.8 1.9 %copy-start.8 = (bf16[32,896]{1,0:T(8,128)(2,1)}, bf16[32,896]{1,0:T(8,128)(2,1)S(1)}, u32[]{:S(2)}) copy-start(bf16[32,896]{1,0:T(8,128)(2,1)S(1)} %collective-permute-done.4.refs_4_) | copy-start | bytes 172036
  46.8 1.9 %copy-start.9 = (bf16[32,896]{1,0:T(8,128)(2,1)}, bf16[32,896]{1,0:T(8,128)(2,1)S(1)}, u32[]{:S(2)}) copy-start(bf16[32,896]{1,0:T(8,128)(2,1)S(1)} %collective-permute-done.3.refs_3_) | copy-start | bytes 172036
  48.7 0.6 copy-start.10
  49.3 0.6 copy-start.11
  79.9 3.2 %copy-start.3 = (bf16[128,128]{1,0:T(8,128)(2,1)S(1)}, bf16[128,128]{1,0:T(8,128)(2,1)}, u32[]{:S(2)}) copy-start(bf16[128,128]{1,0:T(8,128)(2,1)} %gate_ref.1) | copy-start | bytes 98308
  79.9 14.6 %all-to-all-start.2 = ((bf16[32,4,1152]{2,1,0:T(4,128)(2,1)}), bf16[32,4,1152]{2,1,0:T(4,128)(2,1)S(1)}, u32[]{:S(2)}, u32[]{:S(2)}) async-start(bf16[32,4,1152]{2,1,0:T(4,128)(2,1)} %shard_map.122), calls=%async_computation.2 | async-start | bytes 589824 | tf_op jit(solution)/shard_map/all_to_all | solution.py:265
  83.1 11.4 %copy-start = (bf16[128,512]{1,0:T(8,128)(2,1)S(1)}, bf16[128,512]{1,0:T(8,128)(2,1)}, u32[]{:S(2)}) copy-start(bf16[128,512]{1,0:T(8,128)(2,1)} %in_ref.1) | copy-start | bytes 393220
  83.1 11.4 %copy-start.1 = (bf16[512,128]{1,0:T(8,128)(2,1)S(1)}, bf16[512,128]{1,0:T(8,128)(2,1)}, u32[]{:S(2)}) copy-start(bf16[512,128]{1,0:T(8,128)(2,1)} %back_ref.1) | copy-start | bytes 393220
  83.1 11.4 %copy-start.2 = (bf16[128,128]{1,0:T(8,128)(2,1)S(1)}, bf16[128,128]{1,0:T(8,128)(2,1)}, u32[]{:S(2)}) copy-start(bf16[128,128]{1,0:T(8,128)(2,1)} %out_w_ref.1) | copy-start | bytes 98308

commit v4 on v3

--- a/solution.py
+++ b/solution.py
@@ -314,7 +314,7 @@
     right_lanes = cols * narrow + LANES
     left_lanes = rows * narrow + LANES
     lines = sequences * cols
-    chunks = 4 if lines % 64 == 0 else 1
+    chunks = 1
     pieces = 4 if narrow % 4 == 0 else 1
 
     hbm = pl.BlockSpec(memory_space=pltpu.HBM)
@@ -369,7 +369,7 @@
             ((row_count * sequences, LANES), BF16),
         ],
         [pltpu.VMEM((row_count * sequences, left_lanes), BF16)],
-    )(*in_hbm([triangle_proj] + lefts))
+    )(triangle_proj, *lefts)
 
     first, normed_pair, gated = call(
         functools.partial(outer_kernel, rows, cols, narrow),
@@ -380,7 +380,7 @@
             pltpu.VMEM((2, narrow // pieces * LANES, members * width), BF16),
             pltpu.VMEM((places, width), F32),
         ],
-    )(left_t, left_mask, right, tri_rows, pair_mask, *in_hbm([pair_features.reshape(places, width), outer_proj]))
+    )(left_t, left_mask, right, tri_rows, pair_mask, pair_features.reshape(places, width), outer_proj)
 
     first_t, gate = call(gate_kernel, 16, [((width, places), F32)] * 2, [])(first, normed_pair, triangle_gate)
     triangle = triangle_by_channel if by_channel else triangle_by_residue

time: 96.7 us -> 92.4 us (0.956)
  Pallas kernels: 16.4 us -> 13.3 us
  local copies, waits for them, and re-layouts: 2.15 us -> 0.96 us
    unnamed x26 -> x16, local copies, waits for them, and re-layouts: 1.9 us -> 0.72 us
    pallas_call x1, Pallas kernels: 2.24 us -> 1.15 us  [shards(): call(functools.partial(prepare_kernel, rows, narrow, turns, col_count, ow...]
    pallas_call x1, Pallas kernels: 4.65 us -> 3.61 us  [shards(): call(functools.partial(outer_kernel, rows, cols, narrow), 24, [((places,...]
    pallas_call x1, Pallas kernels: 4.29 us -> 3.29 us  [shards(): call(functools.partial(side_kernel, chunks, narrow), 16, [((row_count, se...]
  transfers between devices with their start and end apart: 10 -> 10, of which waited for: 4 -> 4; matrix products, arithmetic and copies ran while one was open for 0% -> 0% of each run, Pallas kernels for 3% -> 2%
where the time goes in v4:
time: 92.4 us; the launch traced here: 92 us
  starting transfers between devices  43.1 us (47%)
  blocking collectives  19.9 us (22%)
  waiting for transfers between devices  14.5 us (16%)
  Pallas kernels  13.3 us (14%)
  local copies, waits for them, and re-layouts  0.96 us (1%)
    ppermute x7, starting transfers between devices, shards(): lax.ppermute(left[d], ('row', 'col'), near)  31.8 us
    all_to_all x1, blocking collectives, triangle_by_channel(): lax.all_to_all(gated, ('row', 'col'), split_axis=0, concat_axis=0, tiled=...  19.9 us
    all_to_all x1, waiting for transfers between devices, triangle_by_channel(): lax.all_to_all(summed, ('row', 'col'), split_axis=0, concat_axis=0, tiled...  11.1 us
    all_to_all x1, starting transfers between devices, shards(): lax.all_to_all(right, 'row', split_axis=0, concat_axis=0, tiled=True)  7.29 us
    pallas_call x1, Pallas kernels, shards(): call(functools.partial(outer_kernel, rows, cols, narrow), 24, [((places,...  3.61 us
    ppermute x7, waiting for transfers between devices, shards(): lax.ppermute(left[d], ('row', 'col'), near)  3.41 us
    pallas_call x1, Pallas kernels, shards(): call(functools.partial(side_kernel, chunks, narrow), 16, [((row_count, se...  3.29 us
    all_to_all x1, starting transfers between devices, triangle_by_channel(): lax.all_to_all(summed, ('row', 'col'), split_axis=0, concat_axis=0, tiled...  3.2 us
  transfers between devices with their start and end apart: 10, of which 4 were waited for; matrix products, arithmetic and copies ran while one was open for 0% of the time, Pallas kernels for 2%

profile of v4, /device:TPU:0, one launch (start us, length us, event | category | flops | bytes accessed | tf_op | source)
XLA Modules:
  0.0 92.0 jit_solution(5334482134068687446)
XLA Ops:
  0.0 3.3 %shard_map.118 = (bf16[8,32,1664]{2,1,0:T(8,128)(2,1)}, bf16[2,32,896]{2,1,0:T(8,128)(2,1)S(1)}) custom-call(bf16[1536,256]{1,0:T(8,128)(2,1)} %bitcast.12, s32[32,48]{1,0:T(8,128)} %mask_hbm.1, bf16[32,256]{1,0:T(8,128)(2,1)} %bitcast.13, bf16[32,256]{1,0:T(8,128)(2,1)} %bitcast.14), custom_call_target="tpu_custom_call" | custom-call | tf_op jit(solution)/shard_map/pallas_call | solution.py:321
  3.3 7.3 %all-to-all-start = ((bf16[8,32,1664]{2,1,0:T(8,128)(2,1)}), bf16[8,32,1664]{2,1,0:T(8,128)(2,1)S(1)}, u32[]{:S(2)}, u32[]{:S(2)}) async-start(bf16[8,32,1664]{2,1,0:T(8,128)(2,1)} %get-tuple-element.18), calls=%async_computation | async-start | bytes 1703936 | tf_op jit(solution)/shard_map/all_to_all | solution.py:342
  10.6 0.0 copy-start.4
  10.6 0.8 collective-permute-start
  11.4 0.0 collective-permute-done
  11.4 21.4 %collective-permute-start.7 = (bf16[32,896]{1,0:T(8,128)(2,1)S(1)}, bf16[32,896]{1,0:T(8,128)(2,1)S(1)}, u32[]{:S(2)}, u32[]{:S(2)}) collective-permute-start(bf16[32,896]{1,0:T(8,128)(2,1)S(1)} %get-tuple-element.25), channel_id=1, source_target_pairs={{0,7},{1,6},{2,5},{3,4},{4,3},{5,2},{6,1},{7,0},{8,15},{9,14},{10,... | collective-permute-start | bytes 172040 | tf_op jit(solution)/shard_map/ppermute | solution.py:357
  32.8 6.7 %collective-permute-start.6 = (bf16[32,896]{1,0:T(8,128)(2,1)S(1)}, bf16[32,896]{1,0:T(8,128)(2,1)S(1)}, u32[]{:S(2)}, u32[]{:S(2)}) collective-permute-start(bf16[32,896]{1,0:T(8,128)(2,1)S(1)} %get-tuple-element.25), channel_id=1, source_target_pairs={{0,6},{1,7},{2,4},{3,5},{4,2},{5,3},{6,0},{7,1},{8,14},{9,15},{10,... | collective-permute-start | bytes 172040 | tf_op jit(solution)/shard_map/ppermute | solution.py:357
  39.5 0.0 copy-start.7
  39.5 0.7 copy-done.7
  40.2 0.1 dynamic_slice.7
  40.3 0.1 dynamic_slice.6
  40.4 0.3 collective-permute-start.5
  40.7 1.3 %collective-permute-start.4 = (bf16[32,896]{1,0:T(8,128)(2,1)S(1)}, bf16[32,896]{1,0:T(8,128)(2,1)S(1)}, u32[]{:S(2)}, u32[]{:S(2)}) collective-permute-start(bf16[32,896]{1,0:T(8,128)(2,1)S(1)} %get-tuple-element.25), channel_id=1, source_target_pairs={{0,4},{1,5},{2,6},{3,7},{4,0},{5,1},{6,2},{7,3},{8,12},{9,13},{10,... | collective-permute-start | bytes 172040 | tf_op jit(solution)/shard_map/ppermute | solution.py:357
  42.0 0.9 %collective-permute-start.3 = (bf16[32,896]{1,0:T(8,128)(2,1)S(1)}, bf16[32,896]{1,0:T(8,128)(2,1)S(1)}, u32[]{:S(2)}, u32[]{:S(2)}) collective-permute-start(bf16[32,896]{1,0:T(8,128)(2,1)S(1)} %get-tuple-element.26.refs_0_), channel_id=1, source_target_pairs={{0,3},{1,2},{2,1},{3,0},{4,7},{5,6},{6,5},{7,4},{8,11},{9,10},{10,... | collective-permute-start | bytes 172040 | tf_op jit(solution)/shard_map/ppermute | solution.py:357
  43.0 0.0 collective-permute-done.7.refs_7_
  43.0 0.9 %collective-permute-start.2 = (bf16[32,896]{1,0:T(8,128)(2,1)S(1)}, bf16[32,896]{1,0:T(8,128)(2,1)S(1)}, u32[]{:S(2)}, u32[]{:S(2)}) collective-permute-start(bf16[32,896]{1,0:T(8,128)(2,1)S(1)} %get-tuple-element.26.refs_0_), channel_id=1, source_target_pairs={{0,2},{1,3},{2,0},{3,1},{4,6},{5,7},{6,4},{7,5},{8,10},{9,11},{10,... | collective-permute-start | bytes 172040 | tf_op jit(solution)/shard_map/ppermute | solution.py:357
  43.9 0.0 collective-permute-done.6.refs_6_
  43.9 0.2 collective-permute-start.1
  44.1 0.1 broadcast_multiply_fusion
  44.2 0.1 mul.34.pair_mask_ref
  44.3 0.0 copy-start
  44.3 0.0 copy-start.1
  44.3 0.1 collective-permute-done.5.refs_5_
  44.4 1.5 %collective-permute-done.4.refs_4_ = bf16[32,896]{1,0:T(8,128)(2,1)S(1)} collective-permute-done((bf16[32,896]{1,0:T(8,128)(2,1)S(1)}, bf16[32,896]{1,0:T(8,128)(2,1)S(1)}, u32[]{:S(2)}, u32[]{:S(2)}) %collective-permute-start.4) | collective-permute-done | bytes 57376 | tf_op jit(solution)/shard_map/ppermute | solution.py:357
  45.8 0.0 collective-permute-done.3.refs_3_
  45.8 1.9 %collective-permute-done.2.refs_2_ = bf16[32,896]{1,0:T(8,128)(2,1)S(1)} collective-permute-done((bf16[32,896]{1,0:T(8,128)(2,1)S(1)}, bf16[32,896]{1,0:T(8,128)(2,1)S(1)}, u32[]{:S(2)}, u32[]{:S(2)}) %collective-permute-start.2) | collective-permute-done | bytes 57376 | tf_op jit(solution)/shard_map/ppermute | solution.py:357
  47.7 0.0 collective-permute-done.1.refs_1_
  47.7 0.0 copy-done.4
  47.7 1.2 %shard_map.119 = (bf16[512,128]{1,0:T(8,128)(2,1)S(1)}, bf16[768,256]{1,0:T(8,128)(2,1)S(1)}, bf16[256,128]{1,0:T(8,128)(2,1)S(1)}) custom-call(bf16[128,512]{1,0:T(8,128)(2,1)S(1)} %copy-done.4, bf16[32,896]{1,0:T(8,128)(2,1)S(1)} %get-tuple-element.26.refs_0_, bf16[32,896]{1,0:T(8,128)(2,1)S(1)} %collective-permute-done.1.refs_1_, ...), custom_call_target="tpu_custom_call" | custom-call | tf_op jit(solution)/shard_map/pallas_call | solution.py:363
  48.9 0.0 all-to-all-done
  48.9 0.0 copy-done
  48.9 0.0 copy-done.1
  48.9 3.6 %shard_map.120 = (bf16[1152,128]{1,0:T(8,128)(2,1)S(1)}, bf16[1152,128]{1,0:T(8,128)(2,1)S(1)}, bf16[32,8,1152]{2,1,0:T(8,128)(2,1)S(1)}) custom-call(bf16[768,256]{1,0:T(8,128)(2,1)S(1)} %get-tuple-element.16.left_t, bf16[256,128]{1,0:T(8,128)(2,1)S(1)} %get-tuple-element.17.left_mask_ref, bf16[256,1664]{1,0:T(8,128)(2,1)S(1)} %bitcast.10, ...), custom_call_target="tpu_custom_call" | custom-call | tf_op jit(solution)/shard_map/pallas_call | solution.py:374
  52.5 19.9 %all_to_all.15.given_ref = bf16[32,8,1152]{2,1,0:T(8,128)(2,1)S(1)} all-to-all(bf16[32,8,1152]{2,1,0:T(8,128)(2,1)S(1)} %get-tuple-element.24), channel_id=1, replica_groups=mesh['row'=8,'col'=4] {'row','col'}, dimensions={0} | all-to-all | bytes 1179648 | tf_op jit(solution)/shard_map/all_to_all | solution.py:256
  72.4 3.1 %shard_map.122 = bf16[32,4,1152]{2,1,0:T(4,128)(2,1)} custom-call(bf16[32,8,1152]{2,1,0:T(8,128)(2,1)S(1)} %all_to_all.15.given_ref), custom_call_target="tpu_custom_call" | custom-call | tf_op jit(solution)/shard_map/pallas_call | solution.py:259
  75.5 0.0 copy-start.6
  75.5 3.2 %all-to-all-start.2 = ((bf16[32,4,1152]{2,1,0:T(4,128)(2,1)}), bf16[32,4,1152]{2,1,0:T(4,128)(2,1)S(1)}, u32[]{:S(2)}, u32[]{:S(2)}) async-start(bf16[32,4,1152]{2,1,0:T(4,128)(2,1)} %shard_map.122), calls=%async_computation.2 | async-start | bytes 589824 | tf_op jit(solution)/shard_map/all_to_all | solution.py:265
  78.7 0.0 copy-done.6
  78.7 0.0 copy-start.2
  78.8 0.0 copy-start.3
  78.8 0.0 copy-start.5
  78.8 0.3 shard_map.121
  79.1 11.1 %all-to-all-done.2.summed_ref = bf16[32,4,1152]{2,1,0:T(4,128)(2,1)S(1)} async-done(((bf16[32,4,1152]{2,1,0:T(4,128)(2,1)}), bf16[32,4,1152]{2,1,0:T(4,128)(2,1)S(1)}, u32[]{:S(2)}, u32[]{:S(2)}) %all-to-all-start.2) | async-done | bytes 294944 | tf_op jit(solution)/shard_map/all_to_all | solution.py:265
  90.1 0.0 copy-done.2
  90.1 0.0 copy-done.3
  90.1 0.0 copy-done.5
  90.1 1.9 %shard_map.123 = bf16[1152,128]{1,0:T(8,128)(2,1)} custom-call(f32[128,1152]{1,0:T(8,128)S(1)} %get-tuple-element.22.first_ref, f32[128,1152]{1,0:T(8,128)S(1)} %get-tuple-element.23.gated_ref, bf16[32,4,1152]{2,1,0:T(4,128)(2,1)S(1)} %all-to-all-done.2.summed_ref, bf16[128,128]{1,0:T(8,128)(2,1)S(1)} %copy-done.5, bf16[128,512]{1,0:T(8,128)(2,1)S(1)} %copy-done.2, ...), custom_call_target="tpu_custom_call" | custom-call | tf_op jit(solution)/shard_map/pallas_call | solution.py:388
  (2 shorter events, 0.0 us)
Async XLA Ops:
  3.3 45.6 %all-to-all-start = ((bf16[8,32,1664]{2,1,0:T(8,128)(2,1)}), bf16[8,32,1664]{2,1,0:T(8,128)(2,1)S(1)}, u32[]{:S(2)}, u32[]{:S(2)}) async-start(bf16[8,32,1664]{2,1,0:T(8,128)(2,1)} %get-tuple-element.18), calls=%async_computation | async-start | bytes 1703936 | tf_op jit(solution)/shard_map/all_to_all | solution.py:342
  10.6 37.1 %copy-start.4 = (bf16[128,512]{1,0:T(8,128)(2,1)S(1)}, bf16[128,512]{1,0:T(8,128)(2,1)}, u32[]{:S(2)}) copy-start(bf16[128,512]{1,0:T(8,128)(2,1)} %tri_ref.1) | copy-start | bytes 393220
  10.6 0.8 collective-permute-start
  11.4 31.6 %collective-permute-start.7 = (bf16[32,896]{1,0:T(8,128)(2,1)S(1)}, bf16[32,896]{1,0:T(8,128)(2,1)S(1)}, u32[]{:S(2)}, u32[]{:S(2)}) collective-permute-start(bf16[32,896]{1,0:T(8,128)(2,1)S(1)} %get-tuple-element.25), channel_id=1, source_target_pairs={{0,7},{1,6},{2,5},{3,4},{4,3},{5,2},{6,1},{7,0},{8,15},{9,14},{10,... | collective-permute-start | bytes 172040 | tf_op jit(solution)/shard_map/ppermute | solution.py:357
  32.8 11.1 %collective-permute-start.6 = (bf16[32,896]{1,0:T(8,128)(2,1)S(1)}, bf16[32,896]{1,0:T(8,128)(2,1)S(1)}, u32[]{:S(2)}, u32[]{:S(2)}) collective-permute-start(bf16[32,896]{1,0:T(8,128)(2,1)S(1)} %get-tuple-element.25), channel_id=1, source_target_pairs={{0,6},{1,7},{2,4},{3,5},{4,2},{5,3},{6,0},{7,1},{8,14},{9,15},{10,... | collective-permute-start | bytes 172040 | tf_op jit(solution)/shard_map/ppermute | solution.py:357
  39.5 0.7 copy-start.7
  40.4 4.0 %collective-permute-start.5 = (bf16[32,896]{1,0:T(8,128)(2,1)S(1)}, bf16[32,896]{1,0:T(8,128)(2,1)S(1)}, u32[]{:S(2)}, u32[]{:S(2)}) collective-permute-start(bf16[32,896]{1,0:T(8,128)(2,1)S(1)} %get-tuple-element.25), channel_id=1, source_target_pairs={{0,5},{1,4},{2,7},{3,6},{4,1},{5,0},{6,3},{7,2},{8,13},{9,12},{10,... | collective-permute-start | bytes 172040 | tf_op jit(solution)/shard_map/ppermute | solution.py:357
  40.7 5.1 %collective-permute-start.4 = (bf16[32,896]{1,0:T(8,128)(2,1)S(1)}, bf16[32,896]{1,0:T(8,128)(2,1)S(1)}, u32[]{:S(2)}, u32[]{:S(2)}) collective-permute-start(bf16[32,896]{1,0:T(8,128)(2,1)S(1)} %get-tuple-element.25), channel_id=1, source_target_pairs={{0,4},{1,5},{2,6},{3,7},{4,0},{5,1},{6,2},{7,3},{8,12},{9,13},{10,... | collective-permute-start | bytes 172040 | tf_op jit(solution)/shard_map/ppermute | solution.py:357
  42.0 3.8 %collective-permute-start.3 = (bf16[32,896]{1,0:T(8,128)(2,1)S(1)}, bf16[32,896]{1,0:T(8,128)(2,1)S(1)}, u32[]{:S(2)}, u32[]{:S(2)}) collective-permute-start(bf16[32,896]{1,0:T(8,128)(2,1)S(1)} %get-tuple-element.26.refs_0_), channel_id=1, source_target_pairs={{0,3},{1,2},{2,1},{3,0},{4,7},{5,6},{6,5},{7,4},{8,11},{9,10},{10,... | collective-permute-start | bytes 172040 | tf_op jit(solution)/shard_map/ppermute | solution.py:357
  43.0 4.7 %collective-permute-start.2 = (bf16[32,896]{1,0:T(8,128)(2,1)S(1)}, bf16[32,896]{1,0:T(8,128)(2,1)S(1)}, u32[]{:S(2)}, u32[]{:S(2)}) collective-permute-start(bf16[32,896]{1,0:T(8,128)(2,1)S(1)} %get-tuple-element.26.refs_0_), channel_id=1, source_target_pairs={{0,2},{1,3},{2,0},{3,1},{4,6},{5,7},{6,4},{7,5},{8,10},{9,11},{10,... | collective-permute-start | bytes 172040 | tf_op jit(solution)/shard_map/ppermute | solution.py:357
  43.9 3.8 %collective-permute-start.1 = (bf16[32,896]{1,0:T(8,128)(2,1)S(1)}, bf16[32,896]{1,0:T(8,128)(2,1)S(1)}, u32[]{:S(2)}, u32[]{:S(2)}) collective-permute-start(bf16[32,896]{1,0:T(8,128)(2,1)S(1)} %get-tuple-element.26.refs_0_), channel_id=1, source_target_pairs={{0,1},{1,0},{2,3},{3,2},{4,5},{5,4},{6,7},{7,6},{8,9},{9,8},{10,11... | collective-permute-start | bytes 172040 | tf_op jit(solution)/shard_map/ppermute | solution.py:357
  44.3 4.6 %copy-start = (bf16[24,48,128]{2,1,0:T(8,128)(2,1)S(1)}, bf16[24,48,128]{2,1,0:T(8,128)(2,1)}, u32[]{:S(2)}) copy-start(bf16[24,48,128]{2,1,0:T(8,128)(2,1)} %param.15) | copy-start | bytes 884740
  44.3 4.6 %copy-start.1 = (bf16[1024,128]{1,0:T(8,128)(2,1)S(1)}, bf16[1024,128]{1,0:T(8,128)(2,1)}, u32[]{:S(2)}) copy-start(bf16[1024,128]{1,0:T(8,128)(2,1)} %proj_ref.1) | copy-start | bytes 786436
  75.5 3.2 %copy-start.6 = (bf16[128,128]{1,0:T(8,128)(2,1)S(1)}, bf16[128,128]{1,0:T(8,128)(2,1)}, u32[]{:S(2)}) copy-start(bf16[128,128]{1,0:T(8,128)(2,1)} %gate_ref.1) | copy-start | bytes 98308
  75.5 14.6 %all-to-all-start.2 = ((bf16[32,4,1152]{2,1,0:T(4,128)(2,1)}), bf16[32,4,1152]{2,1,0:T(4,128)(2,1)S(1)}, u32[]{:S(2)}, u32[]{:S(2)}) async-start(bf16[32,4,1152]{2,1,0:T(4,128)(2,1)} %shard_map.122), calls=%async_computation.2 | async-start | bytes 589824 | tf_op jit(solution)/shard_map/all_to_all | solution.py:265
  78.7 11.4 %copy-start.2 = (bf16[128,512]{1,0:T(8,128)(2,1)S(1)}, bf16[128,512]{1,0:T(8,128)(2,1)}, u32[]{:S(2)}) copy-start(bf16[128,512]{1,0:T(8,128)(2,1)} %in_ref.1) | copy-start | bytes 393220
  78.8 11.4 %copy-start.3 = (bf16[512,128]{1,0:T(8,128)(2,1)S(1)}, bf16[512,128]{1,0:T(8,128)(2,1)}, u32[]{:S(2)}) copy-start(bf16[512,128]{1,0:T(8,128)(2,1)} %back_ref.1) | copy-start | bytes 393220
  78.8 11.4 %copy-start.5 = (bf16[128,128]{1,0:T(8,128)(2,1)S(1)}, bf16[128,128]{1,0:T(8,128)(2,1)}, u32[]{:S(2)}) copy-start(bf16[128,128]{1,0:T(8,128)(2,1)} %out_w_ref.1) | copy-start | bytes 98308

commit v5 on v4

v5 whole, which is shorter than its diff:
```python
import functools

import jax
import jax.numpy as jnp
from jax import lax
from jax.experimental import pallas as pl
from jax.experimental.pallas import tpu as pltpu
from jax.sharding import PartitionSpec as P


epsilon = 1e-05
LANES = 128
BF16 = jnp.bfloat16
F32 = jnp.float32
NT = (((1,), (1,)), ((), ()))
TN = (((0,), (0,)), ((), ()))


def matmul(a, b, dims=(((1,), (0,)), ((), ()))):
    return lax.dot_general(a, b, dims, preferred_element_type=F32)


def iota(shape, axis):
    return lax.broadcasted_iota(jnp.int32, shape, axis)


def normalize(values, axis=-1):
    mean_value = jnp.mean(values, axis=axis, keepdims=True)
    centered = values - mean_value
    variance = jnp.mean(centered * centered, axis=axis, keepdims=True)
    return centered * lax.rsqrt(variance + epsilon)


def in_hbm(values):
    return [pltpu.with_memory_space_constraint(value, pltpu.HBM) for value in values]


def call(kernel, mebibytes, outs, scratch, in_specs=None, out_specs=None):
    return pl.pallas_call(
        kernel,
        out_shape=tuple(jax.ShapeDtypeStruct(*out) for out in outs),
        out_specs=out_specs or (VMEM,) * len(outs),
        scratch_shapes=scratch,
        compiler_params=pltpu.CompilerParams(vmem_limit_bytes=mebibytes * 1024 * 1024),
        **({} if in_specs is None else {"in_specs": in_specs}),
    )


VMEM = pl.BlockSpec(memory_space=pltpu.VMEM)


def pack_side(projected, mask, narrow, first, count, put):
    sequences, cols = mask.shape
    members = LANES // narrow
    lane = iota((sequences, LANES), 1)
    groups = count // members
    width = groups * LANES
    residue = first + iota((cols, width), 1) // narrow
    masks = matmul(mask, (iota((cols, width), 0) == residue).astype(BF16))
    for group in range(groups):
        value = None
        for member in range(members):
            part = projected[pl.ds(first + group * members + member, sequences, stride=cols), :]
            value = part if value is None else jnp.where(lane >= member * narrow, part, value)
        put(group, (value * masks[:, group * LANES : (group + 1) * LANES]).astype(BF16))
    at = iota((cols, LANES), 1)
    pick = (iota((cols, LANES), 0) - first == at) & (at < count)
    put(groups, matmul(mask, pick.astype(BF16)).astype(BF16))


def side_kernel(
    narrow, align_hbm, mask_hbm, left_w_hbm, right_w_hbm, right_hbm, left_ref,
    left_rows, right_rows, align, mask_int, left_w, right_w, packed, align_sem, mask_sem, left_sem, right_sem, out_sem,
):
    fetches = [
        pltpu.make_async_copy(left_w_hbm, left_w, left_sem),
        pltpu.make_async_copy(right_w_hbm, right_w, right_sem),
        pltpu.make_async_copy(align_hbm, align, align_sem),
        pltpu.make_async_copy(mask_hbm, mask_int, mask_sem),
    ]
    for copy in fetches:
        copy.start()
    for copy in fetches:
        copy.wait()
    members = LANES // narrow
    both = jnp.concatenate([left_w[...]] * members + [right_w[...]] * members, axis=0)
    normed = normalize(align[...].astype(F32)).astype(BF16)
    value = matmul(normed, both, NT)
    left_rows[...] = value[:, :LANES]
    right_rows[...] = value[:, LANES:]
    mask = mask_int[...].astype(BF16)
    cols = mask.shape[1]
    parts = packed.shape[0]
    for h in range(parts):

        def put_right(group, value):
            packed[h, :, group * LANES : (group + 1) * LANES] = value

        pack_side(right_rows, mask, narrow, h * (cols // parts), cols // parts, put_right)
    copies = [
        pltpu.make_async_copy(packed.at[n % parts], right_hbm.at[n], out_sem.at[n])
        for n in range(right_hbm.shape[0])
    ]
    for copy in copies:
        copy.start()

    def put_left(group, value):
        left_ref[:, group * LANES : (group + 1) * LANES] = value

    pack_side(left_rows, mask, narrow, 0, cols, put_left)
    for copy in copies:
        copy.wait()


def prepare_kernel(own, tri_ref, pair_ref, *refs):
    *given_refs, block_ref, tri_rows_ref = refs
    rows, cols, _ = pair_ref.shape
    parts = cols // rows
    x = lax.rem(lax.axis_index("row"), parts)
    for i in range(rows):
        at = pl.ds(pl.multiple_of((x * rows + i) * rows, 8), rows)
        block_ref[at, :] = pair_ref[i, pl.ds(pl.multiple_of(x * rows, 8), rows), :]
        for d, given_ref in enumerate(given_refs, 1):
            at = pl.ds(pl.multiple_of((lax.rem(x - d + parts, parts) * rows + i) * rows, 8), rows)
            block_ref[at, :] = given_ref[i]
    out = tri_ref.shape[0]
    at = iota((4 * out, 4 * out), 0)
    kind, rest = at // (2 * out), at % (2 * out)
    owner, side, channel = rest // (2 * own), rest // own % 2, rest % own
    column = side * 2 * out + kind * out + owner * own + channel
    pick = (iota((4 * out, 4 * out), 1) == column).astype(BF16)
    tri_rows_ref[...] = matmul(pick, tri_ref[...], NT).astype(BF16)


def outer_kernel(tall, short, narrow, parts, right_ref, pair_ref, proj_ref, tri_ref, pair_mask_ref, *refs):
    *left_refs, first_ref, tri_out_ref, left, right_t, proj, stacked, spread, moved, normed = refs
    sources = len(left_refs) // parts
    sequences = left_refs[0].shape[0]
    x, column = lax.rem(lax.axis_index("row"), parts), lax.axis_index("col")
    for n, left_ref in enumerate(left_refs):
        d, k = n // sources, n % sources
        start = (source(column, k, sources) * parts + lax.rem(x - d + parts, parts)) * sequences
        left[pl.ds(pl.multiple_of(start, sequences), sequences), :] = left_ref[...]
    members = LANES // narrow
    groups = tall // members
    left_width, right_width = tall * narrow, short * narrow
    width = pair_ref.shape[1]
    planes = right_t.shape[0]
    for p in range(planes):
        right_t[p] = right_ref[p * LANES : (p + 1) * LANES, :right_width].astype(F32).T
    proj[...] = proj_ref[...].astype(F32)
    steps = stacked.shape[0]
    step = narrow // steps
    spread[...] = jnp.zeros_like(spread)
    total = None
    for n in range(steps):
        some = []
        for p in range(planes):
            each = [right_t.at[p][pl.ds(n * step + d, short, stride=narrow), :] for d in range(step)]
            some.append(jnp.concatenate(each, axis=0).astype(BF16))
        block = matmul(jnp.concatenate(some, axis=1), left[:, :left_width])
        for d in range(step):
            lanes = slice(d * LANES, (d + 1) * LANES)
            for g in range(0, groups, 2):
                two = [
                    block[d * short : (d + 1) * short, (g + m) * LANES : (g + m + 1) * LANES] for m in range(2)
                ]
                stacked[n, g * short : (g + 2) * short, lanes] = jnp.concatenate(two, axis=0).astype(BF16)
            part = proj[pl.ds(n * step + d, narrow, stride=narrow), :].astype(BF16)
            for m in range(members):
                start = d * LANES + m * narrow
                spread[n % 2, start : start + narrow, m * width : (m + 1) * width] = part
        term = matmul(stacked[n], spread[n % 2])
        total = term if total is None else total + term
    counts = matmul(right_ref[:, right_width:], left[:, left_width:], TN)[:short, :]
    scale = 1.0 / jnp.maximum(counts, 1.0)
    for g in range(groups):
        for m in range(members):
            i = g * members + m
            at = slice(i * short, (i + 1) * short)
            part = total[g * short : (g + 1) * short, m * width : (m + 1) * width]
            moved[at, :] = part * scale[:, i : i + 1] + pair_ref[at, :].astype(F32)
    for j in range(short):
        first = moved[pl.ds(j, tall, stride=short), :].astype(BF16)
        first_ref[j * tall : (j + 1) * tall, :] = first
        normed[j * tall : (j + 1) * tall, :] = normalize(first.astype(F32)).astype(BF16)
    devices, pair, _ = tri_out_ref.shape
    half = devices * pair
    projections = matmul(tri_ref[...], normed[...], NT)
    gated = jax.nn.sigmoid(projections[:half]) * projections[half:] * pair_mask_ref[...]
    gated = gated.astype(BF16)
    for d in range(devices):
        tri_out_ref[d] = gated[d * pair : (d + 1) * pair, :]


def triangle_kernel(row_count, col_count, rows, cols, own, given_ref, out_ref, opened, summed):
    pair = 2 * own
    planes = opened.shape[0]
    parts = cols // rows
    each = -(-col_count // planes)
    used = each * cols

    def open_column(c, carry):
        for a in range(col_count):
            lanes = slice(a % each * cols, (a % each + 1) * cols)
            for x in range(parts):
                value = given_ref[(a * parts + x) * col_count + c].astype(F32)
                for k in range(rows):
                    start = pl.multiple_of((c * cols + x * rows + k) * pair, pair)
                    opened[a // each, pl.ds(start, pair), lanes] = value[:, k * cols : (k + 1) * cols]
        return carry

    residues = row_count * rows
    lax.fori_loop(0, col_count, open_column, 0)
    for t in range(own):
        left = [opened.at[p][pl.ds(t, residues, stride=pair), :].astype(BF16) for p in range(planes)]
        right = [opened.at[p][pl.ds(own + t, residues, stride=pair), :].astype(BF16) for p in range(planes)]
        for p in range(planes):
            count = min(used, residues - p * used)
            for q in range(planes):
                total = matmul(left[p], right[q], TN)[:count]
                summed.at[q][pl.ds(p * used * pair + t, count, stride=pair), :] = total

    def close_row(r, carry):
        for c in range(col_count):
            lanes = slice(c % each * cols, (c % each + 1) * cols)
            parts = []
            for i in range(rows):
                start = pl.multiple_of((r * rows + i) * pair, pair)
                parts.append(summed[c // each, pl.ds(start, pair), lanes])
            out_ref[r * col_count + c] = jnp.concatenate(parts, axis=1)[:own].astype(BF16)
        return carry

    lax.fori_loop(0, row_count, close_row, 0)


def partner(index, k, count):
    return index ^ k if count & (count - 1) == 0 else (index + k) % count


def source(index, k, count):
    return index ^ k if count & (count - 1) == 0 else lax.rem(index - k + count, count)


def triangle_by_channel(row_count, col_count, rows, cols, gated):
    devices, pair, places = gated.shape
    own = pair // 2
    gated = lax.all_to_all(gated, ("row", "col"), split_axis=0, concat_axis=0, tiled=True)
    residues = row_count * rows
    planes = -(-col_count // (LANES // cols))
    (summed,) = call(
        functools.partial(triangle_kernel, row_count, col_count, rows, cols, own),
        16,
        [((devices, own, places), BF16)],
        [pltpu.VMEM((planes, residues * pair, LANES), F32)] * 2,
    )(gated)
    summed = lax.all_to_all(summed, ("row", "col"), split_axis=0, concat_axis=0, tiled=True)
    return summed


def triangle_by_residue(row_count, col_count, rows, cols, gated):
    _, pair, places = gated.shape
    both = gated.reshape(2, pair // 2, cols, rows).transpose(0, 3, 2, 1)
    right = lax.all_gather(both[1], "row", axis=0, tiled=True)
    right = lax.all_to_all(right, "col", split_axis=0, concat_axis=1, tiled=True)
    left = lax.all_gather(both[0], "col", axis=1, tiled=True)
    summed = jnp.einsum("ikc,jkc->cij", left, right, preferred_element_type=F32)
    return summed.reshape(1, pair // 2, places).astype(BF16)


def gate_kernel(first_ref, gate_w_ref, *refs):
    *given_refs, first_t_ref, gated_ref, home = refs
    rows, cols, _ = first_ref.shape
    parts = cols // rows
    x = lax.rem(lax.axis_index("row"), parts)
    for j in range(rows):
        value = first_ref[j, pl.ds(pl.multiple_of(x * rows, 8), rows), :]
        home[pl.ds(x * rows + j, rows, stride=cols), :] = value.astype(F32)
        for d, given_ref in enumerate(given_refs, 1):
            at = pl.ds(lax.rem(x - d + parts, parts) * rows + j, rows, stride=cols)
            home[at, :] = given_ref[j].astype(F32)
    first = home[...]
    first_t_ref[...] = first.T
    gated_ref[...] = jax.nn.sigmoid(matmul(gate_w_ref[...].T, normalize(first).astype(BF16), NT))


def tail_kernel(first_ref, gated_ref, summed_ref, out_w_ref, in_ref, back_ref, out_ref, summed):
    own = summed_ref.shape[1]
    for d in range(summed_ref.shape[0]):
        summed[d * own : (d + 1) * own, :] = summed_ref[d].astype(F32)
    normed_sum = normalize(summed[...], 0).astype(BF16)
    update = gated_ref[...] * matmul(out_w_ref[...].T, normed_sum)
    second = (first_ref[...] + update).astype(BF16).astype(F32)
    normed_second = normalize(second, 0).astype(BF16)
    hidden = jnp.maximum(matmul(in_ref[...].T, normed_second), 0.0).astype(BF16)
    result = second + matmul(back_ref[...].T, hidden)
    out_ref[...] = result.T.astype(BF16)


def shards(
    row_count, col_count, alignment, alignment_mask, residue_mask, pair_features, outer_product_left, outer_product_right,
    outer_proj, triangle_proj, triangle_gate, triangle_out, transition_in, transition_out,
):
    rows, cols, width = pair_features.shape
    sequences, _, channels = alignment.shape
    narrow = outer_product_left.shape[1]
    inner = triangle_out.shape[0]
    devices = row_count * col_count
    turns = cols // rows
    places = rows * cols
    r, c = lax.axis_index("row"), lax.axis_index("col")
    by_channel = inner % devices == 0
    owners = devices if by_channel else 1
    own = inner // owners
    members = LANES // narrow
    right_lanes = rows * narrow + LANES
    left_lanes = cols * narrow + LANES
    lines = sequences * cols
    pieces = 4 if narrow % 4 == 0 else 1
    x = r % turns

    hbm = pl.BlockSpec(memory_space=pltpu.HBM)
    right, left = call(
        functools.partial(side_kernel, narrow),
        16,
        [((row_count, sequences, right_lanes), BF16), ((sequences, left_lanes), BF16)],
        [
            pltpu.VMEM((lines, LANES), F32),
            pltpu.VMEM((lines, LANES), F32),
            pltpu.VMEM((lines, channels), BF16),
            pltpu.VMEM((sequences, cols), jnp.int32),
            pltpu.VMEM((narrow, channels), BF16),
            pltpu.VMEM((narrow, channels), BF16),
            pltpu.VMEM((turns, sequences, right_lanes), BF16),
            pltpu.SemaphoreType.DMA,
            pltpu.SemaphoreType.DMA,
            pltpu.SemaphoreType.DMA,
            pltpu.SemaphoreType.DMA,
            pltpu.SemaphoreType.DMA((row_count,)),
        ],
        [hbm] * 4,
        (hbm, VMEM),
    )(*in_hbm([alignment.reshape(lines, channels), alignment_mask, outer_product_left.T, outer_product_right.T]))
    right = lax.all_to_all(right, "row", split_axis=0, concat_axis=0, tiled=True)
    right = right.reshape(row_count * sequences, right_lanes)
    places_of = [(row, col) for row in range(row_count) for col in range(col_count)]

    def route(to):
        return [(row * col_count + col, to(row, col)[0] * col_count + to(row, col)[1]) for row, col in places_of]

    def near(d, k):
        return route(lambda row, col: (row // turns * turns + (row + d) % turns, partner(col, k, col_count)))

    def exchange(values):
        given = []
        for d in range(1, turns):
            part = lax.dynamic_slice_in_dim(values, (x + d) % turns * rows, rows, 1)
            given.append(lax.ppermute(part, ("row", "col"), near(d, 0)))
        return given

    turned = route(lambda row, col: (turns * col + row % turns, row // turns))
    left = lax.ppermute(left, ("row", "col"), turned)
    across = [left] + [lax.ppermute(left, ("row", "col"), near(d, 0)) for d in range(1, turns)]
    blocks = {(d, 0): value for d, value in enumerate(across)}
    if col_count & (col_count - 1) == 0:
        bit = col_count // 2
        while bit:
            for d, k in list(blocks):
                blocks[d, k | bit] = lax.ppermute(blocks[d, k], ("row", "col"), near(0, bit))
            bit //= 2
    else:
        for d in range(turns):
            for k in range(1, col_count):
                blocks[d, k] = lax.ppermute(across[d], ("row", "col"), near(0, k))
    lefts = [blocks[d, k] for d in range(turns) for k in range(col_count)]
    pairs = exchange(pair_features)

    residue_float = residue_mask.astype(F32)
    row_mask = lax.dynamic_slice_in_dim(residue_float, r // turns * cols, cols)
    col_mask = lax.dynamic_slice_in_dim(residue_float, c * cols + x * rows, rows)
    pair_mask = (col_mask[:, None] * row_mask[None, :]).reshape(1, places)
    block, tri_rows = call(
        functools.partial(prepare_kernel, own), 16, [((places, width), BF16), ((4 * inner, width), BF16)], []
    )(triangle_proj, pair_features, *pairs)

    first, gated = call(
        functools.partial(outer_kernel, cols, rows, narrow, turns),
        24,
        [((places, width), BF16), ((owners, 2 * own, places), BF16)],
        [
            pltpu.VMEM((row_count * sequences, left_lanes), BF16),
            pltpu.VMEM((row_count * sequences // LANES, rows * narrow, LANES), F32),
            pltpu.VMEM((narrow * narrow, width), F32),
            pltpu.VMEM((pieces, cols // members * rows, narrow // pieces * LANES), BF16),
            pltpu.VMEM((2, narrow // pieces * LANES, members * width), BF16),
            pltpu.VMEM((places, width), F32),
            pltpu.VMEM((places, width), BF16),
        ],
    )(right, block, outer_proj, tri_rows, pair_mask, *lefts)

    first = first.reshape(rows, cols, width)
    firsts = exchange(first)
    first_t, gate = call(gate_kernel, 16, [((width, places), F32)] * 2, [pltpu.VMEM((places, width), F32)])(
        first, triangle_gate, *firsts
    )
    triangle = triangle_by_channel if by_channel else triangle_by_residue
    summed = triangle(row_count, col_count, rows, cols, gated)
    (out,) = call(tail_kernel, 16, [((places, width), BF16)], [pltpu.VMEM((inner, places), F32)])(
        first_t, gate, summed, triangle_out, transition_in, transition_out
    )
    return out.reshape(rows, cols, width)


def solution(mesh):
    placed = (
        P("row", "col", None),
        P("row", "col"),
        P(),
        P("row", "col", None),
    ) + (P(),) * 8

    def body(*args):
        return shards(mesh.shape["row"], mesh.shape["col"], *args)

    return jax.shard_map(body, mesh=mesh, in_specs=placed, out_specs=P("row", "col", None), check_vma=False)
```

time: 92.4 us -> 83 us (0.90)
  waiting for transfers between devices: 14.5 us -> 10.1 us
  starting transfers between devices: 43.1 us -> 39.4 us
  blocking collectives: 19.9 us -> 18.5 us
    all_to_all x1, waiting for transfers between devices: 11.1 us -> 1.67 us  [triangle_by_channel(): lax.all_to_all(summed, ('row', 'col'), split_axis=0, concat_axis=0, tiled...]
    ppermute x7 -> x9, waiting for transfers between devices: 3.41 us -> 8.43 us  [the longest x2 8.41 us: exchange(): given.append(lax.ppermute(part, ('row', 'col'), near(d, 0)))]
    ppermute x7 -> x9, starting transfers between devices: 31.8 us -> 28.1 us  [the longest x6 22.7 us: shards(): lax.ppermute(blocks[d, k], ('row', 'col'), near(0, bit))]
    all_to_all x1, blocking collectives: 19.9 us -> 18.5 us  [triangle_by_channel(): lax.all_to_all(gated, ('row', 'col'), split_axis=0, concat_axis=0, tiled=...]
  transfers between devices with their start and end apart: 10 -> 12, of which waited for: 4 -> 3; matrix products, arithmetic and copies ran while one was open for 0% -> 0% of each run, Pallas kernels for 2% -> 2%
where the time goes in v5:
time: 83 us; the launch traced here: 82.6 us
  starting transfers between devices  39.4 us (47%)
  blocking collectives  18.5 us (22%)
  Pallas kernels  13.4 us (16%)
  waiting for transfers between devices  10.1 us (12%)
  local copies, waits for them, and re-layouts  0.99 us (1%)
    ppermute x6, starting transfers between devices, shards(): lax.ppermute(blocks[d, k], ('row', 'col'), near(0, bit))  22.7 us
    all_to_all x1, blocking collectives, triangle_by_channel(): lax.all_to_all(gated, ('row', 'col'), split_axis=0, concat_axis=0, tiled=...  18.5 us
    ppermute x2, waiting for transfers between devices, exchange(): given.append(lax.ppermute(part, ('row', 'col'), near(d, 0)))  8.41 us
    all_to_all x1, starting transfers between devices, shards(): lax.all_to_all(right, 'row', split_axis=0, concat_axis=0, tiled=True)  7.42 us
    pallas_call x1, Pallas kernels, shards(): call(functools.partial(outer_kernel, cols, rows, narrow, turns), 24, [((p...  4.12 us
    ppermute x2, starting transfers between devices, exchange(): given.append(lax.ppermute(part, ('row', 'col'), near(d, 0)))  3.41 us
    all_to_all x1, starting transfers between devices, triangle_by_channel(): lax.all_to_all(summed, ('row', 'col'), split_axis=0, concat_axis=0, tiled...  3.15 us
    pallas_call x1, Pallas kernels, shards(): call(functools.partial(side_kernel, narrow), 16, [((row_count, sequences,...  3.09 us
  transfers between devices with their start and end apart: 12, of which 3 were waited for; matrix products, arithmetic and copies ran while one was open for 0% of the time, Pallas kernels for 2%

profile of v5, /device:TPU:0, one launch (start us, length us, event | category | flops | bytes accessed | tf_op | source)
XLA Modules:
  0.0 82.6 jit_solution(2753519248425370865)
XLA Ops:
  0.0 3.1 %shard_map.118 = (bf16[8,32,896]{2,1,0:T(8,128)(2,1)}, bf16[32,1664]{1,0:T(8,128)(2,1)S(1)}) custom-call(bf16[1536,256]{1,0:T(8,128)(2,1)} %bitcast.9, s32[32,48]{1,0:T(8,128)} %mask_hbm.1, bf16[32,256]{1,0:T(8,128)(2,1)} %bitcast.10, bf16[32,256]{1,0:T(8,128)(2,1)} %bitcast.11), custom_call_target="tpu_custom_call" | custom-call | tf_op jit(solution)/shard_map/pallas_call | solution.py:323
  3.1 0.0 copy-start
  3.1 7.4 %all-to-all-start = ((bf16[8,32,896]{2,1,0:T(8,128)(2,1)}), bf16[8,32,896]{2,1,0:T(8,128)(2,1)S(1)}, u32[]{:S(2)}, u32[]{:S(2)}) async-start(bf16[8,32,896]{2,1,0:T(8,128)(2,1)} %get-tuple-element.13), calls=%async_computation | async-start | bytes 917504 | tf_op jit(solution)/shard_map/all_to_all | solution.py:344
  10.5 0.7 collective-permute-start.1
  11.2 0.0 collective-permute-done.1.refs_0_
  11.2 2.1 %collective-permute-start.5 = (bf16[32,1664]{1,0:T(8,128)(2,1)S(1)}, bf16[32,1664]{1,0:T(8,128)(2,1)S(1)}, u32[]{:S(2)}, u32[]{:S(2)}) collective-permute-start(bf16[32,1664]{1,0:T(8,128)(2,1)S(1)} %collective-permute-done.1.refs_0_), channel_id=1, source_target_pairs={{0,4},{1,5},{2,6},{3,7},{4,0},{5,1},{6,2},{7,3},{8,12},{9,13},{10,... | collective-permute-start | bytes 319496 | tf_op jit(solution)/shard_map/ppermute | solution.py:363
  13.3 0.0 copy-start.4
  13.3 17.9 %collective-permute-start.3 = (bf16[32,1664]{1,0:T(8,128)(2,1)S(1)}, bf16[32,1664]{1,0:T(8,128)(2,1)S(1)}, u32[]{:S(2)}, u32[]{:S(2)}) collective-permute-start(bf16[32,1664]{1,0:T(8,128)(2,1)S(1)} %collective-permute-done.1.refs_0_), channel_id=1, source_target_pairs={{0,2},{1,3},{2,0},{3,1},{4,6},{5,7},{6,4},{7,5},{8,10},{9,11},{10,... | collective-permute-start | bytes 319496 | tf_op jit(solution)/shard_map/ppermute | solution.py:369
  31.2 0.0 collective-permute-done.5.refs_4_
  31.2 3.7 %collective-permute-start.7 = (bf16[32,1664]{1,0:T(8,128)(2,1)S(1)}, bf16[32,1664]{1,0:T(8,128)(2,1)S(1)}, u32[]{:S(2)}, u32[]{:S(2)}) collective-permute-start(bf16[32,1664]{1,0:T(8,128)(2,1)S(1)} %collective-permute-done.5.refs_4_), channel_id=1, source_target_pairs={{0,2},{1,3},{2,0},{3,1},{4,6},{5,7},{6,4},{7,5},{8,10},{9,11},{10,... | collective-permute-start | bytes 319496 | tf_op jit(solution)/shard_map/ppermute | solution.py:369
  34.9 0.0 copy-done
  35.0 1.6 %collective-permute-start = (bf16[24,24,128]{2,1,0:T(8,128)(2,1)S(1)}, bf16[24,24,128]{2,1,0:T(8,128)(2,1)S(1)}, u32[]{:S(2)}, u32[]{:S(2)}) collective-permute-start(bf16[24,24,128]{2,1,0:T(8,128)(2,1)S(1)} %constant_dynamic-slice_fusion.1), channel_id=1, source_target_pairs={{0,4},{1,5},{2,6},{3,7},{4,0},{5,1},{6,2},{7,3},{8,12},{9,13},{10,... | collective-permute-start | bytes 442376 | tf_op jit(solution)/shard_map/ppermute | solution.py:358
  36.5 0.0 copy-start.7
  36.5 0.7 copy-done.7
  37.2 0.1 dynamic_slice.14
  37.3 0.1 dynamic_slice.13
  37.4 0.0 collective-permute-start.2
  37.4 0.5 collective-permute-start.6
  37.9 0.0 collective-permute-done.3.refs_2_
  37.9 0.0 collective-permute-start.4
  37.9 0.0 collective-permute-done.7.refs_6_
  37.9 0.5 collective-permute-start.8
  38.4 0.1 broadcast_multiply_fusion
  38.5 0.1 mul.43.pair_mask_ref
  38.5 0.0 copy-start.1
  38.6 1.6 %collective-permute-done.refs_0_ = bf16[24,24,128]{2,1,0:T(8,128)(2,1)S(1)} collective-permute-done((bf16[24,24,128]{2,1,0:T(8,128)(2,1)S(1)}, bf16[24,24,128]{2,1,0:T(8,128)(2,1)S(1)}, u32[]{:S(2)}, u32[]{:S(2)}) %collective-permute-start) | collective-permute-done | bytes 147488 | tf_op jit(solution)/shard_map/ppermute | solution.py:358
  40.2 0.0 copy-done.4
  40.2 0.4 shard_map.119
  40.5 0.0 collective-permute-done.2.refs_1_
  40.5 0.0 collective-permute-done.6.refs_5_
  40.5 0.0 collective-permute-done.4.refs_3_
  40.6 0.0 collective-permute-done.8.refs_7_
  40.6 0.0 all-to-all-done
  40.6 0.0 copy-done.1
  40.6 4.1 %shard_map.120 = (bf16[1152,128]{1,0:T(8,128)(2,1)S(1)}, bf16[32,8,1152]{2,1,0:T(8,128)(2,1)S(1)}) custom-call(bf16[256,896]{1,0:T(8,128)(2,1)S(1)} %bitcast.6, bf16[1152,128]{1,0:T(8,128)(2,1)S(1)} %get-tuple-element.14.pair_ref, bf16[1024,128]{1,0:T(8,128)(2,1)S(1)} %copy-done.1, bf16[512,128]{1,0:T(8,128)(2,1)S(1)} %get-tuple-element.15.tri_ref, ...), custom_call_target="tpu_custom_call" | custom-call | tf_op jit(solution)/shard_map/pallas_call | solution.py:386
  44.7 18.5 %all_to_all.15.given_ref = bf16[32,8,1152]{2,1,0:T(8,128)(2,1)S(1)} all-to-all(bf16[32,8,1152]{2,1,0:T(8,128)(2,1)S(1)} %get-tuple-element.20), channel_id=1, replica_groups=mesh['row'=8,'col'=4] {'row','col'}, dimensions={0} | all-to-all | bytes 1179648 | tf_op jit(solution)/shard_map/all_to_all | solution.py:248
  63.2 2.9 %shard_map.122 = bf16[32,4,1152]{2,1,0:T(4,128)(2,1)} custom-call(bf16[32,8,1152]{2,1,0:T(8,128)(2,1)S(1)} %all_to_all.15.given_ref), custom_call_target="tpu_custom_call" | custom-call | tf_op jit(solution)/shard_map/pallas_call | solution.py:251
  66.2 3.1 %all-to-all-start.2 = ((bf16[32,4,1152]{2,1,0:T(4,128)(2,1)}), bf16[32,4,1152]{2,1,0:T(4,128)(2,1)S(1)}, u32[]{:S(2)}, u32[]{:S(2)}) async-start(bf16[32,4,1152]{2,1,0:T(4,128)(2,1)} %shard_map.122), calls=%async_computation.2 | async-start | bytes 589824 | tf_op jit(solution)/shard_map/all_to_all | solution.py:257
  69.3 0.0 copy-start.6
  69.4 0.0 copy-start.2
  69.4 0.0 copy-start.3
  69.4 0.0 copy-start.5
  69.4 1.8 %collective-permute-start.9 = (bf16[24,24,128]{2,1,0:T(8,128)(2,1)S(1)}, bf16[24,24,128]{2,1,0:T(8,128)(2,1)S(1)}, u32[]{:S(2)}, u32[]{:S(2)}) collective-permute-start(bf16[24,24,128]{2,1,0:T(8,128)(2,1)S(1)} %constant_dynamic-slice_fusion), channel_id=1, source_target_pairs={{0,4},{1,5},{2,6},{3,7},{4,0},{5,1},{6,2},{7,3},{8,12},{9,13},{10,... | collective-permute-start | bytes 442376 | tf_op jit(solution)/shard_map/ppermute | solution.py:358
  71.2 6.8 %collective-permute-done.9.refs_0_ = bf16[24,24,128]{2,1,0:T(8,128)(2,1)S(1)} collective-permute-done((bf16[24,24,128]{2,1,0:T(8,128)(2,1)S(1)}, bf16[24,24,128]{2,1,0:T(8,128)(2,1)S(1)}, u32[]{:S(2)}, u32[]{:S(2)}) %collective-permute-start.9) | collective-permute-done | bytes 147488 | tf_op jit(solution)/shard_map/ppermute | solution.py:358
  78.1 0.0 copy-done.6
  78.1 1.0 %shard_map.121 = (f32[128,1152]{1,0:T(8,128)S(1)}, f32[128,1152]{1,0:T(8,128)S(1)}) custom-call(bf16[24,48,128]{2,1,0:T(8,128)(2,1)S(1)} %bitcast.8, bf16[128,128]{1,0:T(8,128)(2,1)S(1)} %copy-done.6, bf16[24,24,128]{2,1,0:T(8,128)(2,1)S(1)} %collective-permute-done.9.refs_0_), custom_call_target="tpu_custom_call" | custom-call | tf_op jit(solution)/shard_map/pallas_call | solution.py:403
  79.1 1.7 %all-to-all-done.2.summed_ref = bf16[32,4,1152]{2,1,0:T(4,128)(2,1)S(1)} async-done(((bf16[32,4,1152]{2,1,0:T(4,128)(2,1)}), bf16[32,4,1152]{2,1,0:T(4,128)(2,1)S(1)}, u32[]{:S(2)}, u32[]{:S(2)}) %all-to-all-start.2) | async-done | bytes 294944 | tf_op jit(solution)/shard_map/all_to_all | solution.py:257
  80.7 0.0 copy-done.2
  80.7 0.0 copy-done.3
  80.7 0.0 copy-done.5
  80.7 1.9 %shard_map.123 = bf16[1152,128]{1,0:T(8,128)(2,1)} custom-call(f32[128,1152]{1,0:T(8,128)S(1)} %get-tuple-element.18.first_ref, f32[128,1152]{1,0:T(8,128)S(1)} %get-tuple-element.19.gated_ref, bf16[32,4,1152]{2,1,0:T(4,128)(2,1)S(1)} %all-to-all-done.2.summed_ref, bf16[128,128]{1,0:T(8,128)(2,1)S(1)} %copy-done.5, bf16[128,512]{1,0:T(8,128)(2,1)S(1)} %copy-done.2, ...), custom_call_target="tpu_custom_call" | custom-call | tf_op jit(solution)/shard_map/pallas_call | solution.py:408
  (3 shorter events, 0.0 us)
Async XLA Ops:
  3.1 31.8 %copy-start = (bf16[24,48,128]{2,1,0:T(8,128)(2,1)S(1)}, bf16[24,48,128]{2,1,0:T(8,128)(2,1)}, u32[]{:S(2)}) copy-start(bf16[24,48,128]{2,1,0:T(8,128)(2,1)} %pair_ref.1) | copy-start | bytes 884740
  3.1 37.5 %all-to-all-start = ((bf16[8,32,896]{2,1,0:T(8,128)(2,1)}), bf16[8,32,896]{2,1,0:T(8,128)(2,1)S(1)}, u32[]{:S(2)}, u32[]{:S(2)}) async-start(bf16[8,32,896]{2,1,0:T(8,128)(2,1)} %get-tuple-element.13), calls=%async_computation | async-start | bytes 917504 | tf_op jit(solution)/shard_map/all_to_all | solution.py:344
  10.5 0.7 collective-permute-start.1
  11.2 20.0 %collective-permute-start.5 = (bf16[32,1664]{1,0:T(8,128)(2,1)S(1)}, bf16[32,1664]{1,0:T(8,128)(2,1)S(1)}, u32[]{:S(2)}, u32[]{:S(2)}) collective-permute-start(bf16[32,1664]{1,0:T(8,128)(2,1)S(1)} %collective-permute-done.1.refs_0_), channel_id=1, source_target_pairs={{0,4},{1,5},{2,6},{3,7},{4,0},{5,1},{6,2},{7,3},{8,12},{9,13},{10,... | collective-permute-start | bytes 319496 | tf_op jit(solution)/shard_map/ppermute | solution.py:363
  13.3 26.9 %copy-start.4 = (bf16[128,512]{1,0:T(8,128)(2,1)S(1)}, bf16[128,512]{1,0:T(8,128)(2,1)}, u32[]{:S(2)}) copy-start(bf16[128,512]{1,0:T(8,128)(2,1)} %tri_ref.1) | copy-start | bytes 393220
  13.3 24.6 %collective-permute-start.3 = (bf16[32,1664]{1,0:T(8,128)(2,1)S(1)}, bf16[32,1664]{1,0:T(8,128)(2,1)S(1)}, u32[]{:S(2)}, u32[]{:S(2)}) collective-permute-start(bf16[32,1664]{1,0:T(8,128)(2,1)S(1)} %collective-permute-done.1.refs_0_), channel_id=1, source_target_pairs={{0,2},{1,3},{2,0},{3,1},{4,6},{5,7},{6,4},{7,5},{8,10},{9,11},{10,... | collective-permute-start | bytes 319496 | tf_op jit(solution)/shard_map/ppermute | solution.py:369
  31.2 6.7 %collective-permute-start.7 = (bf16[32,1664]{1,0:T(8,128)(2,1)S(1)}, bf16[32,1664]{1,0:T(8,128)(2,1)S(1)}, u32[]{:S(2)}, u32[]{:S(2)}) collective-permute-start(bf16[32,1664]{1,0:T(8,128)(2,1)S(1)} %collective-permute-done.5.refs_4_), channel_id=1, source_target_pairs={{0,2},{1,3},{2,0},{3,1},{4,6},{5,7},{6,4},{7,5},{8,10},{9,11},{10,... | collective-permute-start | bytes 319496 | tf_op jit(solution)/shard_map/ppermute | solution.py:369
  35.0 5.2 %collective-permute-start = (bf16[24,24,128]{2,1,0:T(8,128)(2,1)S(1)}, bf16[24,24,128]{2,1,0:T(8,128)(2,1)S(1)}, u32[]{:S(2)}, u32[]{:S(2)}) collective-permute-start(bf16[24,24,128]{2,1,0:T(8,128)(2,1)S(1)} %constant_dynamic-slice_fusion.1), channel_id=1, source_target_pairs={{0,4},{1,5},{2,6},{3,7},{4,0},{5,1},{6,2},{7,3},{8,12},{9,13},{10,... | collective-permute-start | bytes 442376 | tf_op jit(solution)/shard_map/ppermute | solution.py:358
  36.5 0.7 copy-start.7
  37.4 3.2 %collective-permute-start.2 = (bf16[32,1664]{1,0:T(8,128)(2,1)S(1)}, bf16[32,1664]{1,0:T(8,128)(2,1)S(1)}, u32[]{:S(2)}, u32[]{:S(2)}) collective-permute-start(bf16[32,1664]{1,0:T(8,128)(2,1)S(1)} %collective-permute-done.1.refs_0_), channel_id=1, source_target_pairs={{0,1},{1,0},{2,3},{3,2},{4,5},{5,4},{6,7},{7,6},{8,9},{9,8},{10,11... | collective-permute-start | bytes 319496 | tf_op jit(solution)/shard_map/ppermute | solution.py:369
  37.4 3.2 %collective-permute-start.6 = (bf16[32,1664]{1,0:T(8,128)(2,1)S(1)}, bf16[32,1664]{1,0:T(8,128)(2,1)S(1)}, u32[]{:S(2)}, u32[]{:S(2)}) collective-permute-start(bf16[32,1664]{1,0:T(8,128)(2,1)S(1)} %collective-permute-done.5.refs_4_), channel_id=1, source_target_pairs={{0,1},{1,0},{2,3},{3,2},{4,5},{5,4},{6,7},{7,6},{8,9},{9,8},{10,11... | collective-permute-start | bytes 319496 | tf_op jit(solution)/shard_map/ppermute | solution.py:369
  37.9 2.7 %collective-permute-start.4 = (bf16[32,1664]{1,0:T(8,128)(2,1)S(1)}, bf16[32,1664]{1,0:T(8,128)(2,1)S(1)}, u32[]{:S(2)}, u32[]{:S(2)}) collective-permute-start(bf16[32,1664]{1,0:T(8,128)(2,1)S(1)} %collective-permute-done.3.refs_2_), channel_id=1, source_target_pairs={{0,1},{1,0},{2,3},{3,2},{4,5},{5,4},{6,7},{7,6},{8,9},{9,8},{10,11... | collective-permute-start | bytes 319496 | tf_op jit(solution)/shard_map/ppermute | solution.py:369
  37.9 2.6 %collective-permute-start.8 = (bf16[32,1664]{1,0:T(8,128)(2,1)S(1)}, bf16[32,1664]{1,0:T(8,128)(2,1)S(1)}, u32[]{:S(2)}, u32[]{:S(2)}) collective-permute-start(bf16[32,1664]{1,0:T(8,128)(2,1)S(1)} %collective-permute-done.7.refs_6_), channel_id=1, source_target_pairs={{0,1},{1,0},{2,3},{3,2},{4,5},{5,4},{6,7},{7,6},{8,9},{9,8},{10,11... | collective-permute-start | bytes 319496 | tf_op jit(solution)/shard_map/ppermute | solution.py:369
  38.5 2.0 %copy-start.1 = (bf16[1024,128]{1,0:T(8,128)(2,1)S(1)}, bf16[1024,128]{1,0:T(8,128)(2,1)}, u32[]{:S(2)}) copy-start(bf16[1024,128]{1,0:T(8,128)(2,1)} %proj_ref.1) | copy-start | bytes 786436
  66.2 14.6 %all-to-all-start.2 = ((bf16[32,4,1152]{2,1,0:T(4,128)(2,1)}), bf16[32,4,1152]{2,1,0:T(4,128)(2,1)S(1)}, u32[]{:S(2)}, u32[]{:S(2)}) async-start(bf16[32,4,1152]{2,1,0:T(4,128)(2,1)} %shard_map.122), calls=%async_computation.2 | async-start | bytes 589824 | tf_op jit(solution)/shard_map/all_to_all | solution.py:257
  69.3 8.7 %copy-start.6 = (bf16[128,128]{1,0:T(8,128)(2,1)S(1)}, bf16[128,128]{1,0:T(8,128)(2,1)}, u32[]{:S(2)}) copy-start(bf16[128,128]{1,0:T(8,128)(2,1)} %gate_w_ref.1) | copy-start | bytes 98308
  69.4 11.4 %copy-start.2 = (bf16[128,512]{1,0:T(8,128)(2,1)S(1)}, bf16[128,512]{1,0:T(8,128)(2,1)}, u32[]{:S(2)}) copy-start(bf16[128,512]{1,0:T(8,128)(2,1)} %in_ref.1) | copy-start | bytes 393220
  69.4 11.3 %copy-start.3 = (bf16[512,128]{1,0:T(8,128)(2,1)S(1)}, bf16[512,128]{1,0:T(8,128)(2,1)}, u32[]{:S(2)}) copy-start(bf16[512,128]{1,0:T(8,128)(2,1)} %back_ref.1) | copy-start | bytes 393220
  69.4 11.3 %copy-start.5 = (bf16[128,128]{1,0:T(8,128)(2,1)S(1)}, bf16[128,128]{1,0:T(8,128)(2,1)}, u32[]{:S(2)}) copy-start(bf16[128,128]{1,0:T(8,128)(2,1)} %out_w_ref.1) | copy-start | bytes 98308
  69.4 8.6 %collective-permute-start.9 = (bf16[24,24,128]{2,1,0:T(8,128)(2,1)S(1)}, bf16[24,24,128]{2,1,0:T(8,128)(2,1)S(1)}, u32[]{:S(2)}, u32[]{:S(2)}) collective-permute-start(bf16[24,24,128]{2,1,0:T(8,128)(2,1)S(1)} %constant_dynamic-slice_fusion), channel_id=1, source_target_pairs={{0,4},{1,5},{2,6},{3,7},{4,0},{5,1},{6,2},{7,3},{8,12},{9,13},{10,... | collective-permute-start | bytes 442376 | tf_op jit(solution)/shard_map/ppermute | solution.py:358

commit v6 on v5

--- a/solution.py
+++ b/solution.py
@@ -112,11 +112,20 @@
         copy.wait()
 
 
-def prepare_kernel(own, tri_ref, pair_ref, *refs):
-    *given_refs, block_ref, tri_rows_ref = refs
+def prepare_kernel(own, residue_ref, tri_ref, pair_ref, *refs):
+    *given_refs, block_ref, tri_rows_ref, pair_mask_ref = refs
     rows, cols, _ = pair_ref.shape
     parts = cols // rows
-    x = lax.rem(lax.axis_index("row"), parts)
+    row = lax.axis_index("row")
+    x = lax.rem(row, parts)
+    present = residue_ref[...].astype(BF16)
+    residue = iota((present.shape[1], 1), 0)
+    place = iota((1, pair_mask_ref.shape[1]), 1)
+    tall = lax.div(row, parts) * cols + place % cols
+    short = lax.axis_index("col") * cols + x * rows + place // cols
+    pair_mask_ref[...] = matmul(present, (residue == tall).astype(BF16)) * matmul(
+        present, (residue == short).astype(BF16)
+    )
     for i in range(rows):
         at = pl.ds(pl.multiple_of((x * rows + i) * rows, 8), rows)
         block_ref[at, :] = pair_ref[i, pl.ds(pl.multiple_of(x * rows, 8), rows), :]
@@ -133,7 +142,7 @@
 
 
 def outer_kernel(tall, short, narrow, parts, right_ref, pair_ref, proj_ref, tri_ref, pair_mask_ref, *refs):
-    *left_refs, first_ref, tri_out_ref, left, right_t, proj, stacked, spread, moved, normed = refs
+    *left_refs, first_ref, tri_out_ref, left, right_t, proj, stacked, spread, moved, rounded = refs
     sources = len(left_refs) // parts
     sequences = left_refs[0].shape[0]
     x, column = lax.rem(lax.axis_index("row"), parts), lax.axis_index("col")
@@ -159,16 +168,23 @@
             each = [right_t.at[p][pl.ds(n * step + d, short, stride=narrow), :] for d in range(step)]
             some.append(jnp.concatenate(each, axis=0).astype(BF16))
         block = matmul(jnp.concatenate(some, axis=1), left[:, :left_width])
+        for e in range(0, step, 2):
+            lanes = slice(e // 2 * LANES, (e // 2 + 1) * LANES)
+            for g in range(0, groups, 2):
+                pairs = []
+                for d in (e, e + 1):
+                    two = [
+                        block[d * short : (d + 1) * short, (g + m) * LANES : (g + m + 1) * LANES] for m in range(2)
+                    ]
+                    pairs.append(jnp.concatenate(two, axis=0).astype(BF16))
+                for side in range(2):
+                    half = slice(side * LANES // 2, (side + 1) * LANES // 2)
+                    at = side * groups * short + g * short
+                    stacked[n, at : at + 2 * short, lanes] = jnp.concatenate([v[:, half] for v in pairs], axis=1)
         for d in range(step):
-            lanes = slice(d * LANES, (d + 1) * LANES)
-            for g in range(0, groups, 2):
-                two = [
-                    block[d * short : (d + 1) * short, (g + m) * LANES : (g + m + 1) * LANES] for m in range(2)
-                ]
-                stacked[n, g * short : (g + 2) * short, lanes] = jnp.concatenate(two, axis=0).astype(BF16)
             part = proj[pl.ds(n * step + d, narrow, stride=narrow), :].astype(BF16)
-            for m in range(members):
-                start = d * LANES + m * narrow
+            for m in range(members // 2):
+                start = d * LANES // 2 + m * narrow
                 spread[n % 2, start : start + narrow, m * width : (m + 1) * width] = part
         term = matmul(stacked[n], spread[n % 2])
         total = term if total is None else total + term
@@ -178,15 +194,17 @@
         for m in range(members):
             i = g * members + m
             at = slice(i * short, (i + 1) * short)
-            part = total[g * short : (g + 1) * short, m * width : (m + 1) * width]
+            side, n = m // (members // 2), m % (members // 2)
+            start = (side * groups + g) * short
+            part = total[start : start + short, n * width : (n + 1) * width]
             moved[at, :] = part * scale[:, i : i + 1] + pair_ref[at, :].astype(F32)
     for j in range(short):
         first = moved[pl.ds(j, tall, stride=short), :].astype(BF16)
         first_ref[j * tall : (j + 1) * tall, :] = first
-        normed[j * tall : (j + 1) * tall, :] = normalize(first.astype(F32)).astype(BF16)
+        rounded[j * tall : (j + 1) * tall, :] = first.astype(F32)
     devices, pair, _ = tri_out_ref.shape
     half = devices * pair
-    projections = matmul(tri_ref[...], normed[...], NT)
+    projections = matmul(tri_ref[...], normalize(rounded[...].T, 0).astype(BF16))
     gated = jax.nn.sigmoid(projections[:half]) * projections[half:] * pair_mask_ref[...]
     gated = gated.astype(BF16)
     for d in range(devices):
@@ -279,9 +297,9 @@
         for d, given_ref in enumerate(given_refs, 1):
             at = pl.ds(lax.rem(x - d + parts, parts) * rows + j, rows, stride=cols)
             home[at, :] = given_ref[j].astype(F32)
-    first = home[...]
-    first_t_ref[...] = first.T
-    gated_ref[...] = jax.nn.sigmoid(matmul(gate_w_ref[...].T, normalize(first).astype(BF16), NT))
+    first_t = home[...].T
+    first_t_ref[...] = first_t
+    gated_ref[...] = jax.nn.sigmoid(matmul(gate_w_ref[...].T, normalize(first_t, 0).astype(BF16)))
 
 
 def tail_kernel(first_ref, gated_ref, summed_ref, out_w_ref, in_ref, back_ref, out_ref, summed):
@@ -308,7 +326,7 @@
     devices = row_count * col_count
     turns = cols // rows
     places = rows * cols
-    r, c = lax.axis_index("row"), lax.axis_index("col")
+    r = lax.axis_index("row")
     by_channel = inner % devices == 0
     owners = devices if by_channel else 1
     own = inner // owners
@@ -316,7 +334,7 @@
     right_lanes = rows * narrow + LANES
     left_lanes = cols * narrow + LANES
     lines = sequences * cols
-    pieces = 4 if narrow % 4 == 0 else 1
+    pieces = 8 if narrow % 16 == 0 else 1
     x = r % turns
 
     hbm = pl.BlockSpec(memory_space=pltpu.HBM)
@@ -375,13 +393,12 @@
     lefts = [blocks[d, k] for d in range(turns) for k in range(col_count)]
     pairs = exchange(pair_features)
 
-    residue_float = residue_mask.astype(F32)
-    row_mask = lax.dynamic_slice_in_dim(residue_float, r // turns * cols, cols)
-    col_mask = lax.dynamic_slice_in_dim(residue_float, c * cols + x * rows, rows)
-    pair_mask = (col_mask[:, None] * row_mask[None, :]).reshape(1, places)
-    block, tri_rows = call(
-        functools.partial(prepare_kernel, own), 16, [((places, width), BF16), ((4 * inner, width), BF16)], []
-    )(triangle_proj, pair_features, *pairs)
+    block, tri_rows, pair_mask = call(
+        functools.partial(prepare_kernel, own),
+        16,
+        [((places, width), BF16), ((4 * inner, width), BF16), ((1, places), F32)],
+        [],
+    )(residue_mask.reshape(1, -1), triangle_proj, pair_features, *pairs)
 
     first, gated = call(
         functools.partial(outer_kernel, cols, rows, narrow, turns),
@@ -391,10 +408,10 @@
             pltpu.VMEM((row_count * sequences, left_lanes), BF16),
             pltpu.VMEM((row_count * sequences // LANES, rows * narrow, LANES), F32),
             pltpu.VMEM((narrow * narrow, width), F32),
-            pltpu.VMEM((pieces, cols // members * rows, narrow // pieces * LANES), BF16),
-            pltpu.VMEM((2, narrow // pieces * LANES, members * width), BF16),
+            pltpu.VMEM((pieces, cols // members * rows * 2, narrow // pieces * LANES // 2), BF16),
+            pltpu.VMEM((2, narrow // pieces * LANES // 2, members // 2 * width), BF16),
             pltpu.VMEM((places, width), F32),
-            pltpu.VMEM((places, width), BF16),
+            pltpu.VMEM((places, width), F32),
         ],
     )(right, block, outer_proj, tri_rows, pair_mask, *lefts)
 

time: 83 us -> 83 us (level)
  waiting for transfers between devices: 10.1 us -> 11.9 us
    ppermute x2, waiting for transfers between devices: 8.41 us -> 9.37 us  [exchange(): given.append(lax.ppermute(part, ('row', 'col'), near(d, 0)))]
  transfers between devices with their start and end apart: 12 -> 12, of which waited for: 3 -> 4; matrix products, arithmetic and copies ran while one was open for 0% -> 0% of each run, Pallas kernels for 2% -> 1%
where the time goes in v6:
time: 83 us; the launch traced here: 82.6 us
  starting transfers between devices  38.9 us (47%)
  blocking collectives  18.5 us (22%)
  Pallas kernels  12.7 us (15%)
  waiting for transfers between devices  11.9 us (14%)
    ppermute x6, starting transfers between devices, shards(): lax.ppermute(blocks[d, k], ('row', 'col'), near(0, bit))  22.2 us
    all_to_all x1, blocking collectives, triangle_by_channel(): lax.all_to_all(gated, ('row', 'col'), split_axis=0, concat_axis=0, tiled=...  18.5 us
    ppermute x2, waiting for transfers between devices, exchange(): given.append(lax.ppermute(part, ('row', 'col'), near(d, 0)))  9.37 us
    all_to_all x1, starting transfers between devices, shards(): lax.all_to_all(right, 'row', split_axis=0, concat_axis=0, tiled=True)  7.42 us
    pallas_call x1, Pallas kernels, shards(): call(functools.partial(outer_kernel, cols, rows, narrow, turns), 24, [((p...  3.59 us
    ppermute x2, starting transfers between devices, exchange(): given.append(lax.ppermute(part, ('row', 'col'), near(d, 0)))  3.41 us
    all_to_all x1, starting transfers between devices, triangle_by_channel(): lax.all_to_all(summed, ('row', 'col'), split_axis=0, concat_axis=0, tiled...  3.15 us
    pallas_call x1, Pallas kernels, shards(): call(functools.partial(side_kernel, narrow), 16, [((row_count, sequences,...  3.09 us
  transfers between devices with their start and end apart: 12, of which 4 were waited for; matrix products, arithmetic and copies ran while one was open for 0% of the time, Pallas kernels for 1%

profile of v6, /device:TPU:0, one launch (start us, length us, event | category | flops | bytes accessed | tf_op | source)
XLA Modules:
  0.0 82.6 jit_solution(12706559785591030628)
XLA Ops:
  0.0 3.1 %shard_map.118 = (bf16[8,32,896]{2,1,0:T(8,128)(2,1)}, bf16[32,1664]{1,0:T(8,128)(2,1)S(1)}) custom-call(bf16[1536,256]{1,0:T(8,128)(2,1)} %bitcast.11, s32[32,48]{1,0:T(8,128)} %mask_hbm.1, bf16[32,256]{1,0:T(8,128)(2,1)} %bitcast.12, bf16[32,256]{1,0:T(8,128)(2,1)} %bitcast.13), custom_call_target="tpu_custom_call" | custom-call | tf_op jit(solution)/shard_map/pallas_call | solution.py:341
  3.1 0.0 copy-start
  3.1 7.4 %all-to-all-start = ((bf16[8,32,896]{2,1,0:T(8,128)(2,1)}), bf16[8,32,896]{2,1,0:T(8,128)(2,1)S(1)}, u32[]{:S(2)}, u32[]{:S(2)}) async-start(bf16[8,32,896]{2,1,0:T(8,128)(2,1)} %get-tuple-element.14), calls=%async_computation | async-start | bytes 917504 | tf_op jit(solution)/shard_map/all_to_all | solution.py:362
  10.5 0.7 collective-permute-start.1
  11.2 0.0 collective-permute-done.1.refs_0_
  11.2 2.1 %collective-permute-start.5 = (bf16[32,1664]{1,0:T(8,128)(2,1)S(1)}, bf16[32,1664]{1,0:T(8,128)(2,1)S(1)}, u32[]{:S(2)}, u32[]{:S(2)}) collective-permute-start(bf16[32,1664]{1,0:T(8,128)(2,1)S(1)} %collective-permute-done.1.refs_0_), channel_id=1, source_target_pairs={{0,4},{1,5},{2,6},{3,7},{4,0},{5,1},{6,2},{7,3},{8,12},{9,13},{10,... | collective-permute-start | bytes 319496 | tf_op jit(solution)/shard_map/ppermute | solution.py:381
  13.3 0.0 copy-start.4
  13.3 17.9 %collective-permute-start.3 = (bf16[32,1664]{1,0:T(8,128)(2,1)S(1)}, bf16[32,1664]{1,0:T(8,128)(2,1)S(1)}, u32[]{:S(2)}, u32[]{:S(2)}) collective-permute-start(bf16[32,1664]{1,0:T(8,128)(2,1)S(1)} %collective-permute-done.1.refs_0_), channel_id=1, source_target_pairs={{0,2},{1,3},{2,0},{3,1},{4,6},{5,7},{6,4},{7,5},{8,10},{9,11},{10,... | collective-permute-start | bytes 319496 | tf_op jit(solution)/shard_map/ppermute | solution.py:387
  31.2 0.0 collective-permute-done.5.refs_4_
  31.2 3.7 %collective-permute-start.7 = (bf16[32,1664]{1,0:T(8,128)(2,1)S(1)}, bf16[32,1664]{1,0:T(8,128)(2,1)S(1)}, u32[]{:S(2)}, u32[]{:S(2)}) collective-permute-start(bf16[32,1664]{1,0:T(8,128)(2,1)S(1)} %collective-permute-done.5.refs_4_), channel_id=1, source_target_pairs={{0,2},{1,3},{2,0},{3,1},{4,6},{5,7},{6,4},{7,5},{8,10},{9,11},{10,... | collective-permute-start | bytes 319496 | tf_op jit(solution)/shard_map/ppermute | solution.py:387
  34.9 0.0 copy-done
  35.0 0.0 copy-start.7
  35.0 1.6 %collective-permute-start = (bf16[24,24,128]{2,1,0:T(8,128)(2,1)S(1)}, bf16[24,24,128]{2,1,0:T(8,128)(2,1)S(1)}, u32[]{:S(2)}, u32[]{:S(2)}) collective-permute-start(bf16[24,24,128]{2,1,0:T(8,128)(2,1)S(1)} %constant_dynamic-slice_fusion.1), channel_id=1, source_target_pairs={{0,4},{1,5},{2,6},{3,7},{4,0},{5,1},{6,2},{7,3},{8,12},{9,13},{10,... | collective-permute-start | bytes 442376 | tf_op jit(solution)/shard_map/ppermute | solution.py:376
  36.5 0.0 collective-permute-start.2
  36.6 0.5 collective-permute-start.6
  37.1 0.0 collective-permute-done.3.refs_2_
  37.1 0.0 collective-permute-start.4
  37.1 0.6 collective-permute-done.7.refs_6_
  37.6 0.0 collective-permute-start.8
  37.6 2.6 %collective-permute-done.refs_0_ = bf16[24,24,128]{2,1,0:T(8,128)(2,1)S(1)} collective-permute-done((bf16[24,24,128]{2,1,0:T(8,128)(2,1)S(1)}, bf16[24,24,128]{2,1,0:T(8,128)(2,1)S(1)}, u32[]{:S(2)}, u32[]{:S(2)}) %collective-permute-start) | collective-permute-done | bytes 147488 | tf_op jit(solution)/shard_map/ppermute | solution.py:376
  40.2 0.0 copy-done.4
  40.2 0.0 copy-done.7
  40.2 0.0 copy-start.1
  40.2 0.5 shard_map.119
  40.7 0.0 collective-permute-done.2.refs_1_
  40.7 0.0 collective-permute-done.6.refs_5_
  40.7 0.0 collective-permute-done.4.refs_3_
  40.7 0.0 collective-permute-done.8.refs_7_
  40.7 0.0 all-to-all-done
  40.7 0.4 copy-done.1
  41.1 3.6 %shard_map.120 = (bf16[1152,128]{1,0:T(8,128)(2,1)S(1)}, bf16[32,8,1152]{2,1,0:T(8,128)(2,1)S(1)}) custom-call(bf16[256,896]{1,0:T(8,128)(2,1)S(1)} %bitcast.7, bf16[1152,128]{1,0:T(8,128)(2,1)S(1)} %get-tuple-element.15.pair_ref, bf16[1024,128]{1,0:T(8,128)(2,1)S(1)} %copy-done.1, bf16[512,128]{1,0:T(8,128)(2,1)S(1)} %get-tuple-element.16.tri_ref, ...), custom_call_target="tpu_custom_call" | custom-call | tf_op jit(solution)/shard_map/pallas_call | solution.py:403
  44.7 18.5 %all_to_all.15.given_ref = bf16[32,8,1152]{2,1,0:T(8,128)(2,1)S(1)} all-to-all(bf16[32,8,1152]{2,1,0:T(8,128)(2,1)S(1)} %get-tuple-element.22), channel_id=1, replica_groups=mesh['row'=8,'col'=4] {'row','col'}, dimensions={0} | all-to-all | bytes 1179648 | tf_op jit(solution)/shard_map/all_to_all | solution.py:266
  63.3 2.9 %shard_map.122 = bf16[32,4,1152]{2,1,0:T(4,128)(2,1)} custom-call(bf16[32,8,1152]{2,1,0:T(8,128)(2,1)S(1)} %all_to_all.15.given_ref), custom_call_target="tpu_custom_call" | custom-call | tf_op jit(solution)/shard_map/pallas_call | solution.py:269
  66.2 3.2 %all-to-all-start.2 = ((bf16[32,4,1152]{2,1,0:T(4,128)(2,1)}), bf16[32,4,1152]{2,1,0:T(4,128)(2,1)S(1)}, u32[]{:S(2)}, u32[]{:S(2)}) async-start(bf16[32,4,1152]{2,1,0:T(4,128)(2,1)} %shard_map.122), calls=%async_computation.2 | async-start | bytes 589824 | tf_op jit(solution)/shard_map/all_to_all | solution.py:275
  69.4 0.0 copy-start.6
  69.4 0.0 copy-start.2
  69.4 0.0 copy-start.3
  69.4 0.0 copy-start.5
  69.4 1.8 %collective-permute-start.9 = (bf16[24,24,128]{2,1,0:T(8,128)(2,1)S(1)}, bf16[24,24,128]{2,1,0:T(8,128)(2,1)S(1)}, u32[]{:S(2)}, u32[]{:S(2)}) collective-permute-start(bf16[24,24,128]{2,1,0:T(8,128)(2,1)S(1)} %constant_dynamic-slice_fusion), channel_id=1, source_target_pairs={{0,4},{1,5},{2,6},{3,7},{4,0},{5,1},{6,2},{7,3},{8,12},{9,13},{10,... | collective-permute-start | bytes 442376 | tf_op jit(solution)/shard_map/ppermute | solution.py:376
  71.3 6.8 %collective-permute-done.9.refs_0_ = bf16[24,24,128]{2,1,0:T(8,128)(2,1)S(1)} collective-permute-done((bf16[24,24,128]{2,1,0:T(8,128)(2,1)S(1)}, bf16[24,24,128]{2,1,0:T(8,128)(2,1)S(1)}, u32[]{:S(2)}, u32[]{:S(2)}) %collective-permute-start.9) | collective-permute-done | bytes 147488 | tf_op jit(solution)/shard_map/ppermute | solution.py:376
  78.1 0.0 copy-done.6
  78.1 0.7 shard_map.121
  78.8 2.0 %all-to-all-done.2.summed_ref = bf16[32,4,1152]{2,1,0:T(4,128)(2,1)S(1)} async-done(((bf16[32,4,1152]{2,1,0:T(4,128)(2,1)}), bf16[32,4,1152]{2,1,0:T(4,128)(2,1)S(1)}, u32[]{:S(2)}, u32[]{:S(2)}) %all-to-all-start.2) | async-done | bytes 294944 | tf_op jit(solution)/shard_map/all_to_all | solution.py:275
  80.8 0.0 copy-done.2
  80.8 0.0 copy-done.3
  80.8 0.0 copy-done.5
  80.8 1.9 %shard_map.123 = bf16[1152,128]{1,0:T(8,128)(2,1)} custom-call(f32[128,1152]{1,0:T(8,128)S(1)} %get-tuple-element.20.first_ref, f32[128,1152]{1,0:T(8,128)S(1)} %get-tuple-element.21.gated_ref, bf16[32,4,1152]{2,1,0:T(4,128)(2,1)S(1)} %all-to-all-done.2.summed_ref, bf16[128,128]{1,0:T(8,128)(2,1)S(1)} %copy-done.5, bf16[128,512]{1,0:T(8,128)(2,1)S(1)} %copy-done.2, ...), custom_call_target="tpu_custom_call" | custom-call | tf_op jit(solution)/shard_map/pallas_call | solution.py:425
  (2 shorter events, 0.0 us)
Async XLA Ops:
  3.1 31.8 %copy-start = (bf16[24,48,128]{2,1,0:T(8,128)(2,1)S(1)}, bf16[24,48,128]{2,1,0:T(8,128)(2,1)}, u32[]{:S(2)}) copy-start(bf16[24,48,128]{2,1,0:T(8,128)(2,1)} %pair_ref.1) | copy-start | bytes 884740
  3.1 37.6 %all-to-all-start = ((bf16[8,32,896]{2,1,0:T(8,128)(2,1)}), bf16[8,32,896]{2,1,0:T(8,128)(2,1)S(1)}, u32[]{:S(2)}, u32[]{:S(2)}) async-start(bf16[8,32,896]{2,1,0:T(8,128)(2,1)} %get-tuple-element.14), calls=%async_computation | async-start | bytes 917504 | tf_op jit(solution)/shard_map/all_to_all | solution.py:362
  10.5 0.7 collective-permute-start.1
  11.2 20.0 %collective-permute-start.5 = (bf16[32,1664]{1,0:T(8,128)(2,1)S(1)}, bf16[32,1664]{1,0:T(8,128)(2,1)S(1)}, u32[]{:S(2)}, u32[]{:S(2)}) collective-permute-start(bf16[32,1664]{1,0:T(8,128)(2,1)S(1)} %collective-permute-done.1.refs_0_), channel_id=1, source_target_pairs={{0,4},{1,5},{2,6},{3,7},{4,0},{5,1},{6,2},{7,3},{8,12},{9,13},{10,... | collective-permute-start | bytes 319496 | tf_op jit(solution)/shard_map/ppermute | solution.py:381
  13.3 26.9 %copy-start.4 = (bf16[128,512]{1,0:T(8,128)(2,1)S(1)}, bf16[128,512]{1,0:T(8,128)(2,1)}, u32[]{:S(2)}) copy-start(bf16[128,512]{1,0:T(8,128)(2,1)} %tri_ref.1) | copy-start | bytes 393220
  13.3 23.8 %collective-permute-start.3 = (bf16[32,1664]{1,0:T(8,128)(2,1)S(1)}, bf16[32,1664]{1,0:T(8,128)(2,1)S(1)}, u32[]{:S(2)}, u32[]{:S(2)}) collective-permute-start(bf16[32,1664]{1,0:T(8,128)(2,1)S(1)} %collective-permute-done.1.refs_0_), channel_id=1, source_target_pairs={{0,2},{1,3},{2,0},{3,1},{4,6},{5,7},{6,4},{7,5},{8,10},{9,11},{10,... | collective-permute-start | bytes 319496 | tf_op jit(solution)/shard_map/ppermute | solution.py:387
  31.2 6.4 %collective-permute-start.7 = (bf16[32,1664]{1,0:T(8,128)(2,1)S(1)}, bf16[32,1664]{1,0:T(8,128)(2,1)S(1)}, u32[]{:S(2)}, u32[]{:S(2)}) collective-permute-start(bf16[32,1664]{1,0:T(8,128)(2,1)S(1)} %collective-permute-done.5.refs_4_), channel_id=1, source_target_pairs={{0,2},{1,3},{2,0},{3,1},{4,6},{5,7},{6,4},{7,5},{8,10},{9,11},{10,... | collective-permute-start | bytes 319496 | tf_op jit(solution)/shard_map/ppermute | solution.py:387
  35.0 5.2 %copy-start.7 = (s32[192]{0:T(256)S(1)}, s32[192]{0:T(256)}, u32[]{:S(2)}) copy-start(s32[192]{0:T(256)} %param.14) | copy-start | bytes 2308
  35.0 5.2 %collective-permute-start = (bf16[24,24,128]{2,1,0:T(8,128)(2,1)S(1)}, bf16[24,24,128]{2,1,0:T(8,128)(2,1)S(1)}, u32[]{:S(2)}, u32[]{:S(2)}) collective-permute-start(bf16[24,24,128]{2,1,0:T(8,128)(2,1)S(1)} %constant_dynamic-slice_fusion.1), channel_id=1, source_target_pairs={{0,4},{1,5},{2,6},{3,7},{4,0},{5,1},{6,2},{7,3},{8,12},{9,13},{10,... | collective-permute-start | bytes 442376 | tf_op jit(solution)/shard_map/ppermute | solution.py:376
  36.5 4.1 %collective-permute-start.2 = (bf16[32,1664]{1,0:T(8,128)(2,1)S(1)}, bf16[32,1664]{1,0:T(8,128)(2,1)S(1)}, u32[]{:S(2)}, u32[]{:S(2)}) collective-permute-start(bf16[32,1664]{1,0:T(8,128)(2,1)S(1)} %collective-permute-done.1.refs_0_), channel_id=1, source_target_pairs={{0,1},{1,0},{2,3},{3,2},{4,5},{5,4},{6,7},{7,6},{8,9},{9,8},{10,11... | collective-permute-start | bytes 319496 | tf_op jit(solution)/shard_map/ppermute | solution.py:387
  36.6 4.2 %collective-permute-start.6 = (bf16[32,1664]{1,0:T(8,128)(2,1)S(1)}, bf16[32,1664]{1,0:T(8,128)(2,1)S(1)}, u32[]{:S(2)}, u32[]{:S(2)}) collective-permute-start(bf16[32,1664]{1,0:T(8,128)(2,1)S(1)} %collective-permute-done.5.refs_4_), channel_id=1, source_target_pairs={{0,1},{1,0},{2,3},{3,2},{4,5},{5,4},{6,7},{7,6},{8,9},{9,8},{10,11... | collective-permute-start | bytes 319496 | tf_op jit(solution)/shard_map/ppermute | solution.py:387
  37.1 3.7 %collective-permute-start.4 = (bf16[32,1664]{1,0:T(8,128)(2,1)S(1)}, bf16[32,1664]{1,0:T(8,128)(2,1)S(1)}, u32[]{:S(2)}, u32[]{:S(2)}) collective-permute-start(bf16[32,1664]{1,0:T(8,128)(2,1)S(1)} %collective-permute-done.3.refs_2_), channel_id=1, source_target_pairs={{0,1},{1,0},{2,3},{3,2},{4,5},{5,4},{6,7},{7,6},{8,9},{9,8},{10,11... | collective-permute-start | bytes 319496 | tf_op jit(solution)/shard_map/ppermute | solution.py:387
  37.6 3.1 %collective-permute-start.8 = (bf16[32,1664]{1,0:T(8,128)(2,1)S(1)}, bf16[32,1664]{1,0:T(8,128)(2,1)S(1)}, u32[]{:S(2)}, u32[]{:S(2)}) collective-permute-start(bf16[32,1664]{1,0:T(8,128)(2,1)S(1)} %collective-permute-done.7.refs_6_), channel_id=1, source_target_pairs={{0,1},{1,0},{2,3},{3,2},{4,5},{5,4},{6,7},{7,6},{8,9},{9,8},{10,11... | collective-permute-start | bytes 319496 | tf_op jit(solution)/shard_map/ppermute | solution.py:387
  40.2 1.0 %copy-start.1 = (bf16[1024,128]{1,0:T(8,128)(2,1)S(1)}, bf16[1024,128]{1,0:T(8,128)(2,1)}, u32[]{:S(2)}) copy-start(bf16[1024,128]{1,0:T(8,128)(2,1)} %proj_ref.1) | copy-start | bytes 786436
  66.2 14.6 %all-to-all-start.2 = ((bf16[32,4,1152]{2,1,0:T(4,128)(2,1)}), bf16[32,4,1152]{2,1,0:T(4,128)(2,1)S(1)}, u32[]{:S(2)}, u32[]{:S(2)}) async-start(bf16[32,4,1152]{2,1,0:T(4,128)(2,1)} %shard_map.122), calls=%async_computation.2 | async-start | bytes 589824 | tf_op jit(solution)/shard_map/all_to_all | solution.py:275
  69.4 8.7 %copy-start.6 = (bf16[128,128]{1,0:T(8,128)(2,1)S(1)}, bf16[128,128]{1,0:T(8,128)(2,1)}, u32[]{:S(2)}) copy-start(bf16[128,128]{1,0:T(8,128)(2,1)} %gate_w_ref.1) | copy-start | bytes 98308
  69.4 11.4 %copy-start.2 = (bf16[128,512]{1,0:T(8,128)(2,1)S(1)}, bf16[128,512]{1,0:T(8,128)(2,1)}, u32[]{:S(2)}) copy-start(bf16[128,512]{1,0:T(8,128)(2,1)} %in_ref.1) | copy-start | bytes 393220
  69.4 11.3 %copy-start.3 = (bf16[512,128]{1,0:T(8,128)(2,1)S(1)}, bf16[512,128]{1,0:T(8,128)(2,1)}, u32[]{:S(2)}) copy-start(bf16[512,128]{1,0:T(8,128)(2,1)} %back_ref.1) | copy-start | bytes 393220
  69.4 11.3 %copy-start.5 = (bf16[128,128]{1,0:T(8,128)(2,1)S(1)}, bf16[128,128]{1,0:T(8,128)(2,1)}, u32[]{:S(2)}) copy-start(bf16[128,128]{1,0:T(8,128)(2,1)} %out_w_ref.1) | copy-start | bytes 98308
  69.4 8.6 %collective-permute-start.9 = (bf16[24,24,128]{2,1,0:T(8,128)(2,1)S(1)}, bf16[24,24,128]{2,1,0:T(8,128)(2,1)S(1)}, u32[]{:S(2)}, u32[]{:S(2)}) collective-permute-start(bf16[24,24,128]{2,1,0:T(8,128)(2,1)S(1)} %constant_dynamic-slice_fusion), channel_id=1, source_target_pairs={{0,4},{1,5},{2,6},{3,7},{4,0},{5,1},{6,2},{7,3},{8,12},{9,13},{10,... | collective-permute-start | bytes 442376 | tf_op jit(solution)/shard_map/ppermute | solution.py:376

commit v7 on v6

--- a/solution.py
+++ b/solution.py
@@ -10,6 +10,7 @@
 
 epsilon = 1e-05
 LANES = 128
+ABSENT = 2.0**100
 BF16 = jnp.bfloat16
 F32 = jnp.float32
 NT = (((1,), (1,)), ((), ()))
@@ -49,7 +50,7 @@
 VMEM = pl.BlockSpec(memory_space=pltpu.VMEM)
 
 
-def pack_side(projected, mask, narrow, first, count, put):
+def pack_side(projected, mask, narrow, first, count, put, marked=False):
     sequences, cols = mask.shape
     members = LANES // narrow
     lane = iota((sequences, LANES), 1)
@@ -62,7 +63,10 @@
         for member in range(members):
             part = projected[pl.ds(first + group * members + member, sequences, stride=cols), :]
             value = part if value is None else jnp.where(lane >= member * narrow, part, value)
-        put(group, (value * masks[:, group * LANES : (group + 1) * LANES]).astype(BF16))
+        kept = masks[:, group * LANES : (group + 1) * LANES]
+        put(group, (jnp.where(kept > 0.5, value, ABSENT) if marked else value * kept).astype(BF16))
+    if marked:
+        return
     at = iota((cols, LANES), 1)
     pick = (iota((cols, LANES), 0) - first == at) & (at < count)
     put(groups, matmul(mask, pick.astype(BF16)).astype(BF16))
@@ -96,7 +100,7 @@
         def put_right(group, value):
             packed[h, :, group * LANES : (group + 1) * LANES] = value
 
-        pack_side(right_rows, mask, narrow, h * (cols // parts), cols // parts, put_right)
+        pack_side(right_rows, mask, narrow, h * (cols // parts), cols // parts, put_right, True)
     copies = [
         pltpu.make_async_copy(packed.at[n % parts], right_hbm.at[n], out_sem.at[n])
         for n in range(right_hbm.shape[0])
@@ -152,11 +156,11 @@
         left[pl.ds(pl.multiple_of(start, sequences), sequences), :] = left_ref[...]
     members = LANES // narrow
     groups = tall // members
-    left_width, right_width = tall * narrow, short * narrow
+    left_width = tall * narrow
     width = pair_ref.shape[1]
     planes = right_t.shape[0]
     for p in range(planes):
-        right_t[p] = right_ref[p * LANES : (p + 1) * LANES, :right_width].astype(F32).T
+        right_t[p] = right_ref[p * LANES : (p + 1) * LANES, :].astype(F32).T
     proj[...] = proj_ref[...].astype(F32)
     steps = stacked.shape[0]
     step = narrow // steps
@@ -166,7 +170,8 @@
         some = []
         for p in range(planes):
             each = [right_t.at[p][pl.ds(n * step + d, short, stride=narrow), :] for d in range(step)]
-            some.append(jnp.concatenate(each, axis=0).astype(BF16))
+            each = jnp.concatenate(each, axis=0)
+            some.append(jnp.where(each < ABSENT / 2, each, 0.0).astype(BF16))
         block = matmul(jnp.concatenate(some, axis=1), left[:, :left_width])
         for e in range(0, step, 2):
             lanes = slice(e // 2 * LANES, (e // 2 + 1) * LANES)
@@ -188,7 +193,8 @@
                 spread[n % 2, start : start + narrow, m * width : (m + 1) * width] = part
         term = matmul(stacked[n], spread[n % 2])
         total = term if total is None else total + term
-    counts = matmul(right_ref[:, right_width:], left[:, left_width:], TN)[:short, :]
+    present = [right_t.at[p][pl.ds(0, short, stride=narrow), :] < ABSENT / 2 for p in range(planes)]
+    counts = matmul(jnp.concatenate(present, axis=1).astype(BF16), left[:, left_width:])
     scale = 1.0 / jnp.maximum(counts, 1.0)
     for g in range(groups):
         for m in range(members):
@@ -229,6 +235,7 @@
         return carry
 
     residues = row_count * rows
+    folds = 2 if planes == 2 and residues == 2 * used else 1
     lax.fori_loop(0, col_count, open_column, 0)
     for t in range(own):
         left = [opened.at[p][pl.ds(t, residues, stride=pair), :].astype(BF16) for p in range(planes)]
@@ -237,7 +244,8 @@
             count = min(used, residues - p * used)
             for q in range(planes):
                 total = matmul(left[p], right[q], TN)[:count]
-                summed.at[q][pl.ds(p * used * pair + t, count, stride=pair), :] = total
+                start = p * own if folds == 2 else p * used * pair
+                summed.at[q][pl.ds(start + t, count, stride=pair), :] = total
 
     def close_row(r, carry):
         for c in range(col_count):
@@ -246,10 +254,13 @@
             for i in range(rows):
                 start = pl.multiple_of((r * rows + i) * pair, pair)
                 parts.append(summed[c // each, pl.ds(start, pair), lanes])
-            out_ref[r * col_count + c] = jnp.concatenate(parts, axis=1)[:own].astype(BF16)
+            value = jnp.concatenate(parts, axis=1)
+            for fold in range(folds):
+                at = (r + fold * (row_count // folds)) * col_count + c
+                out_ref[at] = value[fold * own : (fold + 1) * own].astype(BF16)
         return carry
 
-    lax.fori_loop(0, row_count, close_row, 0)
+    lax.fori_loop(0, row_count // folds, close_row, 0)
 
 
 def partner(index, k, count):
@@ -331,7 +342,7 @@
     owners = devices if by_channel else 1
     own = inner // owners
     members = LANES // narrow
-    right_lanes = rows * narrow + LANES
+    right_lanes = rows * narrow
     left_lanes = cols * narrow + LANES
     lines = sequences * cols
     pieces = 8 if narrow % 16 == 0 else 1

time: 83 us -> 81.3 us (0.980)
  starting transfers between devices: 38.9 us -> 37.6 us
    ppermute x6, starting transfers between devices: 22.2 us -> 21 us  [shards(): lax.ppermute(blocks[d, k], ('row', 'col'), near(0, bit))]
where the time goes in v7:
time: 81.3 us; the launch traced here: 81 us
  starting transfers between devices  37.6 us (46%)
  blocking collectives  18.5 us (23%)
  Pallas kernels  12.2 us (15%)
  waiting for transfers between devices  12 us (15%)
    ppermute x6, starting transfers between devices, shards(): lax.ppermute(blocks[d, k], ('row', 'col'), near(0, bit))  21 us
    all_to_all x1, blocking collectives, triangle_by_channel(): lax.all_to_all(gated, ('row', 'col'), split_axis=0, concat_axis=0, tiled=...  18.5 us
    ppermute x2, waiting for transfers between devices, exchange(): given.append(lax.ppermute(part, ('row', 'col'), near(d, 0)))  9.37 us
    all_to_all x1, starting transfers between devices, shards(): lax.all_to_all(right, 'row', split_axis=0, concat_axis=0, tiled=True)  7.42 us
    pallas_call x1, Pallas kernels, shards(): call(functools.partial(outer_kernel, cols, rows, narrow, turns), 24, [((p...  3.62 us
    ppermute x2, starting transfers between devices, exchange(): given.append(lax.ppermute(part, ('row', 'col'), near(d, 0)))  3.36 us
    all_to_all x1, starting transfers between devices, triangle_by_channel(): lax.all_to_all(summed, ('row', 'col'), split_axis=0, concat_axis=0, tiled...  3.11 us
    pallas_call x1, Pallas kernels, shards(): call(functools.partial(side_kernel, narrow), 16, [((row_count, sequences,...  3.08 us
  transfers between devices with their start and end apart: 12, of which 4 were waited for; matrix products, arithmetic and copies ran while one was open for 0% of the time, Pallas kernels for 1%

profile of v7, /device:TPU:0, one launch (start us, length us, event | category | flops | bytes accessed | tf_op | source)
XLA Modules:
  0.0 81.0 jit_solution(8080502130466881168)
XLA Ops:
  0.0 3.1 %shard_map.118 = (bf16[8,32,768]{2,1,0:T(8,128)(2,1)}, bf16[32,1664]{1,0:T(8,128)(2,1)S(1)}) custom-call(bf16[1536,256]{1,0:T(8,128)(2,1)} %bitcast.11, s32[32,48]{1,0:T(8,128)} %mask_hbm.1, bf16[32,256]{1,0:T(8,128)(2,1)} %bitcast.12, bf16[32,256]{1,0:T(8,128)(2,1)} %bitcast.13), custom_call_target="tpu_custom_call" | custom-call | tf_op jit(solution)/shard_map/pallas_call | solution.py:352
  3.1 0.0 copy-start
  3.1 7.4 %all-to-all-start = ((bf16[8,32,768]{2,1,0:T(8,128)(2,1)}), bf16[8,32,768]{2,1,0:T(8,128)(2,1)S(1)}, u32[]{:S(2)}, u32[]{:S(2)}) async-start(bf16[8,32,768]{2,1,0:T(8,128)(2,1)} %get-tuple-element.14), calls=%async_computation | async-start | bytes 786432 | tf_op jit(solution)/shard_map/all_to_all | solution.py:373
  10.5 0.7 collective-permute-start.1
  11.2 0.0 collective-permute-done.1.refs_0_
  11.2 2.1 %collective-permute-start.5 = (bf16[32,1664]{1,0:T(8,128)(2,1)S(1)}, bf16[32,1664]{1,0:T(8,128)(2,1)S(1)}, u32[]{:S(2)}, u32[]{:S(2)}) collective-permute-start(bf16[32,1664]{1,0:T(8,128)(2,1)S(1)} %collective-permute-done.1.refs_0_), channel_id=1, source_target_pairs={{0,4},{1,5},{2,6},{3,7},{4,0},{5,1},{6,2},{7,3},{8,12},{9,13},{10,... | collective-permute-start | bytes 319496 | tf_op jit(solution)/shard_map/ppermute | solution.py:392
  13.3 0.0 copy-start.4
  13.3 16.5 %collective-permute-start.3 = (bf16[32,1664]{1,0:T(8,128)(2,1)S(1)}, bf16[32,1664]{1,0:T(8,128)(2,1)S(1)}, u32[]{:S(2)}, u32[]{:S(2)}) collective-permute-start(bf16[32,1664]{1,0:T(8,128)(2,1)S(1)} %collective-permute-done.1.refs_0_), channel_id=1, source_target_pairs={{0,2},{1,3},{2,0},{3,1},{4,6},{5,7},{6,4},{7,5},{8,10},{9,11},{10,... | collective-permute-start | bytes 319496 | tf_op jit(solution)/shard_map/ppermute | solution.py:398
  29.8 0.0 collective-permute-done.5.refs_4_
  29.8 4.0 %collective-permute-start.7 = (bf16[32,1664]{1,0:T(8,128)(2,1)S(1)}, bf16[32,1664]{1,0:T(8,128)(2,1)S(1)}, u32[]{:S(2)}, u32[]{:S(2)}) collective-permute-start(bf16[32,1664]{1,0:T(8,128)(2,1)S(1)} %collective-permute-done.5.refs_4_), channel_id=1, source_target_pairs={{0,2},{1,3},{2,0},{3,1},{4,6},{5,7},{6,4},{7,5},{8,10},{9,11},{10,... | collective-permute-start | bytes 319496 | tf_op jit(solution)/shard_map/ppermute | solution.py:398
  33.8 0.0 copy-done
  33.8 0.0 copy-start.7
  33.8 1.5 %collective-permute-start = (bf16[24,24,128]{2,1,0:T(8,128)(2,1)S(1)}, bf16[24,24,128]{2,1,0:T(8,128)(2,1)S(1)}, u32[]{:S(2)}, u32[]{:S(2)}) collective-permute-start(bf16[24,24,128]{2,1,0:T(8,128)(2,1)S(1)} %constant_dynamic-slice_fusion.1), channel_id=1, source_target_pairs={{0,4},{1,5},{2,6},{3,7},{4,0},{5,1},{6,2},{7,3},{8,12},{9,13},{10,... | collective-permute-start | bytes 442376 | tf_op jit(solution)/shard_map/ppermute | solution.py:387
  35.3 0.0 collective-permute-start.2
  35.3 0.5 collective-permute-start.6
  35.8 0.0 collective-permute-done.3.refs_2_
  35.8 0.0 collective-permute-start.4
  35.8 0.6 collective-permute-done.7.refs_6_
  36.4 0.0 collective-permute-start.8
  36.4 2.6 %collective-permute-done.refs_0_ = bf16[24,24,128]{2,1,0:T(8,128)(2,1)S(1)} collective-permute-done((bf16[24,24,128]{2,1,0:T(8,128)(2,1)S(1)}, bf16[24,24,128]{2,1,0:T(8,128)(2,1)S(1)}, u32[]{:S(2)}, u32[]{:S(2)}) %collective-permute-start) | collective-permute-done | bytes 147488 | tf_op jit(solution)/shard_map/ppermute | solution.py:387
  39.0 0.0 copy-done.4
  39.0 0.0 copy-done.7
  39.0 0.0 copy-start.1
  39.0 0.5 shard_map.119
  39.5 0.0 collective-permute-done.2.refs_1_
  39.5 0.0 collective-permute-done.6.refs_5_
  39.5 0.0 collective-permute-done.4.refs_3_
  39.5 0.0 collective-permute-done.8.refs_7_
  39.6 0.0 all-to-all-done
  39.6 0.4 copy-done.1
  40.0 3.6 %shard_map.120 = (bf16[1152,128]{1,0:T(8,128)(2,1)S(1)}, bf16[32,8,1152]{2,1,0:T(8,128)(2,1)S(1)}) custom-call(bf16[256,768]{1,0:T(8,128)(2,1)S(1)} %bitcast.7, bf16[1152,128]{1,0:T(8,128)(2,1)S(1)} %get-tuple-element.15.pair_ref, bf16[1024,128]{1,0:T(8,128)(2,1)S(1)} %copy-done.1, bf16[512,128]{1,0:T(8,128)(2,1)S(1)} %get-tuple-element.16.tri_ref, ...), custom_call_target="tpu_custom_call" | custom-call | tf_op jit(solution)/shard_map/pallas_call | solution.py:414
  43.6 18.5 %all_to_all.15.given_ref = bf16[32,8,1152]{2,1,0:T(8,128)(2,1)S(1)} all-to-all(bf16[32,8,1152]{2,1,0:T(8,128)(2,1)S(1)} %get-tuple-element.22), channel_id=1, replica_groups=mesh['row'=8,'col'=4] {'row','col'}, dimensions={0} | all-to-all | bytes 1179648 | tf_op jit(solution)/shard_map/all_to_all | solution.py:277
  62.1 2.5 %shard_map.122 = bf16[32,4,1152]{2,1,0:T(4,128)(2,1)} custom-call(bf16[32,8,1152]{2,1,0:T(8,128)(2,1)S(1)} %all_to_all.15.given_ref), custom_call_target="tpu_custom_call" | custom-call | tf_op jit(solution)/shard_map/pallas_call | solution.py:280
  64.6 3.1 %all-to-all-start.2 = ((bf16[32,4,1152]{2,1,0:T(4,128)(2,1)}), bf16[32,4,1152]{2,1,0:T(4,128)(2,1)S(1)}, u32[]{:S(2)}, u32[]{:S(2)}) async-start(bf16[32,4,1152]{2,1,0:T(4,128)(2,1)} %shard_map.122), calls=%async_computation.2 | async-start | bytes 589824 | tf_op jit(solution)/shard_map/all_to_all | solution.py:286
  67.7 0.0 copy-start.6
  67.7 0.0 copy-start.2
  67.8 0.0 copy-start.3
  67.8 0.0 copy-start.5
  67.8 1.8 %collective-permute-start.9 = (bf16[24,24,128]{2,1,0:T(8,128)(2,1)S(1)}, bf16[24,24,128]{2,1,0:T(8,128)(2,1)S(1)}, u32[]{:S(2)}, u32[]{:S(2)}) collective-permute-start(bf16[24,24,128]{2,1,0:T(8,128)(2,1)S(1)} %constant_dynamic-slice_fusion), channel_id=1, source_target_pairs={{0,4},{1,5},{2,6},{3,7},{4,0},{5,1},{6,2},{7,3},{8,12},{9,13},{10,... | collective-permute-start | bytes 442376 | tf_op jit(solution)/shard_map/ppermute | solution.py:387
  69.6 6.8 %collective-permute-done.9.refs_0_ = bf16[24,24,128]{2,1,0:T(8,128)(2,1)S(1)} collective-permute-done((bf16[24,24,128]{2,1,0:T(8,128)(2,1)S(1)}, bf16[24,24,128]{2,1,0:T(8,128)(2,1)S(1)}, u32[]{:S(2)}, u32[]{:S(2)}) %collective-permute-start.9) | collective-permute-done | bytes 147488 | tf_op jit(solution)/shard_map/ppermute | solution.py:387
  76.4 0.0 copy-done.6
  76.4 0.7 shard_map.121
  77.1 2.0 %all-to-all-done.2.summed_ref = bf16[32,4,1152]{2,1,0:T(4,128)(2,1)S(1)} async-done(((bf16[32,4,1152]{2,1,0:T(4,128)(2,1)}), bf16[32,4,1152]{2,1,0:T(4,128)(2,1)S(1)}, u32[]{:S(2)}, u32[]{:S(2)}) %all-to-all-start.2) | async-done | bytes 294944 | tf_op jit(solution)/shard_map/all_to_all | solution.py:286
  79.1 0.0 copy-done.2
  79.1 0.0 copy-done.3
  79.1 0.0 copy-done.5
  79.1 1.9 %shard_map.123 = bf16[1152,128]{1,0:T(8,128)(2,1)} custom-call(f32[128,1152]{1,0:T(8,128)S(1)} %get-tuple-element.20.first_ref, f32[128,1152]{1,0:T(8,128)S(1)} %get-tuple-element.21.gated_ref, bf16[32,4,1152]{2,1,0:T(4,128)(2,1)S(1)} %all-to-all-done.2.summed_ref, bf16[128,128]{1,0:T(8,128)(2,1)S(1)} %copy-done.5, bf16[128,512]{1,0:T(8,128)(2,1)S(1)} %copy-done.2, ...), custom_call_target="tpu_custom_call" | custom-call | tf_op jit(solution)/shard_map/pallas_call | solution.py:436
  (2 shorter events, 0.0 us)
Async XLA Ops:
  3.1 30.7 %copy-start = (bf16[24,48,128]{2,1,0:T(8,128)(2,1)S(1)}, bf16[24,48,128]{2,1,0:T(8,128)(2,1)}, u32[]{:S(2)}) copy-start(bf16[24,48,128]{2,1,0:T(8,128)(2,1)} %pair_ref.1) | copy-start | bytes 884740
  3.1 36.5 %all-to-all-start = ((bf16[8,32,768]{2,1,0:T(8,128)(2,1)}), bf16[8,32,768]{2,1,0:T(8,128)(2,1)S(1)}, u32[]{:S(2)}, u32[]{:S(2)}) async-start(bf16[8,32,768]{2,1,0:T(8,128)(2,1)} %get-tuple-element.14), calls=%async_computation | async-start | bytes 786432 | tf_op jit(solution)/shard_map/all_to_all | solution.py:373
  10.5 0.7 collective-permute-start.1
  11.2 18.6 %collective-permute-start.5 = (bf16[32,1664]{1,0:T(8,128)(2,1)S(1)}, bf16[32,1664]{1,0:T(8,128)(2,1)S(1)}, u32[]{:S(2)}, u32[]{:S(2)}) collective-permute-start(bf16[32,1664]{1,0:T(8,128)(2,1)S(1)} %collective-permute-done.1.refs_0_), channel_id=1, source_target_pairs={{0,4},{1,5},{2,6},{3,7},{4,0},{5,1},{6,2},{7,3},{8,12},{9,13},{10,... | collective-permute-start | bytes 319496 | tf_op jit(solution)/shard_map/ppermute | solution.py:392
  13.3 25.7 %copy-start.4 = (bf16[128,512]{1,0:T(8,128)(2,1)S(1)}, bf16[128,512]{1,0:T(8,128)(2,1)}, u32[]{:S(2)}) copy-start(bf16[128,512]{1,0:T(8,128)(2,1)} %tri_ref.1) | copy-start | bytes 393220
  13.3 22.6 %collective-permute-start.3 = (bf16[32,1664]{1,0:T(8,128)(2,1)S(1)}, bf16[32,1664]{1,0:T(8,128)(2,1)S(1)}, u32[]{:S(2)}, u32[]{:S(2)}) collective-permute-start(bf16[32,1664]{1,0:T(8,128)(2,1)S(1)} %collective-permute-done.1.refs_0_), channel_id=1, source_target_pairs={{0,2},{1,3},{2,0},{3,1},{4,6},{5,7},{6,4},{7,5},{8,10},{9,11},{10,... | collective-permute-start | bytes 319496 | tf_op jit(solution)/shard_map/ppermute | solution.py:398
  29.8 6.7 %collective-permute-start.7 = (bf16[32,1664]{1,0:T(8,128)(2,1)S(1)}, bf16[32,1664]{1,0:T(8,128)(2,1)S(1)}, u32[]{:S(2)}, u32[]{:S(2)}) collective-permute-start(bf16[32,1664]{1,0:T(8,128)(2,1)S(1)} %collective-permute-done.5.refs_4_), channel_id=1, source_target_pairs={{0,2},{1,3},{2,0},{3,1},{4,6},{5,7},{6,4},{7,5},{8,10},{9,11},{10,... | collective-permute-start | bytes 319496 | tf_op jit(solution)/shard_map/ppermute | solution.py:398
  33.8 5.2 %copy-start.7 = (s32[192]{0:T(256)S(1)}, s32[192]{0:T(256)}, u32[]{:S(2)}) copy-start(s32[192]{0:T(256)} %param.14) | copy-start | bytes 2308
  33.8 5.2 %collective-permute-start = (bf16[24,24,128]{2,1,0:T(8,128)(2,1)S(1)}, bf16[24,24,128]{2,1,0:T(8,128)(2,1)S(1)}, u32[]{:S(2)}, u32[]{:S(2)}) collective-permute-start(bf16[24,24,128]{2,1,0:T(8,128)(2,1)S(1)} %constant_dynamic-slice_fusion.1), channel_id=1, source_target_pairs={{0,4},{1,5},{2,6},{3,7},{4,0},{5,1},{6,2},{7,3},{8,12},{9,13},{10,... | collective-permute-start | bytes 442376 | tf_op jit(solution)/shard_map/ppermute | solution.py:387
  35.3 4.2 %collective-permute-start.2 = (bf16[32,1664]{1,0:T(8,128)(2,1)S(1)}, bf16[32,1664]{1,0:T(8,128)(2,1)S(1)}, u32[]{:S(2)}, u32[]{:S(2)}) collective-permute-start(bf16[32,1664]{1,0:T(8,128)(2,1)S(1)} %collective-permute-done.1.refs_0_), channel_id=1, source_target_pairs={{0,1},{1,0},{2,3},{3,2},{4,5},{5,4},{6,7},{7,6},{8,9},{9,8},{10,11... | collective-permute-start | bytes 319496 | tf_op jit(solution)/shard_map/ppermute | solution.py:398
  35.3 4.2 %collective-permute-start.6 = (bf16[32,1664]{1,0:T(8,128)(2,1)S(1)}, bf16[32,1664]{1,0:T(8,128)(2,1)S(1)}, u32[]{:S(2)}, u32[]{:S(2)}) collective-permute-start(bf16[32,1664]{1,0:T(8,128)(2,1)S(1)} %collective-permute-done.5.refs_4_), channel_id=1, source_target_pairs={{0,1},{1,0},{2,3},{3,2},{4,5},{5,4},{6,7},{7,6},{8,9},{9,8},{10,11... | collective-permute-start | bytes 319496 | tf_op jit(solution)/shard_map/ppermute | solution.py:398
  35.8 3.7 %collective-permute-start.4 = (bf16[32,1664]{1,0:T(8,128)(2,1)S(1)}, bf16[32,1664]{1,0:T(8,128)(2,1)S(1)}, u32[]{:S(2)}, u32[]{:S(2)}) collective-permute-start(bf16[32,1664]{1,0:T(8,128)(2,1)S(1)} %collective-permute-done.3.refs_2_), channel_id=1, source_target_pairs={{0,1},{1,0},{2,3},{3,2},{4,5},{5,4},{6,7},{7,6},{8,9},{9,8},{10,11... | collective-permute-start | bytes 319496 | tf_op jit(solution)/shard_map/ppermute | solution.py:398
  36.4 3.1 %collective-permute-start.8 = (bf16[32,1664]{1,0:T(8,128)(2,1)S(1)}, bf16[32,1664]{1,0:T(8,128)(2,1)S(1)}, u32[]{:S(2)}, u32[]{:S(2)}) collective-permute-start(bf16[32,1664]{1,0:T(8,128)(2,1)S(1)} %collective-permute-done.7.refs_6_), channel_id=1, source_target_pairs={{0,1},{1,0},{2,3},{3,2},{4,5},{5,4},{6,7},{7,6},{8,9},{9,8},{10,11... | collective-permute-start | bytes 319496 | tf_op jit(solution)/shard_map/ppermute | solution.py:398
  39.0 1.0 %copy-start.1 = (bf16[1024,128]{1,0:T(8,128)(2,1)S(1)}, bf16[1024,128]{1,0:T(8,128)(2,1)}, u32[]{:S(2)}) copy-start(bf16[1024,128]{1,0:T(8,128)(2,1)} %proj_ref.1) | copy-start | bytes 786436
  64.6 14.5 %all-to-all-start.2 = ((bf16[32,4,1152]{2,1,0:T(4,128)(2,1)}), bf16[32,4,1152]{2,1,0:T(4,128)(2,1)S(1)}, u32[]{:S(2)}, u32[]{:S(2)}) async-start(bf16[32,4,1152]{2,1,0:T(4,128)(2,1)} %shard_map.122), calls=%async_computation.2 | async-start | bytes 589824 | tf_op jit(solution)/shard_map/all_to_all | solution.py:286
  67.7 8.7 %copy-start.6 = (bf16[128,128]{1,0:T(8,128)(2,1)S(1)}, bf16[128,128]{1,0:T(8,128)(2,1)}, u32[]{:S(2)}) copy-start(bf16[128,128]{1,0:T(8,128)(2,1)} %gate_w_ref.1) | copy-start | bytes 98308
  67.7 11.4 %copy-start.2 = (bf16[128,512]{1,0:T(8,128)(2,1)S(1)}, bf16[128,512]{1,0:T(8,128)(2,1)}, u32[]{:S(2)}) copy-start(bf16[128,512]{1,0:T(8,128)(2,1)} %in_ref.1) | copy-start | bytes 393220
  67.8 11.3 %copy-start.3 = (bf16[512,128]{1,0:T(8,128)(2,1)S(1)}, bf16[512,128]{1,0:T(8,128)(2,1)}, u32[]{:S(2)}) copy-start(bf16[512,128]{1,0:T(8,128)(2,1)} %back_ref.1) | copy-start | bytes 393220
  67.8 11.3 %copy-start.5 = (bf16[128,128]{1,0:T(8,128)(2,1)S(1)}, bf16[128,128]{1,0:T(8,128)(2,1)}, u32[]{:S(2)}) copy-start(bf16[128,128]{1,0:T(8,128)(2,1)} %out_w_ref.1) | copy-start | bytes 98308
  67.8 8.6 %collective-permute-start.9 = (bf16[24,24,128]{2,1,0:T(8,128)(2,1)S(1)}, bf16[24,24,128]{2,1,0:T(8,128)(2,1)S(1)}, u32[]{:S(2)}, u32[]{:S(2)}) collective-permute-start(bf16[24,24,128]{2,1,0:T(8,128)(2,1)S(1)} %constant_dynamic-slice_fusion), channel_id=1, source_target_pairs={{0,4},{1,5},{2,6},{3,7},{4,0},{5,1},{6,2},{7,3},{8,12},{9,13},{10,... | collective-permute-start | bytes 442376 | tf_op jit(solution)/shard_map/ppermute | solution.py:387

commit v8 on v7

--- a/solution.py
+++ b/solution.py
@@ -152,7 +152,8 @@
     x, column = lax.rem(lax.axis_index("row"), parts), lax.axis_index("col")
     for n, left_ref in enumerate(left_refs):
         d, k = n // sources, n % sources
-        start = (source(column, k, sources) * parts + lax.rem(x - d + parts, parts)) * sequences
+        plane = turned_column(source(column, k, sources), sources)
+        start = (plane * parts + lax.rem(x - d + parts, parts)) * sequences
         left[pl.ds(pl.multiple_of(start, sequences), sequences), :] = left_ref[...]
     members = LANES // narrow
     groups = tall // members
@@ -267,6 +268,10 @@
     return index ^ k if count & (count - 1) == 0 else (index + k) % count
 
 
+def turned_column(plane, count):
+    return plane ^ (count // 2) if count & (count - 1) == 0 else plane
+
+
 def source(index, k, count):
     return index ^ k if count & (count - 1) == 0 else lax.rem(index - k + count, count)
 
@@ -387,7 +392,7 @@
             given.append(lax.ppermute(part, ("row", "col"), near(d, 0)))
         return given
 
-    turned = route(lambda row, col: (turns * col + row % turns, row // turns))
+    turned = route(lambda row, col: (turns * col + row % turns, turned_column(row // turns, col_count)))
     left = lax.ppermute(left, ("row", "col"), turned)
     across = [left] + [lax.ppermute(left, ("row", "col"), near(d, 0)) for d in range(1, turns)]
     blocks = {(d, 0): value for d, value in enumerate(across)}

time: 81.3 us -> 81.3 us (level)
  starting transfers between devices: 37.6 us -> 17.5 us
  waiting for transfers between devices: 12 us -> 31 us
  blocking collectives: 18.5 us -> 19.9 us
    ppermute x6, starting transfers between devices: 21 us -> 0.52 us  [shards(): lax.ppermute(blocks[d, k], ('row', 'col'), near(0, bit))]
    ppermute x1, waiting for transfers between devices: 0.01 us -> 14.7 us  [shards(): left = lax.ppermute(left, ('row', 'col'), turned)]
    ppermute x1, waiting for transfers between devices: 0.01 us -> 4.06 us  [shards(): lax.ppermute(left, ('row', 'col'), near(d, 0))]
    ppermute x6, waiting for transfers between devices: 0.61 us -> 2.86 us  [shards(): lax.ppermute(blocks[d, k], ('row', 'col'), near(0, bit))]
    ppermute x2, waiting for transfers between devices: 9.37 us -> 7.35 us  [exchange(): given.append(lax.ppermute(part, ('row', 'col'), near(d, 0)))]
    all_to_all x1, blocking collectives: 18.5 us -> 19.9 us  [triangle_by_channel(): lax.all_to_all(gated, ('row', 'col'), split_axis=0, concat_axis=0, tiled=...]
    ppermute x1, starting transfers between devices: 0.66 us -> 1.52 us  [shards(): left = lax.ppermute(left, ('row', 'col'), turned)]
  transfers between devices with their start and end apart: 12 -> 12, of which waited for: 4 -> 7; matrix products, arithmetic and copies ran while one was open for 0% -> 0% of each run, Pallas kernels for 1% -> 1%
where the time goes in v8:
time: 81.3 us; the launch traced here: 81 us
  waiting for transfers between devices  31 us (38%)
  blocking collectives  19.9 us (24%)
  starting transfers between devices  17.5 us (22%)
  Pallas kernels  12.2 us (15%)
    all_to_all x1, blocking collectives, triangle_by_channel(): lax.all_to_all(gated, ('row', 'col'), split_axis=0, concat_axis=0, tiled=...  19.9 us
    ppermute x1, waiting for transfers between devices, shards(): left = lax.ppermute(left, ('row', 'col'), turned)  14.7 us
    all_to_all x1, starting transfers between devices, shards(): lax.all_to_all(right, 'row', split_axis=0, concat_axis=0, tiled=True)  7.42 us
    ppermute x2, waiting for transfers between devices, exchange(): given.append(lax.ppermute(part, ('row', 'col'), near(d, 0)))  7.35 us
    ppermute x1, waiting for transfers between devices, shards(): lax.ppermute(left, ('row', 'col'), near(d, 0))  4.06 us
    pallas_call x1, Pallas kernels, shards(): call(functools.partial(outer_kernel, cols, rows, narrow, turns), 24, [((p...  3.62 us
    ppermute x2, starting transfers between devices, exchange(): given.append(lax.ppermute(part, ('row', 'col'), near(d, 0)))  3.36 us
    all_to_all x1, starting transfers between devices, triangle_by_channel(): lax.all_to_all(summed, ('row', 'col'), split_axis=0, concat_axis=0, tiled...  3.2 us
  transfers between devices with their start and end apart: 12, of which 7 were waited for; matrix products, arithmetic and copies ran while one was open for 0% of the time, Pallas kernels for 1%

profile of v8, /device:TPU:0, one launch (start us, length us, event | category | flops | bytes accessed | tf_op | source)
XLA Modules:
  0.0 81.0 jit_solution(10867977502523837379)
XLA Ops:
  0.0 3.1 %shard_map.118 = (bf16[8,32,768]{2,1,0:T(8,128)(2,1)}, bf16[32,1664]{1,0:T(8,128)(2,1)S(1)}) custom-call(bf16[1536,256]{1,0:T(8,128)(2,1)} %bitcast.11, s32[32,48]{1,0:T(8,128)} %mask_hbm.1, bf16[32,256]{1,0:T(8,128)(2,1)} %bitcast.12, bf16[32,256]{1,0:T(8,128)(2,1)} %bitcast.13), custom_call_target="tpu_custom_call" | custom-call | tf_op jit(solution)/shard_map/pallas_call | solution.py:357
  3.1 0.0 copy-start
  3.1 7.4 %all-to-all-start = ((bf16[8,32,768]{2,1,0:T(8,128)(2,1)}), bf16[8,32,768]{2,1,0:T(8,128)(2,1)S(1)}, u32[]{:S(2)}, u32[]{:S(2)}) async-start(bf16[8,32,768]{2,1,0:T(8,128)(2,1)} %get-tuple-element.14), calls=%async_computation | async-start | bytes 786432 | tf_op jit(solution)/shard_map/all_to_all | solution.py:378
  10.5 1.5 %collective-permute-start.1 = (bf16[32,1664]{1,0:T(8,128)(2,1)S(1)}, bf16[32,1664]{1,0:T(8,128)(2,1)S(1)}, u32[]{:S(2)}, u32[]{:S(2)}) collective-permute-start(bf16[32,1664]{1,0:T(8,128)(2,1)S(1)} %get-tuple-element.18), channel_id=1, source_target_pairs={{0,2},{1,10},{2,18},{3,26},{4,6},{5,14},{6,22},{7,30},{8,3},{9,11}... | collective-permute-start | bytes 319496 | tf_op jit(solution)/shard_map/ppermute | solution.py:396
  12.0 14.7 %collective-permute-done.1.refs_0_ = bf16[32,1664]{1,0:T(8,128)(2,1)S(1)} collective-permute-done((bf16[32,1664]{1,0:T(8,128)(2,1)S(1)}, bf16[32,1664]{1,0:T(8,128)(2,1)S(1)}, u32[]{:S(2)}, u32[]{:S(2)}) %collective-permute-start.1) | collective-permute-done | bytes 106528 | tf_op jit(solution)/shard_map/ppermute | solution.py:396
  26.8 1.5 %collective-permute-start.5 = (bf16[32,1664]{1,0:T(8,128)(2,1)S(1)}, bf16[32,1664]{1,0:T(8,128)(2,1)S(1)}, u32[]{:S(2)}, u32[]{:S(2)}) collective-permute-start(bf16[32,1664]{1,0:T(8,128)(2,1)S(1)} %collective-permute-done.1.refs_0_), channel_id=1, source_target_pairs={{0,4},{1,5},{2,6},{3,7},{4,0},{5,1},{6,2},{7,3},{8,12},{9,13},{10,... | collective-permute-start | bytes 319496 | tf_op jit(solution)/shard_map/ppermute | solution.py:397
  28.2 0.0 copy-start.4
  28.2 0.0 collective-permute-start.3
  28.2 4.1 %collective-permute-done.5.refs_4_ = bf16[32,1664]{1,0:T(8,128)(2,1)S(1)} collective-permute-done((bf16[32,1664]{1,0:T(8,128)(2,1)S(1)}, bf16[32,1664]{1,0:T(8,128)(2,1)S(1)}, u32[]{:S(2)}, u32[]{:S(2)}) %collective-permute-start.5) | collective-permute-done | bytes 106528 | tf_op jit(solution)/shard_map/ppermute | solution.py:397
  32.3 0.0 collective-permute-start.7
  32.3 0.0 copy-done
  32.3 0.0 copy-start.7
  32.3 1.5 %collective-permute-start = (bf16[24,24,128]{2,1,0:T(8,128)(2,1)S(1)}, bf16[24,24,128]{2,1,0:T(8,128)(2,1)S(1)}, u32[]{:S(2)}, u32[]{:S(2)}) collective-permute-start(bf16[24,24,128]{2,1,0:T(8,128)(2,1)S(1)} %constant_dynamic-slice_fusion.1), channel_id=1, source_target_pairs={{0,4},{1,5},{2,6},{3,7},{4,0},{5,1},{6,2},{7,3},{8,12},{9,13},{10,... | collective-permute-start | bytes 442376 | tf_op jit(solution)/shard_map/ppermute | solution.py:392
  33.9 0.0 collective-permute-start.2
  33.9 0.5 collective-permute-start.6
  34.4 0.0 collective-permute-done.3.refs_2_
  34.4 0.0 collective-permute-start.4
  34.4 2.6 %collective-permute-done.7.refs_6_ = bf16[32,1664]{1,0:T(8,128)(2,1)S(1)} collective-permute-done((bf16[32,1664]{1,0:T(8,128)(2,1)S(1)}, bf16[32,1664]{1,0:T(8,128)(2,1)S(1)}, u32[]{:S(2)}, u32[]{:S(2)}) %collective-permute-start.7) | collective-permute-done | bytes 106528 | tf_op jit(solution)/shard_map/ppermute | solution.py:403
  37.0 0.0 collective-permute-start.8
  37.0 0.5 collective-permute-done.refs_0_
  37.5 0.0 copy-done.4
  37.5 0.0 copy-done.7
  37.6 0.0 copy-start.1
  37.6 0.5 shard_map.119
  38.1 0.0 collective-permute-done.2.refs_1_
  38.1 0.0 collective-permute-done.6.refs_5_
  38.1 0.0 collective-permute-done.4.refs_3_
  38.1 0.2 collective-permute-done.8.refs_7_
  38.3 0.0 all-to-all-done
  38.3 0.2 copy-done.1
  38.5 3.6 %shard_map.120 = (bf16[1152,128]{1,0:T(8,128)(2,1)S(1)}, bf16[32,8,1152]{2,1,0:T(8,128)(2,1)S(1)}) custom-call(bf16[256,768]{1,0:T(8,128)(2,1)S(1)} %bitcast.7, bf16[1152,128]{1,0:T(8,128)(2,1)S(1)} %get-tuple-element.15.pair_ref, bf16[1024,128]{1,0:T(8,128)(2,1)S(1)} %copy-done.1, bf16[512,128]{1,0:T(8,128)(2,1)S(1)} %get-tuple-element.16.tri_ref, ...), custom_call_target="tpu_custom_call" | custom-call | tf_op jit(solution)/shard_map/pallas_call | solution.py:419
  42.1 19.9 %all_to_all.15.given_ref = bf16[32,8,1152]{2,1,0:T(8,128)(2,1)S(1)} all-to-all(bf16[32,8,1152]{2,1,0:T(8,128)(2,1)S(1)} %get-tuple-element.22), channel_id=1, replica_groups=mesh['row'=8,'col'=4] {'row','col'}, dimensions={0} | all-to-all | bytes 1179648 | tf_op jit(solution)/shard_map/all_to_all | solution.py:282
  62.0 2.5 %shard_map.122 = bf16[32,4,1152]{2,1,0:T(4,128)(2,1)} custom-call(bf16[32,8,1152]{2,1,0:T(8,128)(2,1)S(1)} %all_to_all.15.given_ref), custom_call_target="tpu_custom_call" | custom-call | tf_op jit(solution)/shard_map/pallas_call | solution.py:285
  64.5 3.2 %all-to-all-start.2 = ((bf16[32,4,1152]{2,1,0:T(4,128)(2,1)}), bf16[32,4,1152]{2,1,0:T(4,128)(2,1)S(1)}, u32[]{:S(2)}, u32[]{:S(2)}) async-start(bf16[32,4,1152]{2,1,0:T(4,128)(2,1)} %shard_map.122), calls=%async_computation.2 | async-start | bytes 589824 | tf_op jit(solution)/shard_map/all_to_all | solution.py:291
  67.7 0.0 copy-start.6
  67.7 0.0 copy-start.2
  67.8 0.0 copy-start.3
  67.8 0.0 copy-start.5
  67.8 1.8 %collective-permute-start.9 = (bf16[24,24,128]{2,1,0:T(8,128)(2,1)S(1)}, bf16[24,24,128]{2,1,0:T(8,128)(2,1)S(1)}, u32[]{:S(2)}, u32[]{:S(2)}) collective-permute-start(bf16[24,24,128]{2,1,0:T(8,128)(2,1)S(1)} %constant_dynamic-slice_fusion), channel_id=1, source_target_pairs={{0,4},{1,5},{2,6},{3,7},{4,0},{5,1},{6,2},{7,3},{8,12},{9,13},{10,... | collective-permute-start | bytes 442376 | tf_op jit(solution)/shard_map/ppermute | solution.py:392
  69.6 6.8 %collective-permute-done.9.refs_0_ = bf16[24,24,128]{2,1,0:T(8,128)(2,1)S(1)} collective-permute-done((bf16[24,24,128]{2,1,0:T(8,128)(2,1)S(1)}, bf16[24,24,128]{2,1,0:T(8,128)(2,1)S(1)}, u32[]{:S(2)}, u32[]{:S(2)}) %collective-permute-start.9) | collective-permute-done | bytes 147488 | tf_op jit(solution)/shard_map/ppermute | solution.py:392
  76.4 0.0 copy-done.6
  76.4 0.7 shard_map.121
  77.1 2.0 %all-to-all-done.2.summed_ref = bf16[32,4,1152]{2,1,0:T(4,128)(2,1)S(1)} async-done(((bf16[32,4,1152]{2,1,0:T(4,128)(2,1)}), bf16[32,4,1152]{2,1,0:T(4,128)(2,1)S(1)}, u32[]{:S(2)}, u32[]{:S(2)}) %all-to-all-start.2) | async-done | bytes 294944 | tf_op jit(solution)/shard_map/all_to_all | solution.py:291
  79.1 0.0 copy-done.2
  79.1 0.0 copy-done.3
  79.1 0.0 copy-done.5
  79.1 1.9 %shard_map.123 = bf16[1152,128]{1,0:T(8,128)(2,1)} custom-call(f32[128,1152]{1,0:T(8,128)S(1)} %get-tuple-element.20.first_ref, f32[128,1152]{1,0:T(8,128)S(1)} %get-tuple-element.21.gated_ref, bf16[32,4,1152]{2,1,0:T(4,128)(2,1)S(1)} %all-to-all-done.2.summed_ref, bf16[128,128]{1,0:T(8,128)(2,1)S(1)} %copy-done.5, bf16[128,512]{1,0:T(8,128)(2,1)S(1)} %copy-done.2, ...), custom_call_target="tpu_custom_call" | custom-call | tf_op jit(solution)/shard_map/pallas_call | solution.py:441
  (2 shorter events, 0.0 us)
Async XLA Ops:
  3.1 29.2 %copy-start = (bf16[24,48,128]{2,1,0:T(8,128)(2,1)S(1)}, bf16[24,48,128]{2,1,0:T(8,128)(2,1)}, u32[]{:S(2)}) copy-start(bf16[24,48,128]{2,1,0:T(8,128)(2,1)} %pair_ref.1) | copy-start | bytes 884740
  3.1 35.2 %all-to-all-start = ((bf16[8,32,768]{2,1,0:T(8,128)(2,1)}), bf16[8,32,768]{2,1,0:T(8,128)(2,1)S(1)}, u32[]{:S(2)}, u32[]{:S(2)}) async-start(bf16[8,32,768]{2,1,0:T(8,128)(2,1)} %get-tuple-element.14), calls=%async_computation | async-start | bytes 786432 | tf_op jit(solution)/shard_map/all_to_all | solution.py:378
  10.5 16.2 %collective-permute-start.1 = (bf16[32,1664]{1,0:T(8,128)(2,1)S(1)}, bf16[32,1664]{1,0:T(8,128)(2,1)S(1)}, u32[]{:S(2)}, u32[]{:S(2)}) collective-permute-start(bf16[32,1664]{1,0:T(8,128)(2,1)S(1)} %get-tuple-element.18), channel_id=1, source_target_pairs={{0,2},{1,10},{2,18},{3,26},{4,6},{5,14},{6,22},{7,30},{8,3},{9,11}... | collective-permute-start | bytes 319496 | tf_op jit(solution)/shard_map/ppermute | solution.py:396
  26.8 5.5 %collective-permute-start.5 = (bf16[32,1664]{1,0:T(8,128)(2,1)S(1)}, bf16[32,1664]{1,0:T(8,128)(2,1)S(1)}, u32[]{:S(2)}, u32[]{:S(2)}) collective-permute-start(bf16[32,1664]{1,0:T(8,128)(2,1)S(1)} %collective-permute-done.1.refs_0_), channel_id=1, source_target_pairs={{0,4},{1,5},{2,6},{3,7},{4,0},{5,1},{6,2},{7,3},{8,12},{9,13},{10,... | collective-permute-start | bytes 319496 | tf_op jit(solution)/shard_map/ppermute | solution.py:397
  28.2 9.3 %copy-start.4 = (bf16[128,512]{1,0:T(8,128)(2,1)S(1)}, bf16[128,512]{1,0:T(8,128)(2,1)}, u32[]{:S(2)}) copy-start(bf16[128,512]{1,0:T(8,128)(2,1)} %tri_ref.1) | copy-start | bytes 393220
  28.2 6.1 %collective-permute-start.3 = (bf16[32,1664]{1,0:T(8,128)(2,1)S(1)}, bf16[32,1664]{1,0:T(8,128)(2,1)S(1)}, u32[]{:S(2)}, u32[]{:S(2)}) collective-permute-start(bf16[32,1664]{1,0:T(8,128)(2,1)S(1)} %collective-permute-done.1.refs_0_), channel_id=1, source_target_pairs={{0,2},{1,3},{2,0},{3,1},{4,6},{5,7},{6,4},{7,5},{8,10},{9,11},{10,... | collective-permute-start | bytes 319496 | tf_op jit(solution)/shard_map/ppermute | solution.py:403
  32.3 4.7 %collective-permute-start.7 = (bf16[32,1664]{1,0:T(8,128)(2,1)S(1)}, bf16[32,1664]{1,0:T(8,128)(2,1)S(1)}, u32[]{:S(2)}, u32[]{:S(2)}) collective-permute-start(bf16[32,1664]{1,0:T(8,128)(2,1)S(1)} %collective-permute-done.5.refs_4_), channel_id=1, source_target_pairs={{0,2},{1,3},{2,0},{3,1},{4,6},{5,7},{6,4},{7,5},{8,10},{9,11},{10,... | collective-permute-start | bytes 319496 | tf_op jit(solution)/shard_map/ppermute | solution.py:403
  32.3 5.2 %copy-start.7 = (s32[192]{0:T(256)S(1)}, s32[192]{0:T(256)}, u32[]{:S(2)}) copy-start(s32[192]{0:T(256)} %param.14) | copy-start | bytes 2308
  32.3 5.2 %collective-permute-start = (bf16[24,24,128]{2,1,0:T(8,128)(2,1)S(1)}, bf16[24,24,128]{2,1,0:T(8,128)(2,1)S(1)}, u32[]{:S(2)}, u32[]{:S(2)}) collective-permute-start(bf16[24,24,128]{2,1,0:T(8,128)(2,1)S(1)} %constant_dynamic-slice_fusion.1), channel_id=1, source_target_pairs={{0,4},{1,5},{2,6},{3,7},{4,0},{5,1},{6,2},{7,3},{8,12},{9,13},{10,... | collective-permute-start | bytes 442376 | tf_op jit(solution)/shard_map/ppermute | solution.py:392
  33.9 4.2 %collective-permute-start.2 = (bf16[32,1664]{1,0:T(8,128)(2,1)S(1)}, bf16[32,1664]{1,0:T(8,128)(2,1)S(1)}, u32[]{:S(2)}, u32[]{:S(2)}) collective-permute-start(bf16[32,1664]{1,0:T(8,128)(2,1)S(1)} %collective-permute-done.1.refs_0_), channel_id=1, source_target_pairs={{0,1},{1,0},{2,3},{3,2},{4,5},{5,4},{6,7},{7,6},{8,9},{9,8},{10,11... | collective-permute-start | bytes 319496 | tf_op jit(solution)/shard_map/ppermute | solution.py:403
  33.9 4.2 %collective-permute-start.6 = (bf16[32,1664]{1,0:T(8,128)(2,1)S(1)}, bf16[32,1664]{1,0:T(8,128)(2,1)S(1)}, u32[]{:S(2)}, u32[]{:S(2)}) collective-permute-start(bf16[32,1664]{1,0:T(8,128)(2,1)S(1)} %collective-permute-done.5.refs_4_), channel_id=1, source_target_pairs={{0,1},{1,0},{2,3},{3,2},{4,5},{5,4},{6,7},{7,6},{8,9},{9,8},{10,11... | collective-permute-start | bytes 319496 | tf_op jit(solution)/shard_map/ppermute | solution.py:403
  34.4 3.7 %collective-permute-start.4 = (bf16[32,1664]{1,0:T(8,128)(2,1)S(1)}, bf16[32,1664]{1,0:T(8,128)(2,1)S(1)}, u32[]{:S(2)}, u32[]{:S(2)}) collective-permute-start(bf16[32,1664]{1,0:T(8,128)(2,1)S(1)} %collective-permute-done.3.refs_2_), channel_id=1, source_target_pairs={{0,1},{1,0},{2,3},{3,2},{4,5},{5,4},{6,7},{7,6},{8,9},{9,8},{10,11... | collective-permute-start | bytes 319496 | tf_op jit(solution)/shard_map/ppermute | solution.py:403
  37.0 1.3 %collective-permute-start.8 = (bf16[32,1664]{1,0:T(8,128)(2,1)S(1)}, bf16[32,1664]{1,0:T(8,128)(2,1)S(1)}, u32[]{:S(2)}, u32[]{:S(2)}) collective-permute-start(bf16[32,1664]{1,0:T(8,128)(2,1)S(1)} %collective-permute-done.7.refs_6_), channel_id=1, source_target_pairs={{0,1},{1,0},{2,3},{3,2},{4,5},{5,4},{6,7},{7,6},{8,9},{9,8},{10,11... | collective-permute-start | bytes 319496 | tf_op jit(solution)/shard_map/ppermute | solution.py:403
  37.6 1.0 %copy-start.1 = (bf16[1024,128]{1,0:T(8,128)(2,1)S(1)}, bf16[1024,128]{1,0:T(8,128)(2,1)}, u32[]{:S(2)}) copy-start(bf16[1024,128]{1,0:T(8,128)(2,1)} %proj_ref.1) | copy-start | bytes 786436
  64.5 14.6 %all-to-all-start.2 = ((bf16[32,4,1152]{2,1,0:T(4,128)(2,1)}), bf16[32,4,1152]{2,1,0:T(4,128)(2,1)S(1)}, u32[]{:S(2)}, u32[]{:S(2)}) async-start(bf16[32,4,1152]{2,1,0:T(4,128)(2,1)} %shard_map.122), calls=%async_computation.2 | async-start | bytes 589824 | tf_op jit(solution)/shard_map/all_to_all | solution.py:291
  67.7 8.7 %copy-start.6 = (bf16[128,128]{1,0:T(8,128)(2,1)S(1)}, bf16[128,128]{1,0:T(8,128)(2,1)}, u32[]{:S(2)}) copy-start(bf16[128,128]{1,0:T(8,128)(2,1)} %gate_w_ref.1) | copy-start | bytes 98308
  67.7 11.4 %copy-start.2 = (bf16[128,512]{1,0:T(8,128)(2,1)S(1)}, bf16[128,512]{1,0:T(8,128)(2,1)}, u32[]{:S(2)}) copy-start(bf16[128,512]{1,0:T(8,128)(2,1)} %in_ref.1) | copy-start | bytes 393220
  67.8 11.3 %copy-start.3 = (bf16[512,128]{1,0:T(8,128)(2,1)S(1)}, bf16[512,128]{1,0:T(8,128)(2,1)}, u32[]{:S(2)}) copy-start(bf16[512,128]{1,0:T(8,128)(2,1)} %back_ref.1) | copy-start | bytes 393220
  67.8 11.3 %copy-start.5 = (bf16[128,128]{1,0:T(8,128)(2,1)S(1)}, bf16[128,128]{1,0:T(8,128)(2,1)}, u32[]{:S(2)}) copy-start(bf16[128,128]{1,0:T(8,128)(2,1)} %out_w_ref.1) | copy-start | bytes 98308
  67.8 8.6 %collective-permute-start.9 = (bf16[24,24,128]{2,1,0:T(8,128)(2,1)S(1)}, bf16[24,24,128]{2,1,0:T(8,128)(2,1)S(1)}, u32[]{:S(2)}, u32[]{:S(2)}) collective-permute-start(bf16[24,24,128]{2,1,0:T(8,128)(2,1)S(1)} %constant_dynamic-slice_fusion), channel_id=1, source_target_pairs={{0,4},{1,5},{2,6},{3,7},{4,0},{5,1},{6,2},{7,3},{8,12},{9,13},{10,... | collective-permute-start | bytes 442376 | tf_op jit(solution)/shard_map/ppermute | solution.py:392

commit v9 on v8

--- a/solution.py
+++ b/solution.py
@@ -73,8 +73,8 @@
 
 
 def side_kernel(
-    narrow, align_hbm, mask_hbm, left_w_hbm, right_w_hbm, right_hbm, left_ref,
-    left_rows, right_rows, align, mask_int, left_w, right_w, packed, align_sem, mask_sem, left_sem, right_sem, out_sem,
+    narrow, align_hbm, mask_hbm, left_w_hbm, right_w_hbm, right_ref, left_ref,
+    left_rows, right_rows, align, mask_int, left_w, right_w, align_sem, mask_sem, left_sem, right_sem,
 ):
     fetches = [
         pltpu.make_async_copy(left_w_hbm, left_w, left_sem),
@@ -94,26 +94,20 @@
     right_rows[...] = value[:, LANES:]
     mask = mask_int[...].astype(BF16)
     cols = mask.shape[1]
-    parts = packed.shape[0]
+    copies = right_ref.shape[0]
+    parts = cols * narrow // right_ref.shape[2]
     for h in range(parts):
 
         def put_right(group, value):
-            packed[h, :, group * LANES : (group + 1) * LANES] = value
+            for n in range(h, copies, parts):
+                right_ref[n, :, group * LANES : (group + 1) * LANES] = value
 
         pack_side(right_rows, mask, narrow, h * (cols // parts), cols // parts, put_right, True)
-    copies = [
-        pltpu.make_async_copy(packed.at[n % parts], right_hbm.at[n], out_sem.at[n])
-        for n in range(right_hbm.shape[0])
-    ]
-    for copy in copies:
-        copy.start()
 
     def put_left(group, value):
         left_ref[:, group * LANES : (group + 1) * LANES] = value
 
     pack_side(left_rows, mask, narrow, 0, cols, put_left)
-    for copy in copies:
-        copy.wait()
 
 
 def prepare_kernel(own, residue_ref, tri_ref, pair_ref, *refs):
@@ -365,15 +359,12 @@
             pltpu.VMEM((sequences, cols), jnp.int32),
             pltpu.VMEM((narrow, channels), BF16),
             pltpu.VMEM((narrow, channels), BF16),
-            pltpu.VMEM((turns, sequences, right_lanes), BF16),
             pltpu.SemaphoreType.DMA,
             pltpu.SemaphoreType.DMA,
             pltpu.SemaphoreType.DMA,
             pltpu.SemaphoreType.DMA,
-            pltpu.SemaphoreType.DMA((row_count,)),
         ],
         [hbm] * 4,
-        (hbm, VMEM),
     )(*in_hbm([alignment.reshape(lines, channels), alignment_mask, outer_product_left.T, outer_product_right.T]))
     right = lax.all_to_all(right, "row", split_axis=0, concat_axis=0, tiled=True)
     right = right.reshape(row_count * sequences, right_lanes)

time: 81.3 us -> 81.3 us (level)
  no operation moved by 1% of the time
where the time goes in v9:
time: 81.3 us; the launch traced here: 80.9 us
  waiting for transfers between devices  31 us (38%)
  blocking collectives  19.9 us (24%)
  starting transfers between devices  17.5 us (22%)
  Pallas kernels  12.2 us (15%)
    all_to_all x1, blocking collectives, triangle_by_channel(): lax.all_to_all(gated, ('row', 'col'), split_axis=0, concat_axis=0, tiled=...  19.9 us
    ppermute x1, waiting for transfers between devices, shards(): left = lax.ppermute(left, ('row', 'col'), turned)  14.7 us
    all_to_all x1, starting transfers between devices, shards(): lax.all_to_all(right, 'row', split_axis=0, concat_axis=0, tiled=True)  7.43 us
    ppermute x2, waiting for transfers between devices, exchange(): given.append(lax.ppermute(part, ('row', 'col'), near(d, 0)))  7.35 us
    ppermute x1, waiting for transfers between devices, shards(): lax.ppermute(left, ('row', 'col'), near(d, 0))  4.06 us
    pallas_call x1, Pallas kernels, shards(): call(functools.partial(outer_kernel, cols, rows, narrow, turns), 24, [((p...  3.64 us
    ppermute x2, starting transfers between devices, exchange(): given.append(lax.ppermute(part, ('row', 'col'), near(d, 0)))  3.36 us
    all_to_all x1, starting transfers between devices, triangle_by_channel(): lax.all_to_all(summed, ('row', 'col'), split_axis=0, concat_axis=0, tiled...  3.2 us
  transfers between devices with their start and end apart: 12, of which 7 were waited for; matrix products, arithmetic and copies ran while one was open for 0% of the time, Pallas kernels for 1%

profile of v9, /device:TPU:0, one launch (start us, length us, event | category | flops | bytes accessed | tf_op | source)
XLA Modules:
  0.0 80.9 jit_solution(10326931439777114950)
XLA Ops:
  0.0 3.0 %shard_map.118 = (bf16[8,32,768]{2,1,0:T(8,128)(2,1)}, bf16[32,1664]{1,0:T(8,128)(2,1)S(1)}) custom-call(bf16[1536,256]{1,0:T(8,128)(2,1)} %bitcast.11, s32[32,48]{1,0:T(8,128)} %mask_hbm.1, bf16[32,256]{1,0:T(8,128)(2,1)} %bitcast.12, bf16[32,256]{1,0:T(8,128)(2,1)} %bitcast.13), custom_call_target="tpu_custom_call" | custom-call | tf_op jit(solution)/shard_map/pallas_call | solution.py:351
  3.0 0.0 copy-start
  3.0 7.4 %all-to-all-start = ((bf16[8,32,768]{2,1,0:T(8,128)(2,1)}), bf16[8,32,768]{2,1,0:T(8,128)(2,1)S(1)}, u32[]{:S(2)}, u32[]{:S(2)}) async-start(bf16[8,32,768]{2,1,0:T(8,128)(2,1)} %get-tuple-element.14), calls=%async_computation | async-start | bytes 786432 | tf_op jit(solution)/shard_map/all_to_all | solution.py:369
  10.5 1.5 %collective-permute-start.1 = (bf16[32,1664]{1,0:T(8,128)(2,1)S(1)}, bf16[32,1664]{1,0:T(8,128)(2,1)S(1)}, u32[]{:S(2)}, u32[]{:S(2)}) collective-permute-start(bf16[32,1664]{1,0:T(8,128)(2,1)S(1)} %get-tuple-element.18), channel_id=1, source_target_pairs={{0,2},{1,10},{2,18},{3,26},{4,6},{5,14},{6,22},{7,30},{8,3},{9,11}... | collective-permute-start | bytes 319496 | tf_op jit(solution)/shard_map/ppermute | solution.py:387
  12.0 14.7 %collective-permute-done.1.refs_0_ = bf16[32,1664]{1,0:T(8,128)(2,1)S(1)} collective-permute-done((bf16[32,1664]{1,0:T(8,128)(2,1)S(1)}, bf16[32,1664]{1,0:T(8,128)(2,1)S(1)}, u32[]{:S(2)}, u32[]{:S(2)}) %collective-permute-start.1) | collective-permute-done | bytes 106528 | tf_op jit(solution)/shard_map/ppermute | solution.py:387
  26.7 1.5 %collective-permute-start.5 = (bf16[32,1664]{1,0:T(8,128)(2,1)S(1)}, bf16[32,1664]{1,0:T(8,128)(2,1)S(1)}, u32[]{:S(2)}, u32[]{:S(2)}) collective-permute-start(bf16[32,1664]{1,0:T(8,128)(2,1)S(1)} %collective-permute-done.1.refs_0_), channel_id=1, source_target_pairs={{0,4},{1,5},{2,6},{3,7},{4,0},{5,1},{6,2},{7,3},{8,12},{9,13},{10,... | collective-permute-start | bytes 319496 | tf_op jit(solution)/shard_map/ppermute | solution.py:388
  28.2 0.0 copy-start.4
  28.2 0.0 collective-permute-start.3
  28.2 4.1 %collective-permute-done.5.refs_4_ = bf16[32,1664]{1,0:T(8,128)(2,1)S(1)} collective-permute-done((bf16[32,1664]{1,0:T(8,128)(2,1)S(1)}, bf16[32,1664]{1,0:T(8,128)(2,1)S(1)}, u32[]{:S(2)}, u32[]{:S(2)}) %collective-permute-start.5) | collective-permute-done | bytes 106528 | tf_op jit(solution)/shard_map/ppermute | solution.py:388
  32.2 0.0 collective-permute-start.7
  32.2 0.0 copy-done
  32.3 0.0 copy-start.7
  32.3 1.5 %collective-permute-start = (bf16[24,24,128]{2,1,0:T(8,128)(2,1)S(1)}, bf16[24,24,128]{2,1,0:T(8,128)(2,1)S(1)}, u32[]{:S(2)}, u32[]{:S(2)}) collective-permute-start(bf16[24,24,128]{2,1,0:T(8,128)(2,1)S(1)} %constant_dynamic-slice_fusion.1), channel_id=1, source_target_pairs={{0,4},{1,5},{2,6},{3,7},{4,0},{5,1},{6,2},{7,3},{8,12},{9,13},{10,... | collective-permute-start | bytes 442376 | tf_op jit(solution)/shard_map/ppermute | solution.py:383
  33.8 0.0 collective-permute-start.2
  33.8 0.5 collective-permute-start.6
  34.3 0.0 collective-permute-done.3.refs_2_
  34.3 0.0 collective-permute-start.4
  34.3 2.6 %collective-permute-done.7.refs_6_ = bf16[32,1664]{1,0:T(8,128)(2,1)S(1)} collective-permute-done((bf16[32,1664]{1,0:T(8,128)(2,1)S(1)}, bf16[32,1664]{1,0:T(8,128)(2,1)S(1)}, u32[]{:S(2)}, u32[]{:S(2)}) %collective-permute-start.7) | collective-permute-done | bytes 106528 | tf_op jit(solution)/shard_map/ppermute | solution.py:394
  36.9 0.0 collective-permute-start.8
  37.0 0.5 collective-permute-done.refs_0_
  37.5 0.0 copy-done.4
  37.5 0.0 copy-done.7
  37.5 0.0 copy-start.1
  37.5 0.5 shard_map.119
  38.0 0.0 collective-permute-done.2.refs_1_
  38.0 0.0 collective-permute-done.6.refs_5_
  38.0 0.0 collective-permute-done.4.refs_3_
  38.0 0.2 collective-permute-done.8.refs_7_
  38.3 0.0 all-to-all-done
  38.3 0.2 copy-done.1
  38.4 3.6 %shard_map.120 = (bf16[1152,128]{1,0:T(8,128)(2,1)S(1)}, bf16[32,8,1152]{2,1,0:T(8,128)(2,1)S(1)}) custom-call(bf16[256,768]{1,0:T(8,128)(2,1)S(1)} %bitcast.7, bf16[1152,128]{1,0:T(8,128)(2,1)S(1)} %get-tuple-element.15.pair_ref, bf16[1024,128]{1,0:T(8,128)(2,1)S(1)} %copy-done.1, bf16[512,128]{1,0:T(8,128)(2,1)S(1)} %get-tuple-element.16.tri_ref, ...), custom_call_target="tpu_custom_call" | custom-call | tf_op jit(solution)/shard_map/pallas_call | solution.py:410
  42.1 19.9 %all_to_all.15.given_ref = bf16[32,8,1152]{2,1,0:T(8,128)(2,1)S(1)} all-to-all(bf16[32,8,1152]{2,1,0:T(8,128)(2,1)S(1)} %get-tuple-element.22), channel_id=1, replica_groups=mesh['row'=8,'col'=4] {'row','col'}, dimensions={0} | all-to-all | bytes 1179648 | tf_op jit(solution)/shard_map/all_to_all | solution.py:276
  62.0 2.5 %shard_map.122 = bf16[32,4,1152]{2,1,0:T(4,128)(2,1)} custom-call(bf16[32,8,1152]{2,1,0:T(8,128)(2,1)S(1)} %all_to_all.15.given_ref), custom_call_target="tpu_custom_call" | custom-call | tf_op jit(solution)/shard_map/pallas_call | solution.py:279
  64.5 3.2 %all-to-all-start.2 = ((bf16[32,4,1152]{2,1,0:T(4,128)(2,1)}), bf16[32,4,1152]{2,1,0:T(4,128)(2,1)S(1)}, u32[]{:S(2)}, u32[]{:S(2)}) async-start(bf16[32,4,1152]{2,1,0:T(4,128)(2,1)} %shard_map.122), calls=%async_computation.2 | async-start | bytes 589824 | tf_op jit(solution)/shard_map/all_to_all | solution.py:285
  67.7 0.0 copy-start.6
  67.7 0.0 copy-start.2
  67.7 0.0 copy-start.3
  67.7 0.0 copy-start.5
  67.7 1.8 %collective-permute-start.9 = (bf16[24,24,128]{2,1,0:T(8,128)(2,1)S(1)}, bf16[24,24,128]{2,1,0:T(8,128)(2,1)S(1)}, u32[]{:S(2)}, u32[]{:S(2)}) collective-permute-start(bf16[24,24,128]{2,1,0:T(8,128)(2,1)S(1)} %constant_dynamic-slice_fusion), channel_id=1, source_target_pairs={{0,4},{1,5},{2,6},{3,7},{4,0},{5,1},{6,2},{7,3},{8,12},{9,13},{10,... | collective-permute-start | bytes 442376 | tf_op jit(solution)/shard_map/ppermute | solution.py:383
  69.6 6.8 %collective-permute-done.9.refs_0_ = bf16[24,24,128]{2,1,0:T(8,128)(2,1)S(1)} collective-permute-done((bf16[24,24,128]{2,1,0:T(8,128)(2,1)S(1)}, bf16[24,24,128]{2,1,0:T(8,128)(2,1)S(1)}, u32[]{:S(2)}, u32[]{:S(2)}) %collective-permute-start.9) | collective-permute-done | bytes 147488 | tf_op jit(solution)/shard_map/ppermute | solution.py:383
  76.4 0.0 copy-done.6
  76.4 0.7 shard_map.121
  77.1 2.0 %all-to-all-done.2.summed_ref = bf16[32,4,1152]{2,1,0:T(4,128)(2,1)S(1)} async-done(((bf16[32,4,1152]{2,1,0:T(4,128)(2,1)}), bf16[32,4,1152]{2,1,0:T(4,128)(2,1)S(1)}, u32[]{:S(2)}, u32[]{:S(2)}) %all-to-all-start.2) | async-done | bytes 294944 | tf_op jit(solution)/shard_map/all_to_all | solution.py:285
  79.1 0.0 copy-done.2
  79.1 0.0 copy-done.3
  79.1 0.0 copy-done.5
  79.1 1.9 %shard_map.123 = bf16[1152,128]{1,0:T(8,128)(2,1)} custom-call(f32[128,1152]{1,0:T(8,128)S(1)} %get-tuple-element.20.first_ref, f32[128,1152]{1,0:T(8,128)S(1)} %get-tuple-element.21.gated_ref, bf16[32,4,1152]{2,1,0:T(4,128)(2,1)S(1)} %all-to-all-done.2.summed_ref, bf16[128,128]{1,0:T(8,128)(2,1)S(1)} %copy-done.5, bf16[128,512]{1,0:T(8,128)(2,1)S(1)} %copy-done.2, ...), custom_call_target="tpu_custom_call" | custom-call | tf_op jit(solution)/shard_map/pallas_call | solution.py:432
  (2 shorter events, 0.0 us)
Async XLA Ops:
  3.0 29.2 %copy-start = (bf16[24,48,128]{2,1,0:T(8,128)(2,1)S(1)}, bf16[24,48,128]{2,1,0:T(8,128)(2,1)}, u32[]{:S(2)}) copy-start(bf16[24,48,128]{2,1,0:T(8,128)(2,1)} %pair_ref.1) | copy-start | bytes 884740
  3.0 35.2 %all-to-all-start = ((bf16[8,32,768]{2,1,0:T(8,128)(2,1)}), bf16[8,32,768]{2,1,0:T(8,128)(2,1)S(1)}, u32[]{:S(2)}, u32[]{:S(2)}) async-start(bf16[8,32,768]{2,1,0:T(8,128)(2,1)} %get-tuple-element.14), calls=%async_computation | async-start | bytes 786432 | tf_op jit(solution)/shard_map/all_to_all | solution.py:369
  10.5 16.2 %collective-permute-start.1 = (bf16[32,1664]{1,0:T(8,128)(2,1)S(1)}, bf16[32,1664]{1,0:T(8,128)(2,1)S(1)}, u32[]{:S(2)}, u32[]{:S(2)}) collective-permute-start(bf16[32,1664]{1,0:T(8,128)(2,1)S(1)} %get-tuple-element.18), channel_id=1, source_target_pairs={{0,2},{1,10},{2,18},{3,26},{4,6},{5,14},{6,22},{7,30},{8,3},{9,11}... | collective-permute-start | bytes 319496 | tf_op jit(solution)/shard_map/ppermute | solution.py:387
  26.7 5.5 %collective-permute-start.5 = (bf16[32,1664]{1,0:T(8,128)(2,1)S(1)}, bf16[32,1664]{1,0:T(8,128)(2,1)S(1)}, u32[]{:S(2)}, u32[]{:S(2)}) collective-permute-start(bf16[32,1664]{1,0:T(8,128)(2,1)S(1)} %collective-permute-done.1.refs_0_), channel_id=1, source_target_pairs={{0,4},{1,5},{2,6},{3,7},{4,0},{5,1},{6,2},{7,3},{8,12},{9,13},{10,... | collective-permute-start | bytes 319496 | tf_op jit(solution)/shard_map/ppermute | solution.py:388
  28.2 9.3 %copy-start.4 = (bf16[128,512]{1,0:T(8,128)(2,1)S(1)}, bf16[128,512]{1,0:T(8,128)(2,1)}, u32[]{:S(2)}) copy-start(bf16[128,512]{1,0:T(8,128)(2,1)} %tri_ref.1) | copy-start | bytes 393220
  28.2 6.1 %collective-permute-start.3 = (bf16[32,1664]{1,0:T(8,128)(2,1)S(1)}, bf16[32,1664]{1,0:T(8,128)(2,1)S(1)}, u32[]{:S(2)}, u32[]{:S(2)}) collective-permute-start(bf16[32,1664]{1,0:T(8,128)(2,1)S(1)} %collective-permute-done.1.refs_0_), channel_id=1, source_target_pairs={{0,2},{1,3},{2,0},{3,1},{4,6},{5,7},{6,4},{7,5},{8,10},{9,11},{10,... | collective-permute-start | bytes 319496 | tf_op jit(solution)/shard_map/ppermute | solution.py:394
  32.2 4.7 %collective-permute-start.7 = (bf16[32,1664]{1,0:T(8,128)(2,1)S(1)}, bf16[32,1664]{1,0:T(8,128)(2,1)S(1)}, u32[]{:S(2)}, u32[]{:S(2)}) collective-permute-start(bf16[32,1664]{1,0:T(8,128)(2,1)S(1)} %collective-permute-done.5.refs_4_), channel_id=1, source_target_pairs={{0,2},{1,3},{2,0},{3,1},{4,6},{5,7},{6,4},{7,5},{8,10},{9,11},{10,... | collective-permute-start | bytes 319496 | tf_op jit(solution)/shard_map/ppermute | solution.py:394
  32.3 5.2 %copy-start.7 = (s32[192]{0:T(256)S(1)}, s32[192]{0:T(256)}, u32[]{:S(2)}) copy-start(s32[192]{0:T(256)} %param.14) | copy-start | bytes 2308
  32.3 5.2 %collective-permute-start = (bf16[24,24,128]{2,1,0:T(8,128)(2,1)S(1)}, bf16[24,24,128]{2,1,0:T(8,128)(2,1)S(1)}, u32[]{:S(2)}, u32[]{:S(2)}) collective-permute-start(bf16[24,24,128]{2,1,0:T(8,128)(2,1)S(1)} %constant_dynamic-slice_fusion.1), channel_id=1, source_target_pairs={{0,4},{1,5},{2,6},{3,7},{4,0},{5,1},{6,2},{7,3},{8,12},{9,13},{10,... | collective-permute-start | bytes 442376 | tf_op jit(solution)/shard_map/ppermute | solution.py:383
  33.8 4.2 %collective-permute-start.2 = (bf16[32,1664]{1,0:T(8,128)(2,1)S(1)}, bf16[32,1664]{1,0:T(8,128)(2,1)S(1)}, u32[]{:S(2)}, u32[]{:S(2)}) collective-permute-start(bf16[32,1664]{1,0:T(8,128)(2,1)S(1)} %collective-permute-done.1.refs_0_), channel_id=1, source_target_pairs={{0,1},{1,0},{2,3},{3,2},{4,5},{5,4},{6,7},{7,6},{8,9},{9,8},{10,11... | collective-permute-start | bytes 319496 | tf_op jit(solution)/shard_map/ppermute | solution.py:394
  33.8 4.2 %collective-permute-start.6 = (bf16[32,1664]{1,0:T(8,128)(2,1)S(1)}, bf16[32,1664]{1,0:T(8,128)(2,1)S(1)}, u32[]{:S(2)}, u32[]{:S(2)}) collective-permute-start(bf16[32,1664]{1,0:T(8,128)(2,1)S(1)} %collective-permute-done.5.refs_4_), channel_id=1, source_target_pairs={{0,1},{1,0},{2,3},{3,2},{4,5},{5,4},{6,7},{7,6},{8,9},{9,8},{10,11... | collective-permute-start | bytes 319496 | tf_op jit(solution)/shard_map/ppermute | solution.py:394
  34.3 3.7 %collective-permute-start.4 = (bf16[32,1664]{1,0:T(8,128)(2,1)S(1)}, bf16[32,1664]{1,0:T(8,128)(2,1)S(1)}, u32[]{:S(2)}, u32[]{:S(2)}) collective-permute-start(bf16[32,1664]{1,0:T(8,128)(2,1)S(1)} %collective-permute-done.3.refs_2_), channel_id=1, source_target_pairs={{0,1},{1,0},{2,3},{3,2},{4,5},{5,4},{6,7},{7,6},{8,9},{9,8},{10,11... | collective-permute-start | bytes 319496 | tf_op jit(solution)/shard_map/ppermute | solution.py:394
  36.9 1.3 %collective-permute-start.8 = (bf16[32,1664]{1,0:T(8,128)(2,1)S(1)}, bf16[32,1664]{1,0:T(8,128)(2,1)S(1)}, u32[]{:S(2)}, u32[]{:S(2)}) collective-permute-start(bf16[32,1664]{1,0:T(8,128)(2,1)S(1)} %collective-permute-done.7.refs_6_), channel_id=1, source_target_pairs={{0,1},{1,0},{2,3},{3,2},{4,5},{5,4},{6,7},{7,6},{8,9},{9,8},{10,11... | collective-permute-start | bytes 319496 | tf_op jit(solution)/shard_map/ppermute | solution.py:394
  37.5 1.0 %copy-start.1 = (bf16[1024,128]{1,0:T(8,128)(2,1)S(1)}, bf16[1024,128]{1,0:T(8,128)(2,1)}, u32[]{:S(2)}) copy-start(bf16[1024,128]{1,0:T(8,128)(2,1)} %proj_ref.1) | copy-start | bytes 786436
  64.5 14.6 %all-to-all-start.2 = ((bf16[32,4,1152]{2,1,0:T(4,128)(2,1)}), bf16[32,4,1152]{2,1,0:T(4,128)(2,1)S(1)}, u32[]{:S(2)}, u32[]{:S(2)}) async-start(bf16[32,4,1152]{2,1,0:T(4,128)(2,1)} %shard_map.122), calls=%async_computation.2 | async-start | bytes 589824 | tf_op jit(solution)/shard_map/all_to_all | solution.py:285
  67.7 8.7 %copy-start.6 = (bf16[128,128]{1,0:T(8,128)(2,1)S(1)}, bf16[128,128]{1,0:T(8,128)(2,1)}, u32[]{:S(2)}) copy-start(bf16[128,128]{1,0:T(8,128)(2,1)} %gate_w_ref.1) | copy-start | bytes 98308
  67.7 11.4 %copy-start.2 = (bf16[128,512]{1,0:T(8,128)(2,1)S(1)}, bf16[128,512]{1,0:T(8,128)(2,1)}, u32[]{:S(2)}) copy-start(bf16[128,512]{1,0:T(8,128)(2,1)} %in_ref.1) | copy-start | bytes 393220
  67.7 11.3 %copy-start.3 = (bf16[512,128]{1,0:T(8,128)(2,1)S(1)}, bf16[512,128]{1,0:T(8,128)(2,1)}, u32[]{:S(2)}) copy-start(bf16[512,128]{1,0:T(8,128)(2,1)} %back_ref.1) | copy-start | bytes 393220
  67.7 11.3 %copy-start.5 = (bf16[128,128]{1,0:T(8,128)(2,1)S(1)}, bf16[128,128]{1,0:T(8,128)(2,1)}, u32[]{:S(2)}) copy-start(bf16[128,128]{1,0:T(8,128)(2,1)} %out_w_ref.1) | copy-start | bytes 98308
  67.7 8.6 %collective-permute-start.9 = (bf16[24,24,128]{2,1,0:T(8,128)(2,1)S(1)}, bf16[24,24,128]{2,1,0:T(8,128)(2,1)S(1)}, u32[]{:S(2)}, u32[]{:S(2)}) collective-permute-start(bf16[24,24,128]{2,1,0:T(8,128)(2,1)S(1)} %constant_dynamic-slice_fusion), channel_id=1, source_target_pairs={{0,4},{1,5},{2,6},{3,7},{4,0},{5,1},{6,2},{7,3},{8,12},{9,13},{10,... | collective-permute-start | bytes 442376 | tf_op jit(solution)/shard_map/ppermute | solution.py:383
